TPU v7x, 768 devices: a whole 4x8x12 slice. The times are simulated.
768 devices in a mesh: flow: 48 (over z, y_hi), chem: 16 (over x, y_lo, core).
Axes of the slice: x: 4, y: 8 (y_hi: 4, y_lo: 2; y = y_hi * 2 + y_lo), z: 12, core: 2. Of those that a mesh axis runs over, the one named last changes fastest.
Arguments:
- molar_fractions: float32 [53, 192, 112, 128], P(None, 'flow', 'chem'), may hold values from 0.05 to 2
- fluid_speed_vector: float32 [3, 192, 112, 128], P(None, 'flow', 'chem'), may hold values from -0.3 to 0.3
- thermal_state: float32 [192, 112, 128], P('flow', 'chem'), may hold values from 0.8 to 2
- molecular_spreading: float32 [53], replicated, may hold values from 0.05 to 0.12
- arrhenius_ln_amplitude: float32 [325], replicated, may hold values from -1 to 2
- arrhenius_energy: float32 [325], replicated, may hold values from 0.5 to 3
- consumed_molecules: int32 [325, 2], replicated, may hold values from 0 to 52
- resulting_molecules: int32 [325, 2], replicated, may hold values from 0 to 52
- patch_assignee: int32 [48, 224], P('flow'), may hold values from 0 to 16, as said below
Outputs:
- species_next: float32 [53, 192, 112, 128], P(None, 'flow', 'chem')
Inputs may be any that keep to these rules, and one draw needn't show every extreme that they name: patch_assignee[f, b] names the chemistry index that handles block b of flow index f; the value 16 means that the block takes no chemistry. Exactly 112 blocks of every flow index take chemistry, and some box of every flow index has all its 14 blocks taking chemistry. At most 1 block of one box goes to one chemistry index, and at most 10 blocks of a flow index to one chemistry index; both bounds are reached in every flow index.
All inputs are finite; a program needn't handle non-finite values.
Results may differ from a plain program's by a relative error of at most 0.0003.
Values sent between devices are 32-bit elements; how exact they have to be, the bound alone decides.
No kernel may reach another device: no remote copies, remote signals or barrier semaphores. Data moves between devices by JAX's collectives and lax.ppermute only.
A program may use at most 32 MiB of HBM per device.

v0:
```python
import jax
import jax.numpy as jnp
from jax import lax
from jax.sharding import PartitionSpec as P

PATCHES_ON_UNIT = 14
SUBSTEPS = 4


conc_floor = 0.1
rate_ceiling = 1.0
chem_dt = 0.04


def with_halo(block, sides, width):
    for axis, dim in sides:
        count = lax.axis_size(axis)
        forward = [(i, i + 1) for i in range(count - 1)]
        forward.append((count - 1, 0))
        backward = [(target, source) for source, target in forward]
        low = lax.ppermute(
            lax.slice_in_dim(block, block.shape[dim] - width, None, axis=dim), axis, forward
        )
        high = lax.ppermute(lax.slice_in_dim(block, 0, width, axis=dim), axis, backward)
        block = jnp.concatenate([low, block, high], axis=dim)
    return block


def derivatives(neighbours):
    minus_two, minus_one, center, plus_one, plus_two = neighbours
    first = (minus_two - 8.0 * minus_one + 8.0 * plus_one - plus_two) / 12.0
    second = (-minus_two + 16.0 * minus_one - 30.0 * center + 16.0 * plus_one - plus_two) / 12.0
    return (first, second)


def shifted(padded, length, which_axis):
    return tuple(
        (lax.slice_in_dim(padded, offset, offset + length, axis=which_axis) for offset in range(5))
    )


def stoichiometry(consumed_molecules, resulting_molecules, species_count):
    species_ids = jnp.arange(species_count, dtype=jnp.int32)
    forward = (consumed_molecules[:, 0:1] == species_ids[None, :]).astype(jnp.float32) + (
        consumed_molecules[:, 1:2] == species_ids[None, :]
    ).astype(jnp.float32)
    produced = (resulting_molecules[:, 0:1] == species_ids[None, :]).astype(jnp.float32) + (
        resulting_molecules[:, 1:2] == species_ids[None, :]
    ).astype(jnp.float32)
    return (forward, (produced - forward).T)


def react(initial, kelvin, forward, net_change, arrhenius_ln_amplitude, arrhenius_energy):
    current = initial
    for substep in range(SUBSTEPS):
        logged = jnp.log(jnp.maximum(current, conc_floor))
        exponent = (
            arrhenius_ln_amplitude[:, None]
            + jnp.dot(
                forward, logged, preferred_element_type=jnp.float32, precision=lax.Precision.HIGHEST
            )
            - arrhenius_energy[:, None] / kelvin[None, :]
        )
        progress = jnp.exp(jnp.minimum(exponent, rate_ceiling))
        current = current + chem_dt * jnp.dot(
            net_change,
            progress,
            preferred_element_type=jnp.float32,
            precision=lax.Precision.HIGHEST,
        )
    return current - initial


def react_slots(workload, kelvin_slots, lookup_matrices):
    forward, net_change, arrhenius_ln_amplitude, arrhenius_energy = lookup_matrices
    species_count, slot_total, mesh_point_number = workload.shape
    batch_width = 1
    for candidate in (2, 3, 4):
        if slot_total % candidate == 0:
            batch_width = candidate
    rounds = slot_total // batch_width

    def one_round(counter, result):
        offset = counter * batch_width
        portion = lax.dynamic_slice_in_dim(workload, offset, batch_width, 1).reshape(
            species_count, batch_width * mesh_point_number
        )
        kelvin = lax.dynamic_slice_in_dim(kelvin_slots, offset, batch_width, 0).reshape(
            batch_width * mesh_point_number
        )
        change = react(
            portion, kelvin, forward, net_change, arrhenius_ln_amplitude, arrhenius_energy
        ).reshape(species_count, batch_width, mesh_point_number)
        return lax.dynamic_update_slice_in_dim(result, change, offset, 1)

    return lax.fori_loop(0, rounds, one_round, jnp.zeros_like(workload))


def remote_chemistry(
    patches,
    patch_thermal_state,
    lookup_matrices,
    destination,
    engaged_everywhere,
    my_position,
    kinetics_workers,
    patch_limit,
    heaviest_loaded,
):
    species_count, blocks_per_box, mesh_point_number = patches.shape
    group_blocks = kinetics_workers * blocks_per_box
    slot_count = kinetics_workers * patch_limit
    block_ids = jnp.arange(group_blocks, dtype=jnp.int32)
    sender = block_ids // blocks_per_box
    pairing = (
        (sender[:, None] == sender[None, :])
        & (destination[:, None] == destination[None, :])
        & (block_ids[None, :] < block_ids[:, None])
    )
    slot_all = jnp.sum(pairing.astype(jnp.int32), axis=1)
    server_ids = jnp.arange(kinetics_workers, dtype=jnp.int32)
    slot_ids = jnp.arange(patch_limit, dtype=jnp.int32)
    local_ids = jnp.arange(blocks_per_box, dtype=jnp.int32)
    mine_target = lax.dynamic_slice_in_dim(
        destination, my_position * blocks_per_box, blocks_per_box
    )
    mine_slot = lax.dynamic_slice_in_dim(slot_all, my_position * blocks_per_box, blocks_per_box)
    mine_active = lax.dynamic_slice_in_dim(
        engaged_everywhere, my_position * blocks_per_box, blocks_per_box
    )
    matches = (mine_target[None, None, :] == server_ids[:, None, None]) & (
        mine_slot[None, None, :] == slot_ids[None, :, None]
    )
    selected_patch = jnp.sum(jnp.where(matches, local_ids[None, None, :], 0), axis=2).reshape(
        slot_count
    )
    outgoing = jnp.take(patches, selected_patch, axis=1).reshape(
        species_count, kinetics_workers, patch_limit, mesh_point_number
    )
    exported_enthalpy = jnp.take(patch_thermal_state, selected_patch, axis=0).reshape(
        1, kinetics_workers, patch_limit, mesh_point_number
    )
    arrived, arrived_heat = (
        lax.all_to_all(outgoing, "chem", split_axis=1, concat_axis=1, tiled=True),
        lax.all_to_all(exported_enthalpy, "chem", split_axis=1, concat_axis=1, tiled=True),
    )
    incoming = engaged_everywhere & (destination == my_position)
    present = jnp.any(
        (sender[None, None, :] == server_ids[:, None, None])
        & (slot_all[None, None, :] == slot_ids[None, :, None])
        & incoming[None, None, :],
        axis=2,
    ).reshape(slot_count)
    position = jnp.cumsum(present.astype(jnp.int32)) - 1
    work_ids = jnp.arange(heaviest_loaded, dtype=jnp.int32)
    slot_range = jnp.arange(slot_count, dtype=jnp.int32)
    gathered_ids = jnp.sum(
        jnp.where(
            present[None, :] & (position[None, :] == work_ids[:, None]), slot_range[None, :], 0
        ),
        axis=1,
    )
    workload = jnp.take(
        arrived.reshape(species_count, slot_count, mesh_point_number), gathered_ids, axis=1
    )
    work_heat = jnp.take(arrived_heat.reshape(slot_count, mesh_point_number), gathered_ids, axis=0)
    change = react_slots(workload, work_heat, lookup_matrices)
    returning = jnp.where(
        present[None, :, None], jnp.take(change, jnp.maximum(position, 0), axis=1), 0.0
    ).reshape(species_count, kinetics_workers, patch_limit, mesh_point_number)
    returned = lax.all_to_all(returning, "chem", split_axis=1, concat_axis=1, tiled=True)
    flat_index = jnp.minimum(mine_target, kinetics_workers - 1) * patch_limit + jnp.minimum(
        mine_slot, patch_limit - 1
    )
    delivered = jnp.take(
        returned.reshape(species_count, slot_count, mesh_point_number), flat_index, axis=1
    )
    return jnp.where(mine_active[None, :, None], delivered, 0.0)


def per_device(
    molar_fractions,
    fluid_speed_vector,
    thermal_state,
    molecular_spreading,
    arrhenius_ln_amplitude,
    arrhenius_energy,
    consumed_molecules,
    resulting_molecules,
    patch_assignee,
):
    species_count, box_x, box_y, box_z = molar_fractions.shape
    wide_x = with_halo(molar_fractions, (("flow", 1),), 2)
    wide_y = with_halo(molar_fractions, (("chem", 2),), 2)
    first_x, second_x = derivatives(shifted(wide_x, box_x, 1))
    first_y, second_y = derivatives(shifted(wide_y, box_y, 2))
    first_z, second_z = derivatives(
        (
            jnp.roll(molar_fractions, 2, 3),
            jnp.roll(molar_fractions, 1, 3),
            molar_fractions,
            jnp.roll(molar_fractions, -1, 3),
            jnp.roll(molar_fractions, -2, 3),
        )
    )
    moved = (
        fluid_speed_vector[0][None] * first_x
        + fluid_speed_vector[1][None] * first_y
        + fluid_speed_vector[2][None] * first_z
    )
    advected = (
        molar_fractions
        - moved
        + molecular_spreading[:, None, None, None] * (second_x + second_y + second_z)
    )
    mesh_point_number = box_x * box_y * box_z // PATCHES_ON_UNIT
    patches = advected.reshape(species_count, PATCHES_ON_UNIT, mesh_point_number)
    patch_thermal_state = thermal_state.reshape(PATCHES_ON_UNIT, mesh_point_number)
    forward, net_change = stoichiometry(consumed_molecules, resulting_molecules, species_count)
    lookup_matrices = (forward, net_change, arrhenius_ln_amplitude, arrhenius_energy)
    kinetics_workers = lax.axis_size("chem")
    my_position = lax.axis_index("chem")
    patch_assignees = patch_assignee[0]
    engaged_everywhere = patch_assignees < kinetics_workers
    patch_limit = max(1, -(-PATCHES_ON_UNIT // (kinetics_workers - 1)))
    feeding_count = min(
        kinetics_workers, (PATCHES_ON_UNIT * 3 // 4 + patch_limit - 1) // patch_limit
    )
    heaviest_loaded = feeding_count * patch_limit
    source = remote_chemistry(
        patches,
        patch_thermal_state,
        lookup_matrices,
        patch_assignees,
        engaged_everywhere,
        my_position,
        kinetics_workers,
        patch_limit,
        heaviest_loaded,
    )
    return advected + source.reshape(species_count, box_x, box_y, box_z)


def solution(mesh):
    in_specs = (
        P(None, "flow", "chem", None),
        P(None, "flow", "chem", None),
        P("flow", "chem", None),
        P(),
        P(),
        P(),
        P(),
        P(),
        P("flow", None),
    )
    out_specs = P(None, "flow", "chem", None)
    return jax.shard_map(
        per_device, mesh=mesh, in_specs=in_specs, out_specs=out_specs, check_vma=False
    )
```

profile of v0, /device:TPU:1, one launch (start us, length us, event | category | flops | bytes accessed | tf_op | source)
XLA Modules:
  0.0 121.5 jit_solution(9358304188388591774)
XLA Ops:
  0.0 1.2 %copy.139 = f32[53,4,7,128]{3,2,1,0:T(8,128)S(1)} copy(f32[53,4,7,128]{3,1,2,0:T(4,128)} %param.11) | data formatting | bytes 1519616 | tf_op args[0]
  1.3 5.0 %collective-permute-start = (f32[53,2,7,128]{3,2,1,0:T(8,128)S(1)}, f32[53,2,7,128]{3,2,1,0:T(8,128)S(1)}, u32[]{:S(2)}, u32[]{:S(2)}) collective-permute-start(f32[53,2,7,128]{3,2,1,0:T(8,128)S(1)} %get-tuple-element.274), channel_id=1, source_target_pairs={{0,16},{16,32},{32,48},{48,64},{64,80},{80,96},{96,112},{112,128},... | collective-permute-start | bytes 1139720 | tf_op jit(solution)/shard_map/ppermute | solution.py:21
  6.4 15.7 %collective-permute-start.1 = (f32[53,2,7,128]{3,2,1,0:T(8,128)S(1)}, f32[53,2,7,128]{3,2,1,0:T(8,128)S(1)}, u32[]{:S(2)}, u32[]{:S(2)}) collective-permute-start(f32[53,2,7,128]{3,2,1,0:T(8,128)S(1)} %get-tuple-element.275), channel_id=1, source_target_pairs={{16,0},{32,16},{48,32},{64,48},{80,64},{96,80},{112,96},{128,112},... | collective-permute-start | bytes 1139720 | tf_op jit(solution)/shard_map/ppermute | solution.py:24
  22.3 3.1 %collective-permute-start.2 = (f32[53,4,2,128]{3,2,1,0:T(2,128)S(1)}, f32[53,4,2,128]{3,2,1,0:T(2,128)S(1)}, u32[]{:S(2)}, u32[]{:S(2)}) collective-permute-start(f32[53,4,2,128]{3,2,1,0:T(2,128)S(1)} %get-tuple-element.276), channel_id=1, source_target_pairs={{0,1},{1,2},{2,3},{3,4},{4,5},{5,6},{6,7},{7,8},{8,9},{9,10},{10,1... | collective-permute-start | bytes 651272 | tf_op jit(solution)/shard_map/ppermute | solution.py:21
  25.4 1.9 %collective-permute-start.3 = (f32[53,4,2,128]{3,2,1,0:T(2,128)S(1)}, f32[53,4,2,128]{3,2,1,0:T(2,128)S(1)}, u32[]{:S(2)}, u32[]{:S(2)}) collective-permute-start(f32[53,4,2,128]{3,2,1,0:T(2,128)S(1)} %get-tuple-element.277), channel_id=1, source_target_pairs={{1,0},{2,1},{3,2},{4,3},{5,4},{6,5},{7,6},{8,7},{9,8},{10,9},{11,1... | collective-permute-start | bytes 651272 | tf_op jit(solution)/shard_map/ppermute | solution.py:24
  29.7 6.8 %all-to-all-start.1 = ((f32[1,16,1,256]{3,2,0,1:T(1,128)}), f32[1,16,1,256]{3,2,0,1:T(1,128)S(1)}, u32[]{:S(2)}, u32[]{:S(2)}) async-start(f32[1,16,1,256]{3,2,0,1:T(1,128)} %copy.150), calls=%async_computation.1 | async-start | bytes 32768 | tf_op jit(solution)/shard_map/all_to_all | solution.py:145
  39.4 2.9 %multiply_add_fusion = f32[53,4,7,128]{3,2,1,0:T(8,128)S(1)} fusion(f32[53,4,7,128]{3,2,1,0:T(8,128)S(1)} %copy.139, f32[53,4,7,2]{3,2,1,0:T(8,128)S(1)} %get-tuple-element.283, f32[53,4,7,126]{3,2,1,0:T(8,128)S(1)} %get-tuple-element.285, f32[53,4,7,1]{3,2,1,0:T(8,128)S(1)} %get-tuple-element.279, f32[53,4,7,127]{3,2,1,0:T(8,128)S(1)} %get-tuple-element.281, ...), kind=kLoop, calls=%fused_computation.109 | loop fusion | flops 10447360 | bytes 8075476 | tf_op jit(solution)/shard_map/add | solution.py:212
  43.8 1.8 %copy.146 = f32[53,16,1,256]{3,2,0,1:T(1,128)} copy(f32[53,16,1,256]{3,0,1,2:T(8,128)S(1)} %bitcast_select_fusion.1) | data formatting | bytes 1736704 | tf_op jit(solution)/shard_map/jit(_take)/select_n | solution.py:137
  45.6 5.9 %all-to-all-start = ((f32[53,16,1,256]{3,2,0,1:T(1,128)}), f32[53,16,1,256]{3,2,0,1:T(1,128)S(1)}, u32[]{:S(2)}, u32[]{:S(2)}) async-start(f32[53,16,1,256]{3,2,0,1:T(1,128)} %copy.146), calls=%async_computation | async-start | bytes 1736704 | tf_op jit(solution)/shard_map/all_to_all | solution.py:144
  52.4 12.9 %all-to-all-done = f32[53,16,1,256]{3,2,0,1:T(1,128)S(1)} async-done(((f32[53,16,1,256]{3,2,0,1:T(1,128)}), f32[53,16,1,256]{3,2,0,1:T(1,128)S(1)}, u32[]{:S(2)}, u32[]{:S(2)}) %all-to-all-start) | async-done | bytes 868384 | tf_op jit(solution)/shard_map/all_to_all | solution.py:144
  66.8 31.1 %while.15 = (s32[]{:T(128)}, f32[53,10,256]{2,1,0:T(8,128)S(1)}, f32[53,10,256]{2,1,0:T(8,128)S(1)}, f32[325]{0:T(512)S(1)}, f32[325]{0:T(512)S(1)}, /*index=5*/...) while((s32[]{:T(128)}, f32[53,10,256]{2,1,0:T(8,128)S(1)}, ...), condition=%wide.region_6.7_spmd.clone.clone, body=%wide.region_5.6_spmd.clone.clone.sunk | while | flops 850760704 | bytes 7897931 | solution.py:96
  66.9 0.8 fusion.114
  68.4 0.8 fusion.116
  69.9 0.8 fusion.118
  71.4 0.8 fusion.120
  73.2 0.8 fusion.114
  74.6 0.8 fusion.116
  77.6 0.8 fusion.120
  79.4 0.8 fusion.114
  80.9 0.8 fusion.116
  82.4 0.8 fusion.118
  85.6 0.8 fusion.114
  87.1 0.8 fusion.116
  88.6 0.8 fusion.118
  90.1 0.8 fusion.120
  91.9 0.8 fusion.114
  93.3 0.8 fusion.116
  96.3 0.8 fusion.120
  99.1 1.8 %copy.153 = f32[53,16,1,256]{3,2,0,1:T(1,128)} copy(f32[53,16,1,256]{3,0,1,2:T(8,128)S(1)} %fusion.69) | data formatting | bytes 1736704 | tf_op jit(solution)/shard_map/jit(_where)/select_n | solution.py:168
  100.9 4.4 %all-to-all-start.2 = ((f32[53,16,1,256]{3,2,0,1:T(1,128)}), f32[53,16,1,256]{3,2,0,1:T(1,128)S(1)}, u32[]{:S(2)}, u32[]{:S(2)}) async-start(f32[53,16,1,256]{3,2,0,1:T(1,128)} %copy.153), calls=%async_computation.2 | async-start | bytes 1736704 | tf_op jit(solution)/shard_map/all_to_all | solution.py:171
  105.7 13.4 %all-to-all-done.2 = f32[53,16,1,256]{3,2,0,1:T(1,128)S(1)} async-done(((f32[53,16,1,256]{3,2,0,1:T(1,128)}), f32[53,16,1,256]{3,2,0,1:T(1,128)S(1)}, u32[]{:S(2)}, u32[]{:S(2)}) %all-to-all-start.2) | async-done | bytes 868384 | tf_op jit(solution)/shard_map/all_to_all | solution.py:171
  120.5 1.1 copy.157
  (147 shorter events, 28.1 us)
Async XLA Ops:
  1.2 26.1 %copy-start.3 = (s32[1,224]{1,0:T(1,128)S(1)}, s32[1,224]{1,0:T(1,128)}, u32[]{:S(2)}) copy-start(s32[1,224]{1,0:T(1,128)} %param.19) | copy-start | bytes 2692
  1.3 27.2 %copy-start.2 = (f32[4,7,128]{2,0,1:T(4,128)S(1)}, f32[4,7,128]{2,0,1:T(4,128)}, u32[]{:S(2)}) copy-start(f32[4,7,128]{2,0,1:T(4,128)} %param.13) | copy-start | bytes 43012
  1.3 37.1 %collective-permute-start = (f32[53,2,7,128]{3,2,1,0:T(8,128)S(1)}, f32[53,2,7,128]{3,2,1,0:T(8,128)S(1)}, u32[]{:S(2)}, u32[]{:S(2)}) collective-permute-start(f32[53,2,7,128]{3,2,1,0:T(8,128)S(1)} %get-tuple-element.274), channel_id=1, source_target_pairs={{0,16},{16,32},{32,48},{48,64},{64,80},{80,96},{96,112},{112,128},... | collective-permute-start | bytes 1139720 | tf_op jit(solution)/shard_map/ppermute | solution.py:21
  6.4 33.0 %collective-permute-start.1 = (f32[53,2,7,128]{3,2,1,0:T(8,128)S(1)}, f32[53,2,7,128]{3,2,1,0:T(8,128)S(1)}, u32[]{:S(2)}, u32[]{:S(2)}) collective-permute-start(f32[53,2,7,128]{3,2,1,0:T(8,128)S(1)} %get-tuple-element.275), channel_id=1, source_target_pairs={{16,0},{32,16},{48,32},{64,48},{80,64},{96,80},{112,96},{128,112},... | collective-permute-start | bytes 1139720 | tf_op jit(solution)/shard_map/ppermute | solution.py:24
  22.3 17.1 %collective-permute-start.2 = (f32[53,4,2,128]{3,2,1,0:T(2,128)S(1)}, f32[53,4,2,128]{3,2,1,0:T(2,128)S(1)}, u32[]{:S(2)}, u32[]{:S(2)}) collective-permute-start(f32[53,4,2,128]{3,2,1,0:T(2,128)S(1)} %get-tuple-element.276), channel_id=1, source_target_pairs={{0,1},{1,2},{2,3},{3,4},{4,5},{5,6},{6,7},{7,8},{8,9},{9,10},{10,1... | collective-permute-start | bytes 651272 | tf_op jit(solution)/shard_map/ppermute | solution.py:21
  25.4 14.0 %collective-permute-start.3 = (f32[53,4,2,128]{3,2,1,0:T(2,128)S(1)}, f32[53,4,2,128]{3,2,1,0:T(2,128)S(1)}, u32[]{:S(2)}, u32[]{:S(2)}) collective-permute-start(f32[53,4,2,128]{3,2,1,0:T(2,128)S(1)} %get-tuple-element.277), channel_id=1, source_target_pairs={{1,0},{2,1},{3,2},{4,3},{5,4},{6,5},{7,6},{8,7},{9,8},{10,9},{11,1... | collective-permute-start | bytes 651272 | tf_op jit(solution)/shard_map/ppermute | solution.py:24
  29.7 15.9 %all-to-all-start.1 = ((f32[1,16,1,256]{3,2,0,1:T(1,128)}), f32[1,16,1,256]{3,2,0,1:T(1,128)S(1)}, u32[]{:S(2)}, u32[]{:S(2)}) async-start(f32[1,16,1,256]{3,2,0,1:T(1,128)} %copy.150), calls=%async_computation.1 | async-start | bytes 32768 | tf_op jit(solution)/shard_map/all_to_all | solution.py:145
  37.2 0.8 copy-start.1
  37.2 0.8 copy-start.8
  38.1 1.1 copy-start
  45.6 6.1 %copy-start.4 = (s32[325,2]{0,1:T(2,128)S(1)}, s32[325,2]{0,1:T(2,128)}, u32[]{:S(2)}) copy-start(s32[325,2]{0,1:T(2,128)} %param.18) | copy-start | bytes 7804
  45.6 6.1 %copy-start.5 = (s32[325,2]{0,1:T(2,128)S(1)}, s32[325,2]{0,1:T(2,128)}, u32[]{:S(2)}) copy-start(s32[325,2]{0,1:T(2,128)} %param.17) | copy-start | bytes 7804
  45.6 19.6 %all-to-all-start = ((f32[53,16,1,256]{3,2,0,1:T(1,128)}), f32[53,16,1,256]{3,2,0,1:T(1,128)S(1)}, u32[]{:S(2)}, u32[]{:S(2)}) async-start(f32[53,16,1,256]{3,2,0,1:T(1,128)} %copy.146), calls=%async_computation | async-start | bytes 1736704 | tf_op jit(solution)/shard_map/all_to_all | solution.py:144
  66.1 0.7 copy-start.6
  66.1 0.7 copy-start.7
  100.9 18.2 %all-to-all-start.2 = ((f32[53,16,1,256]{3,2,0,1:T(1,128)}), f32[53,16,1,256]{3,2,0,1:T(1,128)S(1)}, u32[]{:S(2)}, u32[]{:S(2)}) async-start(f32[53,16,1,256]{3,2,0,1:T(1,128)} %copy.153), calls=%async_computation.2 | async-start | bytes 1736704 | tf_op jit(solution)/shard_map/all_to_all | solution.py:171
where the time goes:
time: 122 us
  starting transfers between devices  42.9 us (35%)
  matrix products  29.3 us (24%)
  waiting for transfers between devices  26.3 us (22%)
  local copies, waits for them, and re-layouts  17.1 us (14%)
  other arithmetic  4.76 us (4%)
    ppermute x2, starting transfers between devices, with_halo(): lax.ppermute(lax.slice_in_dim(block, 0, width, axis=dim), axis, backward)  17.6 us
    dot_general x20, matrix products, react(): jnp.dot(forward, logged, preferred_element_type=jnp.float32, precision=la...  16.6 us
    all_to_all x1, waiting for transfers between devices, remote_chemistry(): lax.all_to_all(returning, 'chem', split_axis=1, concat_axis=1, tiled=True)  13.4 us
    all_to_all x1, waiting for transfers between devices, remote_chemistry(): lax.all_to_all(outgoing, 'chem', split_axis=1, concat_axis=1, tiled=True)  12.9 us
    dot_general x20, matrix products, react(): jnp.dot(net_change, progress, preferred_element_type=jnp.float32, precisi...  12.6 us
    ppermute x2, starting transfers between devices, with_halo(): lax.ppermute(lax.slice_in_dim(block, block.shape[dim] - width, None, axis...  8.18 us
    all_to_all x1, starting transfers between devices, remote_chemistry(): lax.all_to_all(exported_enthalpy, 'chem', split_axis=1, concat_axis=1, ti...  6.84 us
    all_to_all x1, starting transfers between devices, remote_chemistry(): lax.all_to_all(outgoing, 'chem', split_axis=1, concat_axis=1, tiled=True)  5.91 us
  transfers between devices with their start and end apart: 7, of which 2 were waited for; matrix products, arithmetic and copies ran while one was open for 9% of the time, Pallas kernels for 0%

commit v1 on v0

v1 whole, which is shorter than its diff:
```python
import jax
import jax.numpy as jnp
from jax import lax
from jax.experimental import pallas as pl
from jax.experimental.pallas import tpu as pltpu
from jax.sharding import PartitionSpec as P

PATCHES_ON_UNIT = 14
SUBSTEPS = 4
LOG2E = 1.4426950408889634
CONC_FLOOR = 0.1
CHEM_DT = 0.04
ROWS = 64
LANES = 128


def ring(axis):
    count = lax.axis_size(axis)
    forward = [(i, (i + 1) % count) for i in range(count)]
    return forward, [(target, source) for source, target in forward]


def pieces(values):
    high = lax.reduce_precision(values, 8, 7)
    middle = lax.reduce_precision(values - high, 8, 7)
    return high, middle, values - high - middle


def tables(consumed, resulting, ln_amplitude, energy, species):
    count = consumed.shape[0]
    padded = -(-count // 16) * 16
    ids = jnp.arange(ROWS, dtype=jnp.int32)
    used = (consumed[:, 0:1] == ids).astype(jnp.float32) + (consumed[:, 1:2] == ids).astype(jnp.float32)
    a_high, a_middle, a_low = pieces(ln_amplitude * LOG2E)
    e_high, e_middle, e_low = pieces(energy * -LOG2E)
    spare = jnp.stack([a_high, e_high, a_middle, a_low, e_middle, e_low], axis=1)
    spare = jnp.pad(spare, ((0, 0), (species, ROWS - species - 6)))
    gather = jnp.concatenate([used + spare, used + spare], axis=1)
    gather = jnp.pad(gather, ((0, padded - count), (0, 0))).astype(jnp.bfloat16)
    takes = consumed.T
    gives = resulting.T
    change = (
        (gives[0:1] == ids[:, None]).astype(jnp.float32)
        + (gives[1:2] == ids[:, None]).astype(jnp.float32)
        - (takes[0:1] == ids[:, None]).astype(jnp.float32)
        - (takes[1:2] == ids[:, None]).astype(jnp.float32)
    )
    change = jnp.pad(change, ((0, 0), (0, padded - count)))
    return gather, jnp.concatenate([change, change], axis=1).astype(jnp.bfloat16)


def split(values):
    high = values.astype(jnp.bfloat16)
    low = (values - high.astype(jnp.float32)).astype(jnp.bfloat16)
    return jnp.concatenate([high, low], axis=0)


def step_kernel(
    u_ref, xlo_ref, xhi_ref, ylo_ref, yhi_ref, field_ref, spread_ref, gather_ref, change_ref, out_ref, wide_ref
):
    species, depth, width, lanes = u_ref.shape
    stride = depth + 4
    slab = wide_ref.shape[1]

    def fill(ref, y_offset, x_offset):
        _, ys, xs, _ = ref.shape
        flat = ref.reshape(species * ys * xs, lanes)
        for y in range(ys):
            for x in range(xs):
                wide_ref[(x + x_offset) * stride + y + y_offset, 0:species, :] = flat[
                    pl.ds(y * xs + x, species, stride=ys * xs), :
                ]

    fill(u_ref, 2, 2)
    fill(xlo_ref, 2, 0)
    fill(xhi_ref, 2, width + 2)
    fill(ylo_ref, 0, 2)
    fill(yhi_ref, depth + 2, 2)

    out_flat = out_ref.reshape(species * depth * width, lanes)
    spread = spread_ref[...] * (1.0 / 12.0)

    def advect(row, field):
        x = row // depth
        y = row - x * depth
        base = (x + 2) * stride + y + 2
        center = wide_ref[base]
        near = jnp.zeros_like(center)
        far = jnp.zeros_like(center)
        moved = jnp.zeros_like(center)
        for axis in range(3):
            if axis == 2:
                low2 = pltpu.roll(center, 2, 1)
                low1 = pltpu.roll(center, 1, 1)
                high1 = pltpu.roll(center, lanes - 1, 1)
                high2 = pltpu.roll(center, lanes - 2, 1)
            else:
                hop = stride if axis == 0 else 1
                low2 = wide_ref[base - 2 * hop]
                low1 = wide_ref[base - hop]
                high1 = wide_ref[base + hop]
                high2 = wide_ref[base + 2 * hop]
            speed = field[axis : axis + 1] * (1.0 / 12.0)
            moved = moved + speed * (8.0 * (high1 - low1) - (high2 - low2))
            near = near + (high1 + low1)
            far = far + (high2 + low2)
        return center - moved + spread * (16.0 * near - far - 90.0 * center)

    row_ids = lax.broadcasted_iota(jnp.int32, (16, 2 * lanes), 0) + (ROWS - 16)
    is_species = row_ids < species
    is_one = (row_ids == species) | (row_ids == species + 2) | (row_ids == species + 3)
    is_heat = (row_ids == species + 1) | (row_ids == species + 4) | (row_ids == species + 5)

    def block(b, carry):
        field = field_ref[b]
        advected = jnp.concatenate(
            [advect(2 * b + k, field[:, k * lanes : (k + 1) * lanes]) for k in range(2)], axis=1
        )
        advected = jnp.concatenate(
            [advected, jnp.zeros((ROWS - slab, 2 * lanes), jnp.float32)], axis=0
        )
        spare = jnp.where(is_one, 1.0, jnp.where(is_heat, field[3:4], 0.0))
        current = advected
        for _ in range(SUBSTEPS):
            logged = jnp.log(jnp.maximum(current, CONC_FLOOR)) * LOG2E
            stacked = jnp.concatenate(
                [logged[: ROWS - 16], jnp.where(is_species, logged[ROWS - 16 :], spare)], axis=0
            )
            exponent = jnp.dot(gather_ref[...], split(stacked), preferred_element_type=jnp.float32)
            progress = jnp.exp2(jnp.minimum(exponent, LOG2E))
            current = current + CHEM_DT * jnp.dot(
                change_ref[...], split(progress), preferred_element_type=jnp.float32
            )
        result = jnp.where(field[4:5] > 0.5, current, advected)
        for k in range(2):
            row = 2 * b + k
            x = row // depth
            y = row - x * depth
            out_flat[pl.ds(y * width + x, species, stride=depth * width), :] = result[
                0:species, k * lanes : (k + 1) * lanes
            ]
        return carry

    lax.fori_loop(0, PATCHES_ON_UNIT, block, 0)


def per_device(
    molar_fractions,
    fluid_speed_vector,
    thermal_state,
    molecular_spreading,
    arrhenius_ln_amplitude,
    arrhenius_energy,
    consumed_molecules,
    resulting_molecules,
    patch_assignee,
):
    species, width, depth, lanes = molar_fractions.shape
    cells = molar_fractions.transpose(0, 2, 1, 3)
    flow_next, flow_back = ring("flow")
    chem_next, chem_back = ring("chem")
    xlo = lax.ppermute(cells[:, :, width - 2 :], "flow", flow_next)
    xhi = lax.ppermute(cells[:, :, :2], "flow", flow_back)
    ylo = lax.ppermute(cells[:, depth - 2 :], "chem", chem_next)
    yhi = lax.ppermute(cells[:, :2], "chem", chem_back)

    gather, change = tables(
        consumed_molecules, resulting_molecules, arrhenius_ln_amplitude, arrhenius_energy, species
    )
    workers = lax.axis_size("chem")
    owners = lax.dynamic_slice_in_dim(
        patch_assignee[0], lax.axis_index("chem") * PATCHES_ON_UNIT, PATCHES_ON_UNIT
    )
    active = (owners < workers).astype(jnp.float32)
    points = width * depth * lanes // PATCHES_ON_UNIT
    field = jnp.concatenate(
        [
            fluid_speed_vector.reshape(3, PATCHES_ON_UNIT, points),
            (1.0 / thermal_state).reshape(1, PATCHES_ON_UNIT, points),
            jnp.broadcast_to(active[None, :, None], (1, PATCHES_ON_UNIT, points)),
            jnp.zeros((3, PATCHES_ON_UNIT, points), jnp.float32),
        ],
        axis=0,
    ).transpose(1, 0, 2)
    slab = -(-species // 8) * 8
    spread = jnp.broadcast_to(
        jnp.pad(molecular_spreading, (0, slab - species))[:, None], (slab, LANES)
    )
    out = pl.pallas_call(
        step_kernel,
        out_shape=jax.ShapeDtypeStruct(cells.shape, jnp.float32),
        scratch_shapes=[pltpu.VMEM(((width + 4) * (depth + 4), slab, lanes), jnp.float32)],
        name="step",
    )(cells, xlo, xhi, ylo, yhi, field, spread, gather, change)
    return out.transpose(0, 2, 1, 3)


def solution(mesh):
    in_specs = (
        P(None, "flow", "chem", None),
        P(None, "flow", "chem", None),
        P("flow", "chem", None),
        P(),
        P(),
        P(),
        P(),
        P(),
        P("flow", None),
    )
    out_specs = P(None, "flow", "chem", None)
    return jax.shard_map(
        per_device, mesh=mesh, in_specs=in_specs, out_specs=out_specs, check_vma=False
    )
```

time: 122 us -> 78.7 us (0.65)
  the two profiles are of different devices: /device:TPU:1 before, /device:TPU:6 now
where the time goes in v1:
time: 78.7 us; the launch traced here: 78.2 us
  Pallas kernels  27.9 us (35%)
  starting transfers between devices  24.5 us (31%)
  waiting for transfers between devices  16.4 us (21%)
  local copies, waits for them, and re-layouts  6.66 us (8%)
  other arithmetic  2.55 us (3%)
    pallas_call x1, Pallas kernels, per_device(): pl.pallas_call(step_kernel, out_shape=jax.ShapeDtypeStruct(cells.shape, j...  27.9 us
    ppermute x1, starting transfers between devices, per_device(): xhi = lax.ppermute(cells[:, :, :2], 'flow', flow_back)  17.5 us
    ppermute x1, waiting for transfers between devices, per_device(): xlo = lax.ppermute(cells[:, :, width - 2:], 'flow', flow_next)  11.6 us
    ppermute x1, waiting for transfers between devices, per_device(): xhi = lax.ppermute(cells[:, :, :2], 'flow', flow_back)  4.76 us
    unnamed x27, local copies, waits for them, and re-layouts  3.98 us
    ppermute x1, starting transfers between devices, per_device(): yhi = lax.ppermute(cells[:, :2], 'chem', chem_back)  3.19 us
    ppermute x1, starting transfers between devices, per_device(): ylo = lax.ppermute(cells[:, depth - 2:], 'chem', chem_next)  1.92 us
    ppermute x1, starting transfers between devices, per_device(): xlo = lax.ppermute(cells[:, :, width - 2:], 'flow', flow_next)  1.92 us
  transfers between devices with their start and end apart: 4, of which 2 were waited for; matrix products, arithmetic and copies ran while one was open for 4% of the time, Pallas kernels for 0%

profile of v1, /device:TPU:6, one launch (start us, length us, event | category | flops | bytes accessed | tf_op | source)
XLA Modules:
  0.0 78.2 jit_solution(2579534260083758118)
XLA Ops:
  0.0 1.1 %fusion.6 = (f32[53,2,4,128]{3,2,1,0:T(4,128)S(1)}, f32[53,2,4,128]{3,2,1,0:T(4,128)S(1)}) fusion(f32[53,7,4,128]{3,2,1,0:T(4,128)} %bitcast.8), kind=kLoop, calls=%fused_computation.32 | loop fusion | bytes 868352 | tf_op jit(solution)/shard_map/slice | solution.py:165
  1.2 3.2 %collective-permute-start.3 = (f32[53,2,4,128]{3,2,1,0:T(4,128)S(1)}, f32[53,2,4,128]{3,2,1,0:T(4,128)S(1)}, u32[]{:S(2)}, u32[]{:S(2)}) collective-permute-start(f32[53,2,4,128]{3,2,1,0:T(4,128)S(1)} %get-tuple-element.11), channel_id=1, source_target_pairs={{1,0},{2,1},{3,2},{4,3},{5,4},{6,5},{7,6},{8,7},{9,8},{10,9},{11,1... | collective-permute-start | bytes 651272 | tf_op jit(solution)/shard_map/ppermute | solution.py:165
  4.4 1.9 %collective-permute-start.2 = (f32[53,2,4,128]{3,2,1,0:T(4,128)S(1)}, f32[53,2,4,128]{3,2,1,0:T(4,128)S(1)}, u32[]{:S(2)}, u32[]{:S(2)}) collective-permute-start(f32[53,2,4,128]{3,2,1,0:T(4,128)S(1)} %get-tuple-element.12), channel_id=1, source_target_pairs={{0,1},{1,2},{2,3},{3,4},{4,5},{5,6},{6,7},{7,8},{8,9},{9,10},{10,1... | collective-permute-start | bytes 651272 | tf_op jit(solution)/shard_map/ppermute | solution.py:164
  6.3 0.0 copy-done
  6.3 0.3 fusion.7
  6.6 17.5 %collective-permute-start.1 = (f32[53,7,2,128]{3,2,1,0:T(2,128)S(1)}, f32[53,7,2,128]{3,2,1,0:T(2,128)S(1)}, u32[]{:S(2)}, u32[]{:S(2)}) collective-permute-start(f32[53,7,2,128]{3,2,1,0:T(2,128)S(1)} %get-tuple-element.13), channel_id=1, source_target_pairs={{16,0},{32,16},{48,32},{64,48},{80,64},{96,80},{112,96},{128,112},... | collective-permute-start | bytes 1139720 | tf_op jit(solution)/shard_map/ppermute | solution.py:163
  24.1 1.9 %collective-permute-start = (f32[53,7,2,128]{3,2,1,0:T(2,128)S(1)}, f32[53,7,2,128]{3,2,1,0:T(2,128)S(1)}, u32[]{:S(2)}, u32[]{:S(2)}) collective-permute-start(f32[53,7,2,128]{3,2,1,0:T(2,128)S(1)} %get-tuple-element.14), channel_id=1, source_target_pairs={{0,16},{16,32},{32,48},{48,64},{64,80},{80,96},{96,112},{112,128},... | collective-permute-start | bytes 1139720 | tf_op jit(solution)/shard_map/ppermute | solution.py:162
  26.0 0.0 copy-start.7
  26.0 0.7 copy-done.7
  26.7 0.7 copy-done.9
  27.5 0.6 copy-done.6
  28.1 0.0 copy-start.8
  28.2 0.7 copy-done.8
  29.0 0.1 copy.25
  29.1 0.2 add_convert_fusion
  29.3 0.0 copy-start.11
  29.3 0.7 fusion.2.gather_ref
  30.1 0.1 fusion.5
  30.2 0.7 copy-done.5
  30.9 0.0 copy-start.12
  30.9 0.6 copy-done.12
  31.5 0.1 pad.28.clone
  31.6 0.7 pad_maximum_fusion.change_ref
  32.3 0.1 broadcast_in_dim.6
  32.4 0.7 maximum_bitcast_fusion.field_ref
  33.2 0.0 collective-permute-done.3.yhi_ref
  33.2 0.0 collective-permute-done.2.ylo_ref
  33.2 4.8 %collective-permute-done.1.xhi_ref = f32[53,7,2,128]{3,2,1,0:T(2,128)S(1)} collective-permute-done((f32[53,7,2,128]{3,2,1,0:T(2,128)S(1)}, f32[53,7,2,128]{3,2,1,0:T(2,128)S(1)}, u32[]{:S(2)}, u32[]{:S(2)}) %collective-permute-start.1) | collective-permute-done | bytes 379936 | tf_op jit(solution)/shard_map/ppermute | solution.py:163
  37.9 11.6 %collective-permute-done.xlo_ref = f32[53,7,2,128]{3,2,1,0:T(2,128)S(1)} collective-permute-done((f32[53,7,2,128]{3,2,1,0:T(2,128)S(1)}, f32[53,7,2,128]{3,2,1,0:T(2,128)S(1)}, u32[]{:S(2)}, u32[]{:S(2)}) %collective-permute-start) | collective-permute-done | bytes 379936 | tf_op jit(solution)/shard_map/ppermute | solution.py:162
  49.6 0.8 broadcast_in_dim.8.spread_ref
  50.3 0.0 copy-done.2
  50.3 27.9 %step.1 = f32[53,7,4,128]{3,2,1,0:T(4,128)} custom-call(f32[53,7,4,128]{3,2,1,0:T(4,128)} %bitcast.9, f32[53,7,2,128]{3,2,1,0:T(2,128)} %copy-done.2, f32[53,7,2,128]{3,2,1,0:T(2,128)} %copy-done.1, f32[53,2,4,128]{3,2,1,0:T(4,128)} %copy-done.4, f32[53,2,4,128]{3,2,1,0:T(4,128)} %copy-done.3, f32[14,8,256]{2,1,0:T(8,128)} %maximum_bitcast_fusion.field_ref, ...), custom_call_target="tpu_custom_call" | custom-call | tf_op jit(solution)/shard_map/step/pallas_call | solution.py:189
  (35 shorter events, 0.3 us)
Async XLA Ops:
  0.0 6.3 %copy-start = (f32[53,4,7,128]{3,1,2,0:T(4,128)S(1)}, f32[53,4,7,128]{3,1,2,0:T(4,128)}, u32[]{:S(2)}) copy-start(f32[53,4,7,128]{3,1,2,0:T(4,128)} %param.9) | copy-start | bytes 2279428
  1.2 32.0 %collective-permute-start.3 = (f32[53,2,4,128]{3,2,1,0:T(4,128)S(1)}, f32[53,2,4,128]{3,2,1,0:T(4,128)S(1)}, u32[]{:S(2)}, u32[]{:S(2)}) collective-permute-start(f32[53,2,4,128]{3,2,1,0:T(4,128)S(1)} %get-tuple-element.11), channel_id=1, source_target_pairs={{1,0},{2,1},{3,2},{4,3},{5,4},{6,5},{7,6},{8,7},{9,8},{10,9},{11,1... | collective-permute-start | bytes 651272 | tf_op jit(solution)/shard_map/ppermute | solution.py:165
  4.4 28.8 %collective-permute-start.2 = (f32[53,2,4,128]{3,2,1,0:T(4,128)S(1)}, f32[53,2,4,128]{3,2,1,0:T(4,128)S(1)}, u32[]{:S(2)}, u32[]{:S(2)}) collective-permute-start(f32[53,2,4,128]{3,2,1,0:T(4,128)S(1)} %get-tuple-element.12), channel_id=1, source_target_pairs={{0,1},{1,2},{2,3},{3,4},{4,5},{5,6},{6,7},{7,8},{8,9},{9,10},{10,1... | collective-permute-start | bytes 651272 | tf_op jit(solution)/shard_map/ppermute | solution.py:164
  6.6 31.3 %collective-permute-start.1 = (f32[53,7,2,128]{3,2,1,0:T(2,128)S(1)}, f32[53,7,2,128]{3,2,1,0:T(2,128)S(1)}, u32[]{:S(2)}, u32[]{:S(2)}) collective-permute-start(f32[53,7,2,128]{3,2,1,0:T(2,128)S(1)} %get-tuple-element.13), channel_id=1, source_target_pairs={{16,0},{32,16},{48,32},{64,48},{80,64},{96,80},{112,96},{128,112},... | collective-permute-start | bytes 1139720 | tf_op jit(solution)/shard_map/ppermute | solution.py:163
  24.1 25.5 %collective-permute-start = (f32[53,7,2,128]{3,2,1,0:T(2,128)S(1)}, f32[53,7,2,128]{3,2,1,0:T(2,128)S(1)}, u32[]{:S(2)}, u32[]{:S(2)}) collective-permute-start(f32[53,7,2,128]{3,2,1,0:T(2,128)S(1)} %get-tuple-element.14), channel_id=1, source_target_pairs={{0,16},{16,32},{32,48},{48,64},{64,80},{80,96},{96,112},{112,128},... | collective-permute-start | bytes 1139720 | tf_op jit(solution)/shard_map/ppermute | solution.py:162
  26.0 0.7 copy-start.7
  26.7 0.7 copy-start.9
  26.7 0.7 copy-start.10
  27.4 0.7 copy-start.6
  28.1 0.7 copy-start.8
  29.3 0.7 copy-start.11
  30.1 0.8 %copy-start.5 = (f32[3,4,7,128]{3,1,2,0:T(4,128)S(1)}, f32[3,4,7,128]{3,1,2,0:T(4,128)}, u32[]{:S(2)}) copy-start(f32[3,4,7,128]{3,1,2,0:T(4,128)} %param.10) | copy-start | bytes 129028
  30.9 0.7 copy-start.12
  33.2 17.2 %copy-start.3 = (f32[53,2,4,128]{3,2,1,0:T(4,128)}, f32[53,2,4,128]{3,2,1,0:T(4,128)S(1)}, u32[]{:S(2)}) copy-start(f32[53,2,4,128]{3,2,1,0:T(4,128)S(1)} %collective-permute-done.3.yhi_ref) | copy-start | bytes 651268
  33.2 17.2 %copy-start.4 = (f32[53,2,4,128]{3,2,1,0:T(4,128)}, f32[53,2,4,128]{3,2,1,0:T(4,128)S(1)}, u32[]{:S(2)}) copy-start(f32[53,2,4,128]{3,2,1,0:T(4,128)S(1)} %collective-permute-done.2.ylo_ref) | copy-start | bytes 651268
  37.9 12.4 %copy-start.1 = (f32[53,7,2,128]{3,2,1,0:T(2,128)}, f32[53,7,2,128]{3,2,1,0:T(2,128)S(1)}, u32[]{:S(2)}) copy-start(f32[53,7,2,128]{3,2,1,0:T(2,128)S(1)} %collective-permute-done.1.xhi_ref) | copy-start | bytes 1139716
  49.6 0.8 copy-start.2

commit v2 on v1

--- a/solution.py
+++ b/solution.py
@@ -1,3 +1,5 @@
+import functools
+
 import jax
 import jax.numpy as jnp
 from jax import lax
@@ -11,7 +13,7 @@
 CONC_FLOOR = 0.1
 CHEM_DT = 0.04
 ROWS = 64
-LANES = 128
+CHUNKS = 3
 
 
 def ring(axis):
@@ -28,7 +30,8 @@
 
 def tables(consumed, resulting, ln_amplitude, energy, species):
     count = consumed.shape[0]
-    padded = -(-count // 16) * 16
+    step = 16 * CHUNKS
+    padded = -(-count // step) * step
     ids = jnp.arange(ROWS, dtype=jnp.int32)
     used = (consumed[:, 0:1] == ids).astype(jnp.float32) + (consumed[:, 1:2] == ids).astype(jnp.float32)
     a_high, a_middle, a_low = pieces(ln_amplitude * LOG2E)
@@ -46,7 +49,8 @@
         - (takes[1:2] == ids[:, None]).astype(jnp.float32)
     )
     change = jnp.pad(change, ((0, 0), (0, padded - count)))
-    return gather, jnp.concatenate([change, change], axis=1).astype(jnp.bfloat16)
+    change = change.reshape(ROWS, CHUNKS, padded // CHUNKS).transpose(1, 0, 2)
+    return gather, jnp.concatenate([change, change], axis=2).astype(jnp.bfloat16)
 
 
 def split(values):
@@ -55,29 +59,27 @@
     return jnp.concatenate([high, low], axis=0)
 
 
-def step_kernel(
-    u_ref, xlo_ref, xhi_ref, ylo_ref, yhi_ref, field_ref, spread_ref, gather_ref, change_ref, out_ref, wide_ref
-):
+def half_kernel(first_x, *refs):
+    u_ref, side_ref, ylo_ref, yhi_ref, field_ref, spread_ref, gather_ref, change_ref = refs[:8]
+    out_ref, wide_ref, advected_ref, current_ref = refs[-4:]
     species, depth, width, lanes = u_ref.shape
+    tiles = field_ref.shape[0]
     stride = depth + 4
     slab = wide_ref.shape[1]
 
-    def fill(ref, y_offset, x_offset):
-        _, ys, xs, _ = ref.shape
-        flat = ref.reshape(species * ys * xs, lanes)
-        for y in range(ys):
-            for x in range(xs):
-                wide_ref[(x + x_offset) * stride + y + y_offset, 0:species, :] = flat[
-                    pl.ds(y * xs + x, species, stride=ys * xs), :
+    def fill(ref, ys, xs, y_offset, slot):
+        _, all_y, all_x, _ = ref.shape
+        flat = ref.reshape(species * all_y * all_x, lanes)
+        for y in ys:
+            for k, x in enumerate(xs):
+                wide_ref[(slot + k) * stride + y + y_offset, 0:species, :] = flat[
+                    pl.ds(y * all_x + x, species, stride=all_y * all_x), :
                 ]
 
-    fill(u_ref, 2, 2)
-    fill(xlo_ref, 2, 0)
-    fill(xhi_ref, 2, width + 2)
-    fill(ylo_ref, 0, 2)
-    fill(yhi_ref, depth + 2, 2)
-
-    out_flat = out_ref.reshape(species * depth * width, lanes)
+    fill(u_ref, range(depth), range(width), 2, 2 - first_x)
+    fill(side_ref, range(depth), range(2), 2, 0 if first_x == 0 else 4)
+    fill(ylo_ref, range(2), (first_x, first_x + 1), 0, 2)
+    fill(yhi_ref, range(2), (first_x, first_x + 1), depth + 2, 2)
     spread = spread_ref[...] * (1.0 / 12.0)
 
     def advect(row, field):
@@ -106,42 +108,79 @@
             far = far + (high2 + low2)
         return center - moved + spread * (16.0 * near - far - 90.0 * center)
 
+    def advect_tile(t, carry):
+        for k in range(2):
+            part = slice(k * lanes, (k + 1) * lanes)
+            advected = advect(2 * t + k, field_ref[t, :, part])
+            current_ref[t, 0:slab, part] = advected
+            advected_ref[t, 0:slab, part] = advected
+        current_ref[t, slab:ROWS] = jnp.zeros((ROWS - slab, 2 * lanes), jnp.float32)
+        return carry
+
+    lax.fori_loop(0, tiles, advect_tile, 0)
+
     row_ids = lax.broadcasted_iota(jnp.int32, (16, 2 * lanes), 0) + (ROWS - 16)
     is_species = row_ids < species
     is_one = (row_ids == species) | (row_ids == species + 2) | (row_ids == species + 3)
     is_heat = (row_ids == species + 1) | (row_ids == species + 4) | (row_ids == species + 5)
 
-    def block(b, carry):
-        field = field_ref[b]
-        advected = jnp.concatenate(
-            [advect(2 * b + k, field[:, k * lanes : (k + 1) * lanes]) for k in range(2)], axis=1
+    def exponent(t):
+        logged = jnp.log(jnp.maximum(current_ref[t], CONC_FLOOR)) * LOG2E
+        spare = jnp.where(is_one, 1.0, jnp.where(is_heat, field_ref[t, 3:4], 0.0))
+        stacked = jnp.concatenate(
+            [logged[: ROWS - 16], jnp.where(is_species, logged[ROWS - 16 :], spare)], axis=0
         )
-        advected = jnp.concatenate(
-            [advected, jnp.zeros((ROWS - slab, 2 * lanes), jnp.float32)], axis=0
-        )
-        spare = jnp.where(is_one, 1.0, jnp.where(is_heat, field[3:4], 0.0))
-        current = advected
-        for _ in range(SUBSTEPS):
-            logged = jnp.log(jnp.maximum(current, CONC_FLOOR)) * LOG2E
-            stacked = jnp.concatenate(
-                [logged[: ROWS - 16], jnp.where(is_species, logged[ROWS - 16 :], spare)], axis=0
-            )
-            exponent = jnp.dot(gather_ref[...], split(stacked), preferred_element_type=jnp.float32)
-            progress = jnp.exp2(jnp.minimum(exponent, LOG2E))
-            current = current + CHEM_DT * jnp.dot(
-                change_ref[...], split(progress), preferred_element_type=jnp.float32
-            )
-        result = jnp.where(field[4:5] > 0.5, current, advected)
-        for k in range(2):
-            row = 2 * b + k
-            x = row // depth
-            y = row - x * depth
-            out_flat[pl.ds(y * width + x, species, stride=depth * width), :] = result[
-                0:species, k * lanes : (k + 1) * lanes
-            ]
+        return jnp.dot(gather_ref[...], split(stacked), preferred_element_type=jnp.float32)
+
+    size = gather_ref.shape[0] // CHUNKS
+
+    def gained(powers):
+        total = None
+        for j in range(CHUNKS):
+            progress = jnp.exp2(jnp.minimum(powers[j * size : (j + 1) * size], LOG2E))
+            part = jnp.dot(change_ref[j], split(progress), preferred_element_type=jnp.float32)
+            total = part if total is None else total + part
+        return CHEM_DT * total
+
+    def substep(i, carry):
+        ready = exponent(0)
+        for t in range(tiles):
+            powers = ready
+            if t + 1 < tiles:
+                ready = exponent(t + 1)
+            current_ref[t] = current_ref[t] + gained(powers)
         return carry
 
-    lax.fori_loop(0, PATCHES_ON_UNIT, block, 0)
+    lax.fori_loop(0, SUBSTEPS, substep, 0)
+
+    for t in range(tiles):
+        result = jnp.where(field_ref[t, 4:5] > 0.5, current_ref[t], advected_ref[t])
+        if first_x != 0:
+            out_ref[t] = result
+            continue
+        out_flat = out_ref.reshape(species * depth * width, lanes)
+        for values, shift in ((result, 0), (refs[8][t], 2)):
+            for k in range(2):
+                x, y = divmod(2 * t + k, depth)
+                out_flat[pl.ds(y * width + x + shift, species, stride=depth * width), :] = values[
+                    0:species, k * lanes : (k + 1) * lanes
+                ]
+
+
+def half(first_x, cells, side, ylo, yhi, field, spread, gather, change, *other):
+    _, depth, _, lanes = cells.shape
+    tiles = field.shape[0]
+    block = (tiles, ROWS, 2 * lanes)
+    shape = block if first_x else cells.shape
+    return pl.pallas_call(
+        functools.partial(half_kernel, first_x),
+        out_shape=jax.ShapeDtypeStruct(shape, jnp.float32),
+        scratch_shapes=[
+            pltpu.VMEM((6 * (depth + 4), spread.shape[0], lanes), jnp.float32),
+            pltpu.VMEM(block, jnp.float32),
+            pltpu.VMEM(block, jnp.float32),
+        ],
+    )(cells, side, ylo, yhi, field, spread, gather, change, *other)
 
 
 def per_device(
@@ -184,14 +223,11 @@
     ).transpose(1, 0, 2)
     slab = -(-species // 8) * 8
     spread = jnp.broadcast_to(
-        jnp.pad(molecular_spreading, (0, slab - species))[:, None], (slab, LANES)
-    )
-    out = pl.pallas_call(
-        step_kernel,
-        out_shape=jax.ShapeDtypeStruct(cells.shape, jnp.float32),
-        scratch_shapes=[pltpu.VMEM(((width + 4) * (depth + 4), slab, lanes), jnp.float32)],
-        name="step",
-    )(cells, xlo, xhi, ylo, yhi, field, spread, gather, change)
+        jnp.pad(molecular_spreading, (0, slab - species))[:, None], (slab, lanes)
+    )
+    middle = PATCHES_ON_UNIT // 2
+    upper = half(2, cells, xhi, ylo, yhi, field[middle:], spread, gather, change)
+    out = half(0, cells, xlo, ylo, yhi, field[:middle], spread, gather, change, upper)
     return out.transpose(0, 2, 1, 3)
 
 

time: 78.7 us -> 58.6 us (0.74)
  the two profiles are of different devices: /device:TPU:6 before, /device:TPU:2 now
where the time goes in v2:
time: 58.6 us; the launch traced here: 58.1 us
  starting transfers between devices  24.5 us (42%)
  Pallas kernels  15.3 us (26%)
  local copies, waits for them, and re-layouts  8.81 us (15%)
  waiting for transfers between devices  7.33 us (13%)
  other arithmetic  1.9 us (3%)
    ppermute x1, starting transfers between devices, per_device(): xhi = lax.ppermute(cells[:, :, :2], 'flow', flow_back)  17.8 us
    pallas_call x2, Pallas kernels, half(): pl.pallas_call(functools.partial(half_kernel, first_x), out_shape=jax.Sha...  15.3 us
    unnamed x27, local copies, waits for them, and re-layouts  5.42 us
    ppermute x1, waiting for transfers between devices, per_device(): xhi = lax.ppermute(cells[:, :, :2], 'flow', flow_back)  4.24 us
    ppermute x1, waiting for transfers between devices, per_device(): xlo = lax.ppermute(cells[:, :, width - 2:], 'flow', flow_next)  3.08 us
    ppermute x1, starting transfers between devices, per_device(): yhi = lax.ppermute(cells[:, :2], 'chem', chem_back)  2.9 us
    ppermute x1, starting transfers between devices, per_device(): ylo = lax.ppermute(cells[:, depth - 2:], 'chem', chem_next)  1.92 us
    ppermute x1, starting transfers between devices, per_device(): xlo = lax.ppermute(cells[:, :, width - 2:], 'flow', flow_next)  1.92 us
  transfers between devices with their start and end apart: 4, of which 2 were waited for; matrix products, arithmetic and copies ran while one was open for 7% of the time, Pallas kernels for 13%

profile of v2, /device:TPU:2, one launch (start us, length us, event | category | flops | bytes accessed | tf_op | source)
XLA Modules:
  0.0 58.1 jit_solution(462817208760318322)
XLA Ops:
  0.0 1.1 %fusion.7 = (f32[53,2,4,128]{3,2,1,0:T(4,128)S(1)}, f32[53,2,4,128]{3,2,1,0:T(4,128)S(1)}) fusion(f32[53,7,4,128]{3,2,1,0:T(4,128)} %bitcast.11), kind=kLoop, calls=%fused_computation.34 | loop fusion | bytes 868352 | tf_op jit(solution)/shard_map/slice | solution.py:204
  1.2 2.9 %collective-permute-start.2 = (f32[53,2,4,128]{3,2,1,0:T(4,128)S(1)}, f32[53,2,4,128]{3,2,1,0:T(4,128)S(1)}, u32[]{:S(2)}, u32[]{:S(2)}) collective-permute-start(f32[53,2,4,128]{3,2,1,0:T(4,128)S(1)} %get-tuple-element.13), channel_id=1, source_target_pairs={{1,0},{2,1},{3,2},{4,3},{5,4},{6,5},{7,6},{8,7},{9,8},{10,9},{11,1... | collective-permute-start | bytes 651272 | tf_op jit(solution)/shard_map/ppermute | solution.py:204
  4.1 1.9 %collective-permute-start.1 = (f32[53,2,4,128]{3,2,1,0:T(4,128)S(1)}, f32[53,2,4,128]{3,2,1,0:T(4,128)S(1)}, u32[]{:S(2)}, u32[]{:S(2)}) collective-permute-start(f32[53,2,4,128]{3,2,1,0:T(4,128)S(1)} %get-tuple-element.14), channel_id=1, source_target_pairs={{0,1},{1,2},{2,3},{3,4},{4,5},{5,6},{6,7},{7,8},{8,9},{9,10},{10,1... | collective-permute-start | bytes 651272 | tf_op jit(solution)/shard_map/ppermute | solution.py:203
  6.0 0.3 fusion.6
  6.3 17.8 %collective-permute-start.3 = (f32[53,7,2,128]{3,2,1,0:T(2,128)S(1)}, f32[53,7,2,128]{3,2,1,0:T(2,128)S(1)}, u32[]{:S(2)}, u32[]{:S(2)}) collective-permute-start(f32[53,7,2,128]{3,2,1,0:T(2,128)S(1)} %get-tuple-element.11), channel_id=1, source_target_pairs={{16,0},{32,16},{48,32},{64,48},{80,64},{96,80},{112,96},{128,112},... | collective-permute-start | bytes 1139720 | tf_op jit(solution)/shard_map/ppermute | solution.py:202
  24.1 1.9 %collective-permute-start = (f32[53,7,2,128]{3,2,1,0:T(2,128)S(1)}, f32[53,7,2,128]{3,2,1,0:T(2,128)S(1)}, u32[]{:S(2)}, u32[]{:S(2)}) collective-permute-start(f32[53,7,2,128]{3,2,1,0:T(2,128)S(1)} %get-tuple-element.12), channel_id=1, source_target_pairs={{0,16},{16,32},{32,48},{48,64},{64,80},{80,96},{96,112},{112,128},... | collective-permute-start | bytes 1139720 | tf_op jit(solution)/shard_map/ppermute | solution.py:201
  26.0 0.0 copy-start.7
  26.0 0.7 %copy-done.7 = s32[325,2]{0,1:T(2,128)S(1)} copy-done((s32[325,2]{0,1:T(2,128)S(1)}, s32[325,2]{0,1:T(2,128)}, u32[]{:S(2)}) %copy-start.7) | copy-done | bytes 2624
  26.7 0.7 %copy-done.9 = f32[325]{0:T(512)S(1)} copy-done((f32[325]{0:T(512)S(1)}, f32[325]{0:T(512)}, u32[]{:S(2)}) %copy-start.9) | copy-done | bytes 1324
  27.5 0.6 %copy-done.6 = f32[4,7,128]{2,0,1:T(4,128)S(1)} copy-done((f32[4,7,128]{2,0,1:T(4,128)S(1)}, f32[4,7,128]{2,0,1:T(4,128)}, u32[]{:S(2)}) %copy-start.6) | copy-done | bytes 14360
  28.2 0.7 %copy-done.5 = f32[3,4,7,128]{3,1,2,0:T(4,128)S(1)} copy-done((f32[3,4,7,128]{3,1,2,0:T(4,128)S(1)}, f32[3,4,7,128]{3,1,2,0:T(4,128)}, u32[]{:S(2)}) %copy-start.5) | copy-done | bytes 43032
  29.0 0.1 copy.26
  29.2 0.2 add_convert_fusion
  29.4 0.7 %fusion.2.refs_6_ = bf16[336,128]{1,0:T(8,128)(2,1)} fusion(bf16[325,64]{1,0:T(8,128)(2,1)S(1)} %add_convert_fusion), kind=kLoop, calls=%fused_computation.14 | loop fusion | flops 301056 | bytes 127616 | tf_op jit(solution)/shard_map/concatenate | solution.py:41
  30.1 0.7 %copy-done.11 = s32[1,224]{1,0:T(1,128)S(1)} copy-done((s32[1,224]{1,0:T(1,128)S(1)}, s32[1,224]{1,0:T(1,128)}, u32[]{:S(2)}) %copy-start.11) | copy-done | bytes 920
  30.8 0.1 fusion.5
  30.9 0.1 pad.28.clone
  30.9 0.6 %copy-done.8 = s32[325,2]{0,1:T(2,128)S(1)} copy-done((s32[325,2]{0,1:T(2,128)S(1)}, s32[325,2]{0,1:T(2,128)}, u32[]{:S(2)}) %copy-start.8) | copy-done | bytes 2624
  31.6 0.1 broadcast_in_dim.6
  31.7 0.1 maximum_bitcast_fusion
  31.8 0.6 %copy-done.12 = f32[53]{0:T(128)S(1)} copy-done((f32[53]{0:T(128)S(1)}, f32[53]{0:T(128)}, u32[]{:S(2)}) %copy-start.12) | copy-done | bytes 236
  32.4 0.1 reshape.27
  32.6 0.7 %pad_maximum_fusion.refs_7_ = bf16[3,64,224]{2,1,0:T(8,128)(2,1)} fusion(bf16[3,64,112]{2,1,0:T(8,128)(2,1)S(1)} %bitcast.15), kind=kLoop, calls=%fused_computation.7 | loop fusion | flops 172032 | bytes 129024 | tf_op jit(solution)/shard_map/concatenate | solution.py:53
  33.3 0.7 %fusion.8 = (f32[7,8,256]{2,1,0:T(8,128)}, f32[7,8,256]{2,1,0:T(8,128)}) fusion(f32[14,8,256]{2,1,0:T(8,128)S(1)} %maximum_bitcast_fusion), kind=kLoop, calls=%fused_computation.35 | loop fusion | bytes 229376 | tf_op jit(solution)/shard_map/slice | solution.py:229
  33.9 0.0 collective-permute-done.2.refs_3_
  34.0 4.2 %collective-permute-done.3.refs_1_ = f32[53,7,2,128]{3,2,1,0:T(2,128)S(1)} collective-permute-done((f32[53,7,2,128]{3,2,1,0:T(2,128)S(1)}, f32[53,7,2,128]{3,2,1,0:T(2,128)S(1)}, u32[]{:S(2)}, u32[]{:S(2)}) %collective-permute-start.3) | collective-permute-done | bytes 379936 | tf_op jit(solution)/shard_map/ppermute | solution.py:202
  38.2 0.7 %broadcast_in_dim.8.refs_5_ = f32[56,128]{1,0:T(8,128)} broadcast(f32[56]{0:T(128)S(1)} %pad.17), dimensions={0} | broadcast | bytes 28896 | tf_op jit(solution)/shard_map/broadcast_in_dim | solution.py:225
  38.9 0.0 copy-done.4
  39.0 7.5 %shard_map.91.refs_8_ = f32[7,64,256]{2,1,0:T(8,128)} custom-call(f32[53,7,4,128]{3,2,1,0:T(4,128)} %bitcast.12, f32[53,7,2,128]{3,2,1,0:T(2,128)} %copy-done.4, f32[53,2,4,128]{3,2,1,0:T(4,128)} %copy-done.2, f32[53,2,4,128]{3,2,1,0:T(4,128)} %copy-done.1, f32[7,8,256]{2,1,0:T(8,128)} %get-tuple-element.15.refs_4_, f32[56,128]{1,0:T(8,128)} %broadcast_in_dim.8.refs_5_, ...), custom_call_target="tpu_custom_call" | custom-call | tf_op jit(solution)/shard_map/pallas_call | solution.py:175
  46.5 3.1 %collective-permute-done.refs_1_ = f32[53,7,2,128]{3,2,1,0:T(2,128)S(1)} collective-permute-done((f32[53,7,2,128]{3,2,1,0:T(2,128)S(1)}, f32[53,7,2,128]{3,2,1,0:T(2,128)S(1)}, u32[]{:S(2)}, u32[]{:S(2)}) %collective-permute-start) | collective-permute-done | bytes 379936 | tf_op jit(solution)/shard_map/ppermute | solution.py:201
  49.6 0.7 %copy-done.3 = f32[53,7,2,128]{3,2,1,0:T(2,128)} copy-done((f32[53,7,2,128]{3,2,1,0:T(2,128)}, f32[53,7,2,128]{3,2,1,0:T(2,128)S(1)}, u32[]{:S(2)}) %copy-start.3) | copy-done | bytes 379928
  50.3 7.8 %shard_map.92 = f32[53,7,4,128]{3,2,1,0:T(4,128)} custom-call(f32[53,7,4,128]{3,2,1,0:T(4,128)} %bitcast.13, f32[53,7,2,128]{3,2,1,0:T(2,128)} %copy-done.3, f32[53,2,4,128]{3,2,1,0:T(4,128)} %copy-done.2, f32[53,2,4,128]{3,2,1,0:T(4,128)} %copy-done.1, f32[7,8,256]{2,1,0:T(8,128)} %get-tuple-element.16.refs_4_, f32[56,128]{1,0:T(8,128)} %broadcast_in_dim.8.refs_5_, ...), custom_call_target="tpu_custom_call" | custom-call | tf_op jit(solution)/shard_map/pallas_call | solution.py:175
  (39 shorter events, 0.3 us)
Async XLA Ops:
  0.0 6.0 %copy-start = (f32[53,4,7,128]{3,1,2,0:T(4,128)S(1)}, f32[53,4,7,128]{3,1,2,0:T(4,128)}, u32[]{:S(2)}) copy-start(f32[53,4,7,128]{3,1,2,0:T(4,128)} %param.9) | copy-start | bytes 2279428
  1.2 32.8 %collective-permute-start.2 = (f32[53,2,4,128]{3,2,1,0:T(4,128)S(1)}, f32[53,2,4,128]{3,2,1,0:T(4,128)S(1)}, u32[]{:S(2)}, u32[]{:S(2)}) collective-permute-start(f32[53,2,4,128]{3,2,1,0:T(4,128)S(1)} %get-tuple-element.13), channel_id=1, source_target_pairs={{1,0},{2,1},{3,2},{4,3},{5,4},{6,5},{7,6},{8,7},{9,8},{10,9},{11,1... | collective-permute-start | bytes 651272 | tf_op jit(solution)/shard_map/ppermute | solution.py:204
  4.1 29.9 %collective-permute-start.1 = (f32[53,2,4,128]{3,2,1,0:T(4,128)S(1)}, f32[53,2,4,128]{3,2,1,0:T(4,128)S(1)}, u32[]{:S(2)}, u32[]{:S(2)}) collective-permute-start(f32[53,2,4,128]{3,2,1,0:T(4,128)S(1)} %get-tuple-element.14), channel_id=1, source_target_pairs={{0,1},{1,2},{2,3},{3,4},{4,5},{5,6},{6,7},{7,8},{8,9},{9,10},{10,1... | collective-permute-start | bytes 651272 | tf_op jit(solution)/shard_map/ppermute | solution.py:203
  6.3 31.9 %collective-permute-start.3 = (f32[53,7,2,128]{3,2,1,0:T(2,128)S(1)}, f32[53,7,2,128]{3,2,1,0:T(2,128)S(1)}, u32[]{:S(2)}, u32[]{:S(2)}) collective-permute-start(f32[53,7,2,128]{3,2,1,0:T(2,128)S(1)} %get-tuple-element.11), channel_id=1, source_target_pairs={{16,0},{32,16},{48,32},{64,48},{80,64},{96,80},{112,96},{128,112},... | collective-permute-start | bytes 1139720 | tf_op jit(solution)/shard_map/ppermute | solution.py:202
  24.1 25.5 %collective-permute-start = (f32[53,7,2,128]{3,2,1,0:T(2,128)S(1)}, f32[53,7,2,128]{3,2,1,0:T(2,128)S(1)}, u32[]{:S(2)}, u32[]{:S(2)}) collective-permute-start(f32[53,7,2,128]{3,2,1,0:T(2,128)S(1)} %get-tuple-element.12), channel_id=1, source_target_pairs={{0,16},{16,32},{32,48},{48,64},{64,80},{80,96},{96,112},{112,128},... | collective-permute-start | bytes 1139720 | tf_op jit(solution)/shard_map/ppermute | solution.py:201
  26.0 0.7 %copy-start.7 = (s32[325,2]{0,1:T(2,128)S(1)}, s32[325,2]{0,1:T(2,128)}, u32[]{:S(2)}) copy-start(s32[325,2]{0,1:T(2,128)} %param.15) | copy-start | bytes 7804
  26.7 0.7 %copy-start.9 = (f32[325]{0:T(512)S(1)}, f32[325]{0:T(512)}, u32[]{:S(2)}) copy-start(f32[325]{0:T(512)} %param.13) | copy-start | bytes 3904
  26.7 0.7 %copy-start.10 = (f32[325]{0:T(512)S(1)}, f32[325]{0:T(512)}, u32[]{:S(2)}) copy-start(f32[325]{0:T(512)} %param.14) | copy-start | bytes 3904
  27.4 0.7 %copy-start.6 = (f32[4,7,128]{2,0,1:T(4,128)S(1)}, f32[4,7,128]{2,0,1:T(4,128)}, u32[]{:S(2)}) copy-start(f32[4,7,128]{2,0,1:T(4,128)} %param.11) | copy-start | bytes 43012
  28.1 0.8 %copy-start.5 = (f32[3,4,7,128]{3,1,2,0:T(4,128)S(1)}, f32[3,4,7,128]{3,1,2,0:T(4,128)}, u32[]{:S(2)}) copy-start(f32[3,4,7,128]{3,1,2,0:T(4,128)} %param.10) | copy-start | bytes 129028
  30.1 0.7 %copy-start.11 = (s32[1,224]{1,0:T(1,128)S(1)}, s32[1,224]{1,0:T(1,128)}, u32[]{:S(2)}) copy-start(s32[1,224]{1,0:T(1,128)} %param.17) | copy-start | bytes 2692
  30.9 0.7 %copy-start.8 = (s32[325,2]{0,1:T(2,128)S(1)}, s32[325,2]{0,1:T(2,128)}, u32[]{:S(2)}) copy-start(s32[325,2]{0,1:T(2,128)} %param.16) | copy-start | bytes 7804
  31.8 0.7 %copy-start.12 = (f32[53]{0:T(128)S(1)}, f32[53]{0:T(128)}, u32[]{:S(2)}) copy-start(f32[53]{0:T(128)} %param.12) | copy-start | bytes 640
  33.9 5.0 %copy-start.1 = (f32[53,2,4,128]{3,2,1,0:T(4,128)}, f32[53,2,4,128]{3,2,1,0:T(4,128)S(1)}, u32[]{:S(2)}) copy-start(f32[53,2,4,128]{3,2,1,0:T(4,128)S(1)} %collective-permute-done.2.refs_3_) | copy-start | bytes 651268
  34.0 5.0 %copy-start.2 = (f32[53,2,4,128]{3,2,1,0:T(4,128)}, f32[53,2,4,128]{3,2,1,0:T(4,128)S(1)}, u32[]{:S(2)}) copy-start(f32[53,2,4,128]{3,2,1,0:T(4,128)S(1)} %collective-permute-done.1.refs_2_) | copy-start | bytes 651268
  38.2 0.7 %copy-start.4 = (f32[53,7,2,128]{3,2,1,0:T(2,128)}, f32[53,7,2,128]{3,2,1,0:T(2,128)S(1)}, u32[]{:S(2)}) copy-start(f32[53,7,2,128]{3,2,1,0:T(2,128)S(1)} %collective-permute-done.3.refs_1_) | copy-start | bytes 1139716
  49.6 0.8 %copy-start.3 = (f32[53,7,2,128]{3,2,1,0:T(2,128)}, f32[53,7,2,128]{3,2,1,0:T(2,128)S(1)}, u32[]{:S(2)}) copy-start(f32[53,7,2,128]{3,2,1,0:T(2,128)S(1)} %collective-permute-done.refs_1_) | copy-start | bytes 1139716

commit v3 on v2

v3 whole, which is shorter than its diff:
```python
import functools

import jax
import jax.numpy as jnp
from jax import lax
from jax.experimental import pallas as pl
from jax.experimental.pallas import tpu as pltpu
from jax.sharding import PartitionSpec as P

PATCHES_ON_UNIT = 14
SUBSTEPS = 4
LOG2E = 1.4426950408889634
CONC_FLOOR = 0.1
CHEM_DT = 0.04
ROWS = 64
CHUNK = 128
UNROLL = 4


def ring(axis):
    count = lax.axis_size(axis)
    forward = [(i, (i + 1) % count) for i in range(count)]
    return forward, [(target, source) for source, target in forward]


def chunks(count):
    padded = -(-count // 16) * 16
    return [(start, min(CHUNK, padded - start)) for start in range(0, padded, CHUNK)]


def split(values):
    high = values.astype(jnp.bfloat16)
    low = (values - high.astype(jnp.float32)).astype(jnp.bfloat16)
    return jnp.concatenate([high, low], axis=0)


def pieces(values):
    high = values.astype(jnp.bfloat16).astype(jnp.float32)
    middle = (values - high).astype(jnp.bfloat16).astype(jnp.float32)
    return high, middle, values - high - middle


def strided(ref):
    species, ys, xs, lanes = ref.shape
    flat = ref.reshape(species * ys * xs, lanes)
    return lambda y, x: flat.at[pl.ds(y * xs + x, species, stride=ys * xs), :]


def prepare_kernel(
    u_ref, speed_ref, heat_ref, spread_ref, amplitude_ref, energy_ref, consumed_ref, resulting_ref,
    gather_ref, change_ref, field_ref, slow_ref, lower_ref, upper_ref, wide_ref, index_ref, rate_ref
):
    species, depth, width, lanes = u_ref.shape
    count = consumed_ref.shape[1]
    reach = index_ref.shape[1]
    slab = wide_ref.shape[1]
    stride = depth + 4

    index_ref[...] = jnp.full(index_ref.shape, -1, jnp.int32)
    index_ref[0:2, 0:count] = consumed_ref[...]
    index_ref[2:4, 0:count] = resulting_ref[...]
    rate_ref[...] = jnp.zeros_like(rate_ref)
    rate_ref[0:1, 0:count] = amplitude_ref[...] * LOG2E
    rate_ref[1:2, 0:count] = energy_ref[...] * -LOG2E
    ids = lax.broadcasted_iota(jnp.int32, (ROWS, reach), 0)
    ones = [jnp.where(index_ref[k : k + 1] == ids, 1.0, 0.0) for k in range(4)]
    used = ones[0] + ones[1]
    change = ones[2] + ones[3] - used
    a_high, a_middle, a_low = pieces(rate_ref[0:1])
    e_high, e_middle, e_low = pieces(rate_ref[1:2])
    for k, row in enumerate((a_high, e_high, a_middle, a_low, e_middle, e_low)):
        used = jnp.where(ids == species + k, row, used)
    both = jnp.concatenate([used, used], axis=0)
    rows = gather_ref.shape[0]
    for start in range(0, reach, lanes):
        size = min(lanes, rows - start)
        part = jnp.transpose(both[:, start : start + lanes])
        gather_ref[start : start + size] = part[0:size].astype(jnp.bfloat16)
    lane = lax.broadcasted_iota(jnp.int32, (ROWS, 2 * CHUNK), 1)
    for j, (start, size) in enumerate(chunks(count)):
        part = change[:, start : start + CHUNK]
        pair = jnp.concatenate([part, jnp.zeros_like(part)], axis=1)
        pair = jnp.where(lane < size, pair, 0.0)
        change_ref[j] = (pair + pltpu.roll(pair, size, 1)).astype(jnp.bfloat16)

    half = width // 2 * depth // 2
    for x in range(width):
        for y in range(depth):
            t, k = divmod(x * depth + y, 2)
            part = slice(k * lanes, (k + 1) * lanes)
            for c in range(3):
                field_ref[t, c : c + 1, part] = speed_ref[c, y, x : x + 1, :] * (1.0 / 12.0)
            field_ref[t, 3:4, part] = 1.0 / heat_ref[y, x : x + 1, :]
    spread = jnp.concatenate([spread_ref[...], jnp.zeros((1, lanes - species), jnp.float32)], axis=1)
    spread = jnp.transpose(jnp.broadcast_to(spread * (1.0 / 12.0), (lanes, lanes)))[0:slab]
    slow_ref[...] = spread

    for slot in range(width + 4):
        for y in range(stride):
            if 2 <= slot < width + 2 and 2 <= y < depth + 2:
                wide_ref[slot * stride + y, 0:species, :] = strided(u_ref)(y - 2, slot - 2)[...]
            elif 2 <= slot < width + 2 or 2 <= y < depth + 2:
                wide_ref[slot * stride + y] = jnp.zeros((slab, lanes), jnp.float32)

    def advect(row, field):
        x = row // depth
        y = row - x * depth
        base = (x + 2) * stride + y + 2
        center = wide_ref[base]
        near = jnp.zeros_like(center)
        far = jnp.zeros_like(center)
        moved = jnp.zeros_like(center)
        for axis in range(3):
            if axis == 2:
                low2 = pltpu.roll(center, 2, 1)
                low1 = pltpu.roll(center, 1, 1)
                high1 = pltpu.roll(center, lanes - 1, 1)
                high2 = pltpu.roll(center, lanes - 2, 1)
            else:
                hop = stride if axis == 0 else 1
                low2 = wide_ref[base - 2 * hop]
                low1 = wide_ref[base - hop]
                high1 = wide_ref[base + hop]
                high2 = wide_ref[base + 2 * hop]
            moved = moved + field[axis : axis + 1] * (8.0 * (high1 - low1) - (high2 - low2))
            near = near + (high1 + low1)
            far = far + (high2 + low2)
        return center - moved + spread * (16.0 * near - far - 90.0 * center)

    for target, shift in ((lower_ref, 0), (upper_ref, half)):
        def tile(t, carry, target=target, shift=shift):
            for k in range(2):
                part = slice(k * lanes, (k + 1) * lanes)
                target[t, 0:slab, part] = advect(2 * (t + shift) + k, field_ref[t + shift, :, part])
            target[t, slab:ROWS] = jnp.zeros((ROWS - slab, 2 * lanes), jnp.float32)
            return carry

        lax.fori_loop(0, half, tile, 0)


def prepare(cells, speed, heat, spread, amplitude, energy, consumed, resulting):
    species, depth, width, lanes = cells.shape
    count = consumed.shape[1]
    parts = chunks(count)
    reach = len(parts) * CHUNK
    slab = -(-species // 8) * 8
    tiles = width * depth // 2
    shapes = [
        ((parts[-1][0] + parts[-1][1], 2 * ROWS), jnp.bfloat16),
        ((len(parts), ROWS, 2 * CHUNK), jnp.bfloat16),
        ((tiles, 8, 2 * lanes), jnp.float32),
        ((slab, lanes), jnp.float32),
        ((tiles // 2, ROWS, 2 * lanes), jnp.float32),
        ((tiles // 2, ROWS, 2 * lanes), jnp.float32),
    ]
    return pl.pallas_call(
        prepare_kernel,
        out_shape=[jax.ShapeDtypeStruct(*shape) for shape in shapes],
        scratch_shapes=[
            pltpu.VMEM(((width + 4) * (depth + 4), slab, lanes), jnp.float32),
            pltpu.VMEM((8, reach), jnp.int32),
            pltpu.VMEM((8, reach), jnp.float32),
        ],
        name="prepare",
    )(cells, speed, heat, spread, amplitude, energy, consumed, resulting)


def half_kernel(first_x, workers, *refs):
    place_ref, owner_ref, base_ref, side_ref, ylo_ref, yhi_ref, field_ref, spread_ref = refs[:8]
    gather_ref, change_ref = refs[8:10]
    out_ref, advected_ref, current_ref = refs[-3:]
    species, depth, _, lanes = side_ref.shape
    tiles = base_ref.shape[0]
    first_tile = first_x * depth // 2
    side, ylo, yhi = strided(side_ref), strided(ylo_ref), strided(yhi_ref)
    spread = spread_ref[0:species]

    for t in range(tiles):
        for k in range(2):
            x, y = divmod(2 * t + k, depth)
            part = slice(k * lanes, (k + 1) * lanes)
            field = field_ref[first_tile + t, :, part]
            values = base_ref[t, 0:species, part]

            def add(values, axis, far, value):
                speed = field[axis : axis + 1]
                if far > 0:
                    speed = -speed
                return values + (speed * 8.0 + spread * 16.0 if abs(far) == 1 else -speed - spread) * value

            if first_x == 0:
                taps = ((-2, 0), (-1, 1)) if x == 0 else ((-2, 1),)
            else:
                taps = ((2, 0),) if x == 0 else ((1, 0), (2, 1))
            for far, plane in taps:
                values = add(values, 0, far, side(y, plane)[...])
            column = first_x + x
            if y == 0:
                values = add(values, 1, -2, ylo(0, column)[...])
            if y <= 1:
                values = add(values, 1, -1 - y, ylo(1, column)[...])
            if y >= depth - 2:
                values = add(values, 1, depth - y, yhi(0, column)[...])
            if y == depth - 1:
                values = add(values, 1, 2, yhi(1, column)[...])
            advected_ref[t, 0:species, part] = values
            current_ref[t, 0:species, part] = values
        current_ref[t, species:ROWS] = jnp.ones((ROWS - species, 2 * lanes), jnp.float32)

    row_ids = lax.broadcasted_iota(jnp.int32, (16, 2 * lanes), 0) + (ROWS - 16)
    is_species = row_ids < species
    is_one = (row_ids == species) | (row_ids == species + 2) | (row_ids == species + 3)
    is_heat = (row_ids == species + 1) | (row_ids == species + 4) | (row_ids == species + 5)

    def exponent(t):
        logged = jnp.log(jnp.maximum(current_ref[t], CONC_FLOOR)) * LOG2E
        spare = jnp.where(is_one, 1.0, jnp.where(is_heat, field_ref[first_tile + t, 3:4], 0.0))
        stacked = jnp.concatenate(
            [logged[: ROWS - 16], jnp.where(is_species, logged[ROWS - 16 :], spare)], axis=0
        )
        return jnp.dot(gather_ref[...], split(stacked), preferred_element_type=jnp.float32)

    def gained(powers):
        total = None
        for j, (start, size) in enumerate(chunks(powers.shape[0])):
            progress = jnp.exp2(jnp.minimum(powers[start : start + size], LOG2E))
            part = jnp.dot(
                change_ref[j, :, 0 : 2 * size], split(progress), preferred_element_type=jnp.float32
            )
            total = part if total is None else total + part
        return CHEM_DT * total

    def substeps(turns):
        order = [(i, t) for i in range(turns) for t in range(tiles)]
        ready = exponent(0)
        for n, (_, t) in enumerate(order):
            powers = ready
            if n + 1 < len(order):
                ready = exponent(order[n + 1][1])
            current_ref[t] = current_ref[t] + gained(powers)

    if UNROLL == SUBSTEPS:
        substeps(SUBSTEPS)
    else:
        def turn(i, carry):
            substeps(UNROLL)
            return carry

        lax.fori_loop(0, SUBSTEPS // UNROLL, turn, 0)

    for t in range(tiles):
        reacts = owner_ref[0, place_ref[0] * PATCHES_ON_UNIT + first_tile + t] < workers
        result = jnp.where(reacts, current_ref[t, 0:species], advected_ref[t])
        if first_x != 0:
            out_ref[t, 0:species] = result
            continue
        write = strided(out_ref)
        for values, shift in ((result, 0), (refs[10][t, 0:species], 2)):
            for k in range(2):
                x, y = divmod(2 * t + k, depth)
                write(y, x + shift)[...] = values[:, k * lanes : (k + 1) * lanes]


def half(first_x, shape, workers, *args):
    species, _, _, lanes = shape
    tiles = args[2].shape[0]
    block = (tiles, ROWS, 2 * lanes)
    smem = pl.BlockSpec(memory_space=pltpu.SMEM)
    return pl.pallas_call(
        functools.partial(half_kernel, first_x, workers),
        out_shape=jax.ShapeDtypeStruct(block if first_x else shape, jnp.float32),
        in_specs=[smem, smem] + [pl.BlockSpec() for _ in args[2:]],
        scratch_shapes=[
            pltpu.VMEM((tiles, species, 2 * lanes), jnp.float32),
            pltpu.VMEM(block, jnp.float32),
        ],
    )(*args)


def per_device(
    molar_fractions,
    fluid_speed_vector,
    thermal_state,
    molecular_spreading,
    arrhenius_ln_amplitude,
    arrhenius_energy,
    consumed_molecules,
    resulting_molecules,
    patch_assignee,
):
    species, width, depth, _ = molar_fractions.shape
    cells = molar_fractions.transpose(0, 2, 1, 3)
    flow_next, flow_back = ring("flow")
    chem_next, chem_back = ring("chem")
    xlo = lax.ppermute(cells[:, :, width - 2 :], "flow", flow_next)
    xhi = lax.ppermute(cells[:, :, :2], "flow", flow_back)
    ylo = lax.ppermute(cells[:, depth - 2 :], "chem", chem_next)
    yhi = lax.ppermute(cells[:, :2], "chem", chem_back)

    workers = lax.axis_size("chem")
    place = lax.axis_index("chem").astype(jnp.int32).reshape(1)
    gather, change, field, spread, lower, upper = prepare(
        cells,
        fluid_speed_vector.transpose(0, 2, 1, 3),
        thermal_state.transpose(1, 0, 2),
        molecular_spreading.reshape(1, species),
        arrhenius_ln_amplitude.reshape(1, -1),
        arrhenius_energy.reshape(1, -1),
        consumed_molecules.T,
        resulting_molecules.T,
    )
    shared = (field, spread, gather, change)
    owners = (place, patch_assignee)
    upper = half(2, cells.shape, workers, *owners, upper, xhi, ylo, yhi, *shared)
    out = half(0, cells.shape, workers, *owners, lower, xlo, ylo, yhi, *shared, upper)
    return out.transpose(0, 2, 1, 3)


def solution(mesh):
    in_specs = (
        P(None, "flow", "chem", None),
        P(None, "flow", "chem", None),
        P("flow", "chem", None),
        P(),
        P(),
        P(),
        P(),
        P(),
        P("flow", None),
    )
    out_specs = P(None, "flow", "chem", None)
    return jax.shard_map(
        per_device, mesh=mesh, in_specs=in_specs, out_specs=out_specs, check_vma=False
    )
```

time: 58.6 us -> 58 us (0.990)
  the two profiles are of different devices: /device:TPU:2 before, /device:TPU:11 now
where the time goes in v3:
time: 58 us; the launch traced here: 57.7 us
  starting transfers between devices  25.7 us (44%)
  Pallas kernels  15.8 us (27%)
  waiting for transfers between devices  10.6 us (18%)
  local copies, waits for them, and re-layouts  5.4 us (9%)
    ppermute x1, starting transfers between devices, per_device(): xhi = lax.ppermute(cells[:, :, :2], 'flow', flow_back)  17.1 us
    pallas_call x2, Pallas kernels, half(): pl.pallas_call(functools.partial(half_kernel, first_x, workers), out_shap...  11.3 us
    ppermute x1, waiting for transfers between devices, per_device(): yhi = lax.ppermute(cells[:, :2], 'chem', chem_back)  10.6 us
    pallas_call x1, Pallas kernels, prepare(): pl.pallas_call(prepare_kernel, out_shape=[jax.ShapeDtypeStruct(*shape) fo...  4.59 us
    ppermute x1, starting transfers between devices, per_device(): ylo = lax.ppermute(cells[:, depth - 2:], 'chem', chem_next)  3.8 us
    ppermute x1, starting transfers between devices, per_device(): yhi = lax.ppermute(cells[:, :2], 'chem', chem_back)  2.86 us
    unnamed x14, local copies, waits for them, and re-layouts  2.51 us
    ppermute x1, starting transfers between devices, per_device(): xlo = lax.ppermute(cells[:, :, width - 2:], 'flow', flow_next)  1.92 us
  transfers between devices with their start and end apart: 4, of which 1 were waited for; matrix products, arithmetic and copies ran while one was open for 2% of the time, Pallas kernels for 17%

profile of v3, /device:TPU:11, one launch (start us, length us, event | category | flops | bytes accessed | tf_op | source)
XLA Modules:
  0.0 57.7 jit_solution(6792537456323502116)
XLA Ops:
  0.0 0.0 copy-start
  0.0 1.8 %fusion = (f32[53,7,2,128]{3,2,1,0:T(2,128)S(1)}, f32[53,7,2,128]{3,2,1,0:T(2,128)S(1)}) fusion(f32[53,7,4,128]{3,2,1,0:T(4,128)} %bitcast.8), kind=kLoop, calls=%fused_computation | loop fusion | bytes 1519616 | tf_op jit(solution)/shard_map/slice | solution.py:296
  1.8 17.1 %collective-permute-start.3 = (f32[53,7,2,128]{3,2,1,0:T(2,128)S(1)}, f32[53,7,2,128]{3,2,1,0:T(2,128)S(1)}, u32[]{:S(2)}, u32[]{:S(2)}) collective-permute-start(f32[53,7,2,128]{3,2,1,0:T(2,128)S(1)} %get-tuple-element.17), channel_id=1, source_target_pairs={{16,0},{32,16},{48,32},{64,48},{80,64},{96,80},{112,96},{128,112},... | collective-permute-start | bytes 1139720 | tf_op jit(solution)/shard_map/ppermute | solution.py:296
  18.9 1.9 %collective-permute-start = (f32[53,7,2,128]{3,2,1,0:T(2,128)S(1)}, f32[53,7,2,128]{3,2,1,0:T(2,128)S(1)}, u32[]{:S(2)}, u32[]{:S(2)}) collective-permute-start(f32[53,7,2,128]{3,2,1,0:T(2,128)S(1)} %get-tuple-element.18), channel_id=1, source_target_pairs={{0,16},{16,32},{32,48},{48,64},{64,80},{80,96},{96,112},{112,128},... | collective-permute-start | bytes 1139720 | tf_op jit(solution)/shard_map/ppermute | solution.py:295
  20.8 0.0 copy-done
  20.8 2.9 %collective-permute-start.2 = (f32[53,2,4,128]{3,2,1,0:T(4,128)S(1)}, f32[53,2,4,128]{3,2,1,0:T(4,128)S(1)}, u32[]{:S(2)}, u32[]{:S(2)}) collective-permute-start(f32[53,2,4,128]{3,2,1,0:T(4,128)S(1)} %get-tuple-element.19), channel_id=1, source_target_pairs={{1,0},{2,1},{3,2},{4,3},{5,4},{6,5},{7,6},{8,7},{9,8},{10,9},{11,1... | collective-permute-start | bytes 651272 | tf_op jit(solution)/shard_map/ppermute | solution.py:298
  23.7 3.8 %collective-permute-start.1 = (f32[53,2,4,128]{3,2,1,0:T(4,128)S(1)}, f32[53,2,4,128]{3,2,1,0:T(4,128)S(1)}, u32[]{:S(2)}, u32[]{:S(2)}) collective-permute-start(f32[53,2,4,128]{3,2,1,0:T(4,128)S(1)} %get-tuple-element.20), channel_id=1, source_target_pairs={{0,1},{1,2},{2,3},{3,4},{4,5},{5,6},{6,7},{7,8},{8,9},{9,10},{10,1... | collective-permute-start | bytes 651272 | tf_op jit(solution)/shard_map/ppermute | solution.py:297
  27.5 0.0 copy-start.5
  27.5 0.7 %copy-done.5 = f32[325]{0:T(512)S(1)} copy-done((f32[325]{0:T(512)S(1)}, f32[325]{0:T(512)}, u32[]{:S(2)}) %copy-start.5) | copy-done | bytes 1324
  28.2 0.0 copy-start.6
  28.2 0.5 reshape.14.amplitude_ref
  28.8 0.1 copy-done.6
  28.9 0.6 reshape.15.energy_ref
  29.5 4.6 %prepare.1 = (bf16[336,128]{1,0:T(8,128)(2,1)}, bf16[3,64,256]{2,1,0:T(8,128)(2,1)}, f32[14,8,256]{2,1,0:T(8,128)}, f32[56,128]{1,0:T(8,128)}, f32[7,64,256]{2,1,0:T(8,128)}, /*index=5*/f32[7,64,256]{2,1,0:T(8,128)}) custom-call(f32[53,7,4,128]{3,2,1,0:T(4,128)} %bitcast.9, f32[3,7,4,128]{3,2,1,0:T(4,128)} %bitcast.11, f32[7,4,128]{2,1,0:T(4,128)} %bitcast.12, ...), custom_call_target="tpu_custom_call" | custom-call | tf_op jit(solution)/shard_map/prepare/pallas_call | solution.py:156
  34.1 10.6 %collective-permute-done.2.refs_5_ = f32[53,2,4,128]{3,2,1,0:T(4,128)S(1)} collective-permute-done((f32[53,2,4,128]{3,2,1,0:T(4,128)S(1)}, f32[53,2,4,128]{3,2,1,0:T(4,128)S(1)}, u32[]{:S(2)}, u32[]{:S(2)}) %collective-permute-start.2) | collective-permute-done | bytes 217120 | tf_op jit(solution)/shard_map/ppermute | solution.py:298
  44.7 0.0 copy-start.1
  44.7 0.0 collective-permute-done.1.refs_4_
  44.7 0.0 copy-start.2
  44.7 0.0 collective-permute-done.3.refs_3_
  44.7 0.0 copy-start.4
  44.7 0.7 %copy-done.1 = f32[53,2,4,128]{3,2,1,0:T(4,128)} copy-done((f32[53,2,4,128]{3,2,1,0:T(4,128)}, f32[53,2,4,128]{3,2,1,0:T(4,128)S(1)}, u32[]{:S(2)}) %copy-start.1) | copy-done | bytes 217112
  45.4 0.1 copy-done.2
  45.5 0.2 copy-done.4
  45.6 5.5 %shard_map.91.refs_10_ = f32[7,64,256]{2,1,0:T(8,128)} custom-call(s32[1]{0:T(128)} %bitcast.refs_0_, s32[1,224]{1,0:T(1,128)} %refs_1_.3, f32[7,64,256]{2,1,0:T(8,128)} %get-tuple-element.16.refs_2_, f32[53,7,2,128]{3,2,1,0:T(2,128)} %copy-done.4, f32[53,2,4,128]{3,2,1,0:T(4,128)} %copy-done.2, f32[53,2,4,128]{3,2,1,0:T(4,128)} %copy-done.1, ...), custom_call_target="tpu_custom_call" | custom-call | tf_op jit(solution)/shard_map/pallas_call | solution.py:269
  51.1 0.0 collective-permute-done.refs_3_
  51.1 0.0 copy-start.3
  51.1 0.8 %copy-done.3 = f32[53,7,2,128]{3,2,1,0:T(2,128)} copy-done((f32[53,7,2,128]{3,2,1,0:T(2,128)}, f32[53,7,2,128]{3,2,1,0:T(2,128)S(1)}, u32[]{:S(2)}) %copy-start.3) | copy-done | bytes 379928
  51.9 5.8 %shard_map.92 = f32[53,7,4,128]{3,2,1,0:T(4,128)} custom-call(s32[1]{0:T(128)} %bitcast.refs_0_, s32[1,224]{1,0:T(1,128)} %refs_1_.3, f32[7,64,256]{2,1,0:T(8,128)} %get-tuple-element.11.refs_2_, f32[53,7,2,128]{3,2,1,0:T(2,128)} %copy-done.3, f32[53,2,4,128]{3,2,1,0:T(4,128)} %copy-done.2, f32[53,2,4,128]{3,2,1,0:T(4,128)} %copy-done.1, ...), custom_call_target="tpu_custom_call" | custom-call | tf_op jit(solution)/shard_map/pallas_call | solution.py:269
  (1 shorter events, 0.0 us)
Async XLA Ops:
  0.0 20.8 %copy-start = (f32[53,4,7,128]{3,1,2,0:T(4,128)S(1)}, f32[53,4,7,128]{3,1,2,0:T(4,128)}, u32[]{:S(2)}) copy-start(f32[53,4,7,128]{3,1,2,0:T(4,128)} %param.9) | copy-start | bytes 2279428
  1.8 42.9 %collective-permute-start.3 = (f32[53,7,2,128]{3,2,1,0:T(2,128)S(1)}, f32[53,7,2,128]{3,2,1,0:T(2,128)S(1)}, u32[]{:S(2)}, u32[]{:S(2)}) collective-permute-start(f32[53,7,2,128]{3,2,1,0:T(2,128)S(1)} %get-tuple-element.17), channel_id=1, source_target_pairs={{16,0},{32,16},{48,32},{64,48},{80,64},{96,80},{112,96},{128,112},... | collective-permute-start | bytes 1139720 | tf_op jit(solution)/shard_map/ppermute | solution.py:296
  18.9 32.2 %collective-permute-start = (f32[53,7,2,128]{3,2,1,0:T(2,128)S(1)}, f32[53,7,2,128]{3,2,1,0:T(2,128)S(1)}, u32[]{:S(2)}, u32[]{:S(2)}) collective-permute-start(f32[53,7,2,128]{3,2,1,0:T(2,128)S(1)} %get-tuple-element.18), channel_id=1, source_target_pairs={{0,16},{16,32},{32,48},{48,64},{64,80},{80,96},{96,112},{112,128},... | collective-permute-start | bytes 1139720 | tf_op jit(solution)/shard_map/ppermute | solution.py:295
  20.8 23.9 %collective-permute-start.2 = (f32[53,2,4,128]{3,2,1,0:T(4,128)S(1)}, f32[53,2,4,128]{3,2,1,0:T(4,128)S(1)}, u32[]{:S(2)}, u32[]{:S(2)}) collective-permute-start(f32[53,2,4,128]{3,2,1,0:T(4,128)S(1)} %get-tuple-element.19), channel_id=1, source_target_pairs={{1,0},{2,1},{3,2},{4,3},{5,4},{6,5},{7,6},{8,7},{9,8},{10,9},{11,1... | collective-permute-start | bytes 651272 | tf_op jit(solution)/shard_map/ppermute | solution.py:298
  23.7 21.0 %collective-permute-start.1 = (f32[53,2,4,128]{3,2,1,0:T(4,128)S(1)}, f32[53,2,4,128]{3,2,1,0:T(4,128)S(1)}, u32[]{:S(2)}, u32[]{:S(2)}) collective-permute-start(f32[53,2,4,128]{3,2,1,0:T(4,128)S(1)} %get-tuple-element.20), channel_id=1, source_target_pairs={{0,1},{1,2},{2,3},{3,4},{4,5},{5,6},{6,7},{7,8},{8,9},{9,10},{10,1... | collective-permute-start | bytes 651272 | tf_op jit(solution)/shard_map/ppermute | solution.py:297
  27.5 0.7 %copy-start.5 = (f32[325]{0:T(512)S(1)}, f32[325]{0:T(512)}, u32[]{:S(2)}) copy-start(f32[325]{0:T(512)} %param.13) | copy-start | bytes 3904
  28.2 0.7 %copy-start.6 = (f32[325]{0:T(512)S(1)}, f32[325]{0:T(512)}, u32[]{:S(2)}) copy-start(f32[325]{0:T(512)} %param.14) | copy-start | bytes 3904
  44.7 0.7 %copy-start.1 = (f32[53,2,4,128]{3,2,1,0:T(4,128)}, f32[53,2,4,128]{3,2,1,0:T(4,128)S(1)}, u32[]{:S(2)}) copy-start(f32[53,2,4,128]{3,2,1,0:T(4,128)S(1)} %collective-permute-done.2.refs_5_) | copy-start | bytes 651268
  44.7 0.8 %copy-start.2 = (f32[53,2,4,128]{3,2,1,0:T(4,128)}, f32[53,2,4,128]{3,2,1,0:T(4,128)S(1)}, u32[]{:S(2)}) copy-start(f32[53,2,4,128]{3,2,1,0:T(4,128)S(1)} %collective-permute-done.1.refs_4_) | copy-start | bytes 651268
  44.7 0.9 %copy-start.4 = (f32[53,7,2,128]{3,2,1,0:T(2,128)}, f32[53,7,2,128]{3,2,1,0:T(2,128)S(1)}, u32[]{:S(2)}) copy-start(f32[53,7,2,128]{3,2,1,0:T(2,128)S(1)} %collective-permute-done.3.refs_3_) | copy-start | bytes 1139716
  51.1 0.8 %copy-start.3 = (f32[53,7,2,128]{3,2,1,0:T(2,128)}, f32[53,7,2,128]{3,2,1,0:T(2,128)S(1)}, u32[]{:S(2)}) copy-start(f32[53,7,2,128]{3,2,1,0:T(2,128)S(1)} %collective-permute-done.refs_3_) | copy-start | bytes 1139716

commit v4 on v3

--- a/solution.py
+++ b/solution.py
@@ -21,6 +21,10 @@
     count = lax.axis_size(axis)
     forward = [(i, (i + 1) % count) for i in range(count)]
     return forward, [(target, source) for source, target in forward]
+
+
+def on_chip(values):
+    return pltpu.with_memory_space_constraint(values, pltpu.VMEM)
 
 
 def chunks(count):
@@ -155,7 +159,7 @@
     ]
     return pl.pallas_call(
         prepare_kernel,
-        out_shape=[jax.ShapeDtypeStruct(*shape) for shape in shapes],
+        out_shape=[pltpu.VMEM(*shape) for shape in shapes],
         scratch_shapes=[
             pltpu.VMEM(((width + 4) * (depth + 4), slab, lanes), jnp.float32),
             pltpu.VMEM((8, reach), jnp.int32),
@@ -268,7 +272,7 @@
     smem = pl.BlockSpec(memory_space=pltpu.SMEM)
     return pl.pallas_call(
         functools.partial(half_kernel, first_x, workers),
-        out_shape=jax.ShapeDtypeStruct(block if first_x else shape, jnp.float32),
+        out_shape=pltpu.VMEM(block, jnp.float32) if first_x else jax.ShapeDtypeStruct(shape, jnp.float32),
         in_specs=[smem, smem] + [pl.BlockSpec() for _ in args[2:]],
         scratch_shapes=[
             pltpu.VMEM((tiles, species, 2 * lanes), jnp.float32),
@@ -293,7 +297,8 @@
     flow_next, flow_back = ring("flow")
     chem_next, chem_back = ring("chem")
     xlo = lax.ppermute(cells[:, :, width - 2 :], "flow", flow_next)
-    xhi = lax.ppermute(cells[:, :, :2], "flow", flow_back)
+    again = lax.optimization_barrier(cells)
+    xhi = lax.ppermute(again[:, :, :2], "flow", flow_back)
     ylo = lax.ppermute(cells[:, depth - 2 :], "chem", chem_next)
     yhi = lax.ppermute(cells[:, :2], "chem", chem_back)
 
@@ -309,10 +314,11 @@
         consumed_molecules.T,
         resulting_molecules.T,
     )
-    shared = (field, spread, gather, change)
+    shared = tuple(map(on_chip, (field, spread, gather, change)))
     owners = (place, patch_assignee)
+    xlo, xhi, ylo, yhi, lower, upper = map(on_chip, (xlo, xhi, ylo, yhi, lower, upper))
     upper = half(2, cells.shape, workers, *owners, upper, xhi, ylo, yhi, *shared)
-    out = half(0, cells.shape, workers, *owners, lower, xlo, ylo, yhi, *shared, upper)
+    out = half(0, cells.shape, workers, *owners, lower, xlo, ylo, yhi, *shared, on_chip(upper))
     return out.transpose(0, 2, 1, 3)
 
 

time: 58 us -> 54.7 us (0.943)
  the two profiles are of different devices: /device:TPU:11 before, /device:TPU:9 now
where the time goes in v4:
time: 54.7 us; the launch traced here: 54.4 us
  starting transfers between devices  25.8 us (47%)
  Pallas kernels  12.8 us (23%)
  waiting for transfers between devices  11.4 us (21%)
  local copies, waits for them, and re-layouts  4.32 us (8%)
    ppermute x1, starting transfers between devices, per_device(): xhi = lax.ppermute(again[:, :, :2], 'flow', flow_back)  17.1 us
    ppermute x1, waiting for transfers between devices, per_device(): yhi = lax.ppermute(cells[:, :2], 'chem', chem_back)  11.4 us
    pallas_call x2, Pallas kernels, half(): pl.pallas_call(functools.partial(half_kernel, first_x, workers), out_shap...  9.19 us
    ppermute x1, starting transfers between devices, per_device(): ylo = lax.ppermute(cells[:, depth - 2:], 'chem', chem_next)  4.86 us
    pallas_call x1, Pallas kernels, prepare(): pl.pallas_call(prepare_kernel, out_shape=[pltpu.VMEM(*shape) for shape in...  3.61 us
    slice x1, local copies, waits for them, and re-layouts, per_device(): xhi = lax.ppermute(again[:, :, :2], 'flow', flow_back)  2.07 us
    ppermute x1, starting transfers between devices, per_device(): xlo = lax.ppermute(cells[:, :, width - 2:], 'flow', flow_next)  1.92 us
    ppermute x1, starting transfers between devices, per_device(): yhi = lax.ppermute(cells[:, :2], 'chem', chem_back)  1.92 us
  transfers between devices with their start and end apart: 4, of which 1 were waited for; matrix products, arithmetic and copies ran while one was open for 4% of the time, Pallas kernels for 14%

profile of v4, /device:TPU:9, one launch (start us, length us, event | category | flops | bytes accessed | tf_op | source)
XLA Modules:
  0.0 54.4 jit_solution(4515661042080249821)
XLA Ops:
  0.0 0.0 copy-start
  0.0 2.1 %slice.19 = f32[53,7,2,128]{3,2,1,0:T(2,128)} slice(f32[53,7,4,128]{3,2,1,0:T(4,128)} %bitcast.8), slice={[0:53], [0:7], [0:2], [0:128]} | slice | bytes 759808 | tf_op jit(solution)/shard_map/slice | solution.py:301
  2.1 17.1 %collective-permute-start.3 = (f32[53,7,2,128]{3,2,1,0:T(2,128)}, f32[53,7,2,128]{3,2,1,0:T(2,128)S(1)}, u32[]{:S(2)}, u32[]{:S(2)}) collective-permute-start(f32[53,7,2,128]{3,2,1,0:T(2,128)} %slice.19), channel_id=1, source_target_pairs={{16,0},{32,16},{48,32},{64,48},{80,64},{96,80},{112,96},{128,112},... | collective-permute-start | bytes 1139720 | tf_op jit(solution)/shard_map/ppermute | solution.py:301
  19.2 0.0 copy-done
  19.2 0.2 slice.16
  19.4 1.9 %collective-permute-start = (f32[53,7,2,128]{3,2,1,0:T(2,128)S(1)}, f32[53,7,2,128]{3,2,1,0:T(2,128)S(1)}, u32[]{:S(2)}, u32[]{:S(2)}) collective-permute-start(f32[53,7,2,128]{3,2,1,0:T(2,128)S(1)} %slice.16), channel_id=1, source_target_pairs={{0,16},{16,32},{32,48},{48,64},{64,80},{80,96},{96,112},{112,128},... | collective-permute-start | bytes 1139720 | tf_op jit(solution)/shard_map/ppermute | solution.py:299
  21.3 0.8 %fusion = (f32[53,2,4,128]{3,2,1,0:T(4,128)}, f32[53,2,4,128]{3,2,1,0:T(4,128)}) fusion(f32[53,7,4,128]{3,2,1,0:T(4,128)S(1)} %bitcast.11), kind=kLoop, calls=%fused_computation | loop fusion | bytes 868352 | tf_op jit(solution)/shard_map/slice | solution.py:303
  22.1 0.0 copy-start.1
  22.1 4.9 %collective-permute-start.1 = (f32[53,2,4,128]{3,2,1,0:T(4,128)}, f32[53,2,4,128]{3,2,1,0:T(4,128)S(1)}, u32[]{:S(2)}, u32[]{:S(2)}) collective-permute-start(f32[53,2,4,128]{3,2,1,0:T(4,128)} %get-tuple-element.18), channel_id=1, source_target_pairs={{0,1},{1,2},{2,3},{3,4},{4,5},{5,6},{6,7},{7,8},{8,9},{9,10},{10,1... | collective-permute-start | bytes 651272 | tf_op jit(solution)/shard_map/ppermute | solution.py:302
  27.0 1.9 %collective-permute-start.2 = (f32[53,2,4,128]{3,2,1,0:T(4,128)}, f32[53,2,4,128]{3,2,1,0:T(4,128)S(1)}, u32[]{:S(2)}, u32[]{:S(2)}) collective-permute-start(f32[53,2,4,128]{3,2,1,0:T(4,128)} %get-tuple-element.17), channel_id=1, source_target_pairs={{1,0},{2,1},{3,2},{4,3},{5,4},{6,5},{7,6},{8,7},{9,8},{10,9},{11,1... | collective-permute-start | bytes 651272 | tf_op jit(solution)/shard_map/ppermute | solution.py:303
  28.9 0.0 copy-done.1
  28.9 0.0 copy-start.2
  28.9 0.6 %reshape.14.amplitude_ref = f32[1,325]{1,0:T(1,128)} reshape(f32[325]{0:T(512)S(1)} %copy-done.1) | data formatting | bytes 2600 | tf_op jit(solution)/shard_map/reshape | solution.py:312
  29.5 0.1 copy-done.2
  29.6 0.6 %reshape.15.energy_ref = f32[1,325]{1,0:T(1,128)} reshape(f32[325]{0:T(512)S(1)} %copy-done.2) | data formatting | bytes 2600 | tf_op jit(solution)/shard_map/reshape | solution.py:313
  30.2 3.6 %prepare.1 = (bf16[336,128]{1,0:T(8,128)(2,1)S(1)}, bf16[3,64,256]{2,1,0:T(8,128)(2,1)S(1)}, f32[14,8,256]{2,1,0:T(8,128)S(1)}, f32[56,128]{1,0:T(8,128)S(1)}, f...) custom-call(f32[53,7,4,128]{3,2,1,0:T(4,128)} %bitcast.9, f32[3,7,4,128]{3,2,1,0:T(4,128)} %bitcast.12, ...), custom_call_target="tpu_custom_call" | custom-call | tf_op jit(solution)/shard_map/prepare/pallas_call | solution.py:160
  33.8 0.0 collective-permute-done.1.refs_4_
  33.8 11.4 %collective-permute-done.2.refs_5_ = f32[53,2,4,128]{3,2,1,0:T(4,128)S(1)} collective-permute-done((f32[53,2,4,128]{3,2,1,0:T(4,128)}, f32[53,2,4,128]{3,2,1,0:T(4,128)S(1)}, u32[]{:S(2)}, u32[]{:S(2)}) %collective-permute-start.2) | collective-permute-done | bytes 217120 | tf_op jit(solution)/shard_map/ppermute | solution.py:303
  45.2 0.0 collective-permute-done.3.refs_3_
  45.2 4.1 %shard_map.91.refs_10_ = f32[7,64,256]{2,1,0:T(8,128)S(1)} custom-call(s32[1]{0:T(128)} %bitcast.refs_0_, s32[1,224]{1,0:T(1,128)} %refs_1_.3, f32[7,64,256]{2,1,0:T(8,128)S(1)} %get-tuple-element.16.refs_2_, f32[53,7,2,128]{3,2,1,0:T(2,128)S(1)} %collective-permute-done.3.refs_3_, f32[53,2,4,128]{3,2,1,0:T(4,128)S(1)} %collective-permute-done.1.refs_4_, ...), custom_call_target="tpu_custom_call" | custom-call | tf_op jit(solution)/shard_map/pallas_call | solution.py:273
  49.3 0.0 collective-permute-done.refs_3_
  49.3 5.1 %shard_map.92 = f32[53,7,4,128]{3,2,1,0:T(4,128)} custom-call(s32[1]{0:T(128)} %bitcast.refs_0_, s32[1,224]{1,0:T(1,128)} %refs_1_.3, f32[7,64,256]{2,1,0:T(8,128)S(1)} %get-tuple-element.11.refs_2_, f32[53,7,2,128]{3,2,1,0:T(2,128)S(1)} %collective-permute-done.refs_3_, f32[53,2,4,128]{3,2,1,0:T(4,128)S(1)} %collective-permute-done.1.refs_4_, ...), custom_call_target="tpu_custom_call" | custom-call | tf_op jit(solution)/shard_map/pallas_call | solution.py:273
Async XLA Ops:
  0.0 19.2 %copy-start = (f32[53,4,7,128]{3,1,2,0:T(4,128)S(1)}, f32[53,4,7,128]{3,1,2,0:T(4,128)}, u32[]{:S(2)}) copy-start(f32[53,4,7,128]{3,1,2,0:T(4,128)} %param.9) | copy-start | bytes 2279428
  2.1 43.1 %collective-permute-start.3 = (f32[53,7,2,128]{3,2,1,0:T(2,128)}, f32[53,7,2,128]{3,2,1,0:T(2,128)S(1)}, u32[]{:S(2)}, u32[]{:S(2)}) collective-permute-start(f32[53,7,2,128]{3,2,1,0:T(2,128)} %slice.19), channel_id=1, source_target_pairs={{16,0},{32,16},{48,32},{64,48},{80,64},{96,80},{112,96},{128,112},... | collective-permute-start | bytes 1139720 | tf_op jit(solution)/shard_map/ppermute | solution.py:301
  19.4 30.0 %collective-permute-start = (f32[53,7,2,128]{3,2,1,0:T(2,128)S(1)}, f32[53,7,2,128]{3,2,1,0:T(2,128)S(1)}, u32[]{:S(2)}, u32[]{:S(2)}) collective-permute-start(f32[53,7,2,128]{3,2,1,0:T(2,128)S(1)} %slice.16), channel_id=1, source_target_pairs={{0,16},{16,32},{32,48},{48,64},{64,80},{80,96},{96,112},{112,128},... | collective-permute-start | bytes 1139720 | tf_op jit(solution)/shard_map/ppermute | solution.py:299
  22.1 6.8 %copy-start.1 = (f32[325]{0:T(512)S(1)}, f32[325]{0:T(512)}, u32[]{:S(2)}) copy-start(f32[325]{0:T(512)} %param.13) | copy-start | bytes 3904
  22.1 11.7 %collective-permute-start.1 = (f32[53,2,4,128]{3,2,1,0:T(4,128)}, f32[53,2,4,128]{3,2,1,0:T(4,128)S(1)}, u32[]{:S(2)}, u32[]{:S(2)}) collective-permute-start(f32[53,2,4,128]{3,2,1,0:T(4,128)} %get-tuple-element.18), channel_id=1, source_target_pairs={{0,1},{1,2},{2,3},{3,4},{4,5},{5,6},{6,7},{7,8},{8,9},{9,10},{10,1... | collective-permute-start | bytes 651272 | tf_op jit(solution)/shard_map/ppermute | solution.py:302
  27.0 18.2 %collective-permute-start.2 = (f32[53,2,4,128]{3,2,1,0:T(4,128)}, f32[53,2,4,128]{3,2,1,0:T(4,128)S(1)}, u32[]{:S(2)}, u32[]{:S(2)}) collective-permute-start(f32[53,2,4,128]{3,2,1,0:T(4,128)} %get-tuple-element.17), channel_id=1, source_target_pairs={{1,0},{2,1},{3,2},{4,3},{5,4},{6,5},{7,6},{8,7},{9,8},{10,9},{11,1... | collective-permute-start | bytes 651272 | tf_op jit(solution)/shard_map/ppermute | solution.py:303
  28.9 0.7 %copy-start.2 = (f32[325]{0:T(512)S(1)}, f32[325]{0:T(512)}, u32[]{:S(2)}) copy-start(f32[325]{0:T(512)} %param.14) | copy-start | bytes 3904

commit v5 on v4

--- a/solution.py
+++ b/solution.py
@@ -14,7 +14,7 @@
 CHEM_DT = 0.04
 ROWS = 64
 CHUNK = 128
-UNROLL = 4
+VMEM_LIMIT = 12 << 20
 
 
 def ring(axis):
@@ -52,7 +52,7 @@
 
 def prepare_kernel(
     u_ref, speed_ref, heat_ref, spread_ref, amplitude_ref, energy_ref, consumed_ref, resulting_ref,
-    gather_ref, change_ref, field_ref, slow_ref, lower_ref, upper_ref, wide_ref, index_ref, rate_ref
+    gather_ref, change_ref, field_ref, slow_ref, lower_ref, middle_ref, edge_ref, wide_ref, index_ref, rate_ref
 ):
     species, depth, width, lanes = u_ref.shape
     count = consumed_ref.shape[1]
@@ -87,10 +87,9 @@
         pair = jnp.where(lane < size, pair, 0.0)
         change_ref[j] = (pair + pltpu.roll(pair, size, 1)).astype(jnp.bfloat16)
 
-    half = width // 2 * depth // 2
     for x in range(width):
         for y in range(depth):
-            t, k = divmod(x * depth + y, 2)
+            t, k = x // 2 * depth + y, x % 2
             part = slice(k * lanes, (k + 1) * lanes)
             for c in range(3):
                 field_ref[t, c : c + 1, part] = speed_ref[c, y, x : x + 1, :] * (1.0 / 12.0)
@@ -106,9 +105,7 @@
             elif 2 <= slot < width + 2 or 2 <= y < depth + 2:
                 wide_ref[slot * stride + y] = jnp.zeros((slab, lanes), jnp.float32)
 
-    def advect(row, field):
-        x = row // depth
-        y = row - x * depth
+    def advect(x, y, field):
         base = (x + 2) * stride + y + 2
         center = wide_ref[base]
         near = jnp.zeros_like(center)
@@ -131,15 +128,22 @@
             far = far + (high2 + low2)
         return center - moved + spread * (16.0 * near - far - 90.0 * center)
 
-    for target, shift in ((lower_ref, 0), (upper_ref, half)):
-        def tile(t, carry, target=target, shift=shift):
+    skipped = middle_ref.shape[0]
+    first = edge_ref.shape[0] // 2
+    for target, x0, row in (
+        (lower_ref, 0, lambda t: t),
+        (middle_ref, 2, lambda t: t + first),
+        (edge_ref, 2, lambda t: t + jnp.where(t >= first, skipped, 0)),
+    ):
+        def tile(t, carry, target=target, x0=x0, row=row):
+            y = row(t)
             for k in range(2):
                 part = slice(k * lanes, (k + 1) * lanes)
-                target[t, 0:slab, part] = advect(2 * (t + shift) + k, field_ref[t + shift, :, part])
+                target[t, 0:slab, part] = advect(x0 + k, y, field_ref[x0 // 2 * depth + y, :, part])
             target[t, slab:ROWS] = jnp.zeros((ROWS - slab, 2 * lanes), jnp.float32)
             return carry
 
-        lax.fori_loop(0, half, tile, 0)
+        lax.fori_loop(0, target.shape[0], tile, 0)
 
 
 def prepare(cells, speed, heat, spread, amplitude, energy, consumed, resulting):
@@ -154,8 +158,9 @@
         ((len(parts), ROWS, 2 * CHUNK), jnp.bfloat16),
         ((tiles, 8, 2 * lanes), jnp.float32),
         ((slab, lanes), jnp.float32),
-        ((tiles // 2, ROWS, 2 * lanes), jnp.float32),
-        ((tiles // 2, ROWS, 2 * lanes), jnp.float32),
+        ((depth, ROWS, 2 * lanes), jnp.float32),
+        ((depth - 4, ROWS, 2 * lanes), jnp.float32),
+        ((4, ROWS, 2 * lanes), jnp.float32),
     ]
     return pl.pallas_call(
         prepare_kernel,
@@ -165,25 +170,28 @@
             pltpu.VMEM((8, reach), jnp.int32),
             pltpu.VMEM((8, reach), jnp.float32),
         ],
+        compiler_params=pltpu.CompilerParams(vmem_limit_bytes=VMEM_LIMIT),
         name="prepare",
     )(cells, speed, heat, spread, amplitude, energy, consumed, resulting)
 
 
-def half_kernel(first_x, workers, *refs):
+def part_kernel(first_x, rows, workers, *refs):
     place_ref, owner_ref, base_ref, side_ref, ylo_ref, yhi_ref, field_ref, spread_ref = refs[:8]
     gather_ref, change_ref = refs[8:10]
-    out_ref, advected_ref, current_ref = refs[-3:]
+    if first_x == 0:
+        middle_ref, edge_ref, out_ref, advected_ref, current_ref, whole_ref, sems = refs[10:]
+    else:
+        out_ref, advected_ref, current_ref = refs[10:]
     species, depth, _, lanes = side_ref.shape
-    tiles = base_ref.shape[0]
-    first_tile = first_x * depth // 2
+    tiles = len(rows)
+    first_tile = first_x // 2 * depth
     side, ylo, yhi = strided(side_ref), strided(ylo_ref), strided(yhi_ref)
     spread = spread_ref[0:species]
 
-    for t in range(tiles):
-        for k in range(2):
-            x, y = divmod(2 * t + k, depth)
-            part = slice(k * lanes, (k + 1) * lanes)
-            field = field_ref[first_tile + t, :, part]
+    for t, y in enumerate(rows):
+        for x in range(2):
+            part = slice(x * lanes, (x + 1) * lanes)
+            field = field_ref[first_tile + y, :, part]
             values = base_ref[t, 0:species, part]
 
             def add(values, axis, far, value):
@@ -218,7 +226,7 @@
 
     def exponent(t):
         logged = jnp.log(jnp.maximum(current_ref[t], CONC_FLOOR)) * LOG2E
-        spare = jnp.where(is_one, 1.0, jnp.where(is_heat, field_ref[first_tile + t, 3:4], 0.0))
+        spare = jnp.where(is_one, 1.0, jnp.where(is_heat, field_ref[first_tile + rows[t], 3:4], 0.0))
         stacked = jnp.concatenate(
             [logged[: ROWS - 16], jnp.where(is_species, logged[ROWS - 16 :], spare)], axis=0
         )
@@ -234,50 +242,65 @@
             total = part if total is None else total + part
         return CHEM_DT * total
 
-    def substeps(turns):
-        order = [(i, t) for i in range(turns) for t in range(tiles)]
-        ready = exponent(0)
-        for n, (_, t) in enumerate(order):
-            powers = ready
-            if n + 1 < len(order):
-                ready = exponent(order[n + 1][1])
-            current_ref[t] = current_ref[t] + gained(powers)
-
-    if UNROLL == SUBSTEPS:
-        substeps(SUBSTEPS)
-    else:
-        def turn(i, carry):
-            substeps(UNROLL)
-            return carry
-
-        lax.fori_loop(0, SUBSTEPS // UNROLL, turn, 0)
-
-    for t in range(tiles):
-        reacts = owner_ref[0, place_ref[0] * PATCHES_ON_UNIT + first_tile + t] < workers
-        result = jnp.where(reacts, current_ref[t, 0:species], advected_ref[t])
-        if first_x != 0:
-            out_ref[t, 0:species] = result
+    def settled(t):
+        y = rows[t]
+        picked = []
+        for x in range(2):
+            part = slice(x * lanes, (x + 1) * lanes)
+            block = ((first_x + x) * depth + y) // 2
+            reacts = owner_ref[0, place_ref[0] * PATCHES_ON_UNIT + block] < workers
+            picked.append(jnp.where(reacts, current_ref[t, 0:species, part], advected_ref[t, :, part]))
+        return picked
+
+    copies = []
+    if first_x == 0:
+        write = strided(whole_ref)
+        others = [middle_ref.at[y - 2] if 2 <= y < depth - 2 else edge_ref.at[y if y < 2 else y - depth + 4] for y in rows]
+        for y in rows:
+            for x in range(2):
+                write(y, x + 2)[...] = others[y][0:species, x * lanes : (x + 1) * lanes]
+
+    order = [(i, t) for i in range(SUBSTEPS) for t in range(tiles)]
+    ready = exponent(0)
+    for n, (i, t) in enumerate(order):
+        powers = ready
+        if n + 1 < len(order):
+            ready = exponent(order[n + 1][1])
+        current_ref[t] = current_ref[t] + gained(powers)
+        if i + 1 < SUBSTEPS:
             continue
-        write = strided(out_ref)
-        for values, shift in ((result, 0), (refs[10][t, 0:species], 2)):
-            for k in range(2):
-                x, y = divmod(2 * t + k, depth)
-                write(y, x + shift)[...] = values[:, k * lanes : (k + 1) * lanes]
-
-
-def half(first_x, shape, workers, *args):
+        picked = settled(t)
+        for x in range(2):
+            if first_x == 0:
+                write(rows[t], x)[...] = picked[x]
+            else:
+                out_ref[t, 0:species, x * lanes : (x + 1) * lanes] = picked[x]
+        if first_x == 0:
+            y = rows[t]
+            copies.append(pltpu.make_async_copy(whole_ref.at[:, y], out_ref.at[:, y], sems.at[t]))
+            copies[-1].start()
+    for copy in copies:
+        copy.wait()
+
+
+def part(first_x, rows, shape, workers, *args):
     species, _, _, lanes = shape
-    tiles = args[2].shape[0]
+    tiles = len(rows)
     block = (tiles, ROWS, 2 * lanes)
     smem = pl.BlockSpec(memory_space=pltpu.SMEM)
+    scratch = [
+        pltpu.VMEM((tiles, species, 2 * lanes), jnp.float32),
+        pltpu.VMEM(block, jnp.float32),
+    ]
+    if first_x == 0:
+        scratch += [pltpu.VMEM(shape, jnp.float32), pltpu.SemaphoreType.DMA((tiles,))]
     return pl.pallas_call(
-        functools.partial(half_kernel, first_x, workers),
+        functools.partial(part_kernel, first_x, rows, workers),
         out_shape=pltpu.VMEM(block, jnp.float32) if first_x else jax.ShapeDtypeStruct(shape, jnp.float32),
         in_specs=[smem, smem] + [pl.BlockSpec() for _ in args[2:]],
-        scratch_shapes=[
-            pltpu.VMEM((tiles, species, 2 * lanes), jnp.float32),
-            pltpu.VMEM(block, jnp.float32),
-        ],
+        out_specs=pl.BlockSpec() if first_x else pl.BlockSpec(memory_space=pl.ANY),
+        scratch_shapes=scratch,
+        compiler_params=pltpu.CompilerParams(vmem_limit_bytes=VMEM_LIMIT),
     )(*args)
 
 
@@ -304,7 +327,7 @@
 
     workers = lax.axis_size("chem")
     place = lax.axis_index("chem").astype(jnp.int32).reshape(1)
-    gather, change, field, spread, lower, upper = prepare(
+    gather, change, field, spread, lower, middle, edge = prepare(
         cells,
         fluid_speed_vector.transpose(0, 2, 1, 3),
         thermal_state.transpose(1, 0, 2),
@@ -316,9 +339,15 @@
     )
     shared = tuple(map(on_chip, (field, spread, gather, change)))
     owners = (place, patch_assignee)
-    xlo, xhi, ylo, yhi, lower, upper = map(on_chip, (xlo, xhi, ylo, yhi, lower, upper))
-    upper = half(2, cells.shape, workers, *owners, upper, xhi, ylo, yhi, *shared)
-    out = half(0, cells.shape, workers, *owners, lower, xlo, ylo, yhi, *shared, on_chip(upper))
+    xlo, xhi, ylo, yhi, lower, middle, edge = map(on_chip, (xlo, xhi, ylo, yhi, lower, middle, edge))
+    inner = tuple(range(2, depth - 2))
+    outer = (0, 1, depth - 2, depth - 1)
+    middle = part(2, inner, cells.shape, workers, *owners, middle, xhi, xhi, xhi, *shared)
+    edge = part(2, outer, cells.shape, workers, *owners, edge, xhi, ylo, yhi, *shared)
+    out = part(
+        0, tuple(range(depth)), cells.shape, workers, *owners, lower, xlo, ylo, yhi, *shared,
+        on_chip(middle), on_chip(edge)
+    )
     return out.transpose(0, 2, 1, 3)
 
 

time: 54.7 us -> 46.6 us (0.85)
  the two profiles are of different devices: /device:TPU:9 before, /device:TPU:2 now
where the time goes in v5:
time: 46.6 us; the launch traced here: 46.2 us
  starting transfers between devices  24.5 us (53%)
  Pallas kernels  12.4 us (27%)
  waiting for transfers between devices  6.13 us (13%)
  local copies, waits for them, and re-layouts  2.93 us (6%)
    ppermute x1, starting transfers between devices, per_device(): xhi = lax.ppermute(again[:, :, :2], 'flow', flow_back)  15.7 us
    pallas_call x3, Pallas kernels, part(): pl.pallas_call(functools.partial(part_kernel, first_x, rows, workers), ou...  10.2 us
    ppermute x1, waiting for transfers between devices, per_device(): xhi = lax.ppermute(again[:, :, :2], 'flow', flow_back)  6.12 us
    ppermute x1, starting transfers between devices, per_device(): xlo = lax.ppermute(cells[:, :, width - 2:], 'flow', flow_next)  4.5 us
    ppermute x1, starting transfers between devices, per_device(): ylo = lax.ppermute(cells[:, depth - 2:], 'chem', chem_next)  2.41 us
    pallas_call x1, Pallas kernels, prepare(): pl.pallas_call(prepare_kernel, out_shape=[pltpu.VMEM(*shape) for shape in...  2.23 us
    ppermute x1, starting transfers between devices, per_device(): yhi = lax.ppermute(cells[:, :2], 'chem', chem_back)  1.92 us
    slice x1, local copies, waits for them, and re-layouts, per_device(): xlo = lax.ppermute(cells[:, :, width - 2:], 'flow', flow_next)  1.39 us
  transfers between devices with their start and end apart: 4, of which 1 were waited for; matrix products, arithmetic and copies ran while one was open for 0% of the time, Pallas kernels for 16%

profile of v5, /device:TPU:2, one launch (start us, length us, event | category | flops | bytes accessed | tf_op | source)
XLA Modules:
  0.0 46.2 jit_solution(2845586757556439000)
XLA Ops:
  0.0 0.0 copy-start
  0.0 1.4 %slice.16 = f32[53,7,2,128]{3,2,1,0:T(2,128)S(1)} slice(f32[53,7,4,128]{3,2,1,0:T(4,128)} %bitcast.8), slice={[0:53], [0:7], [2:4], [0:128]} | slice | bytes 759808 | tf_op jit(solution)/shard_map/slice | solution.py:322
  1.4 4.5 %collective-permute-start = (f32[53,7,2,128]{3,2,1,0:T(2,128)S(1)}, f32[53,7,2,128]{3,2,1,0:T(2,128)S(1)}, u32[]{:S(2)}, u32[]{:S(2)}) collective-permute-start(f32[53,7,2,128]{3,2,1,0:T(2,128)S(1)} %slice.16), channel_id=1, source_target_pairs={{0,16},{16,32},{32,48},{48,64},{64,80},{80,96},{96,112},{112,128},... | collective-permute-start | bytes 1139720 | tf_op jit(solution)/shard_map/ppermute | solution.py:322
  5.9 0.0 copy-done
  5.9 0.1 slice.19
  6.1 15.7 %collective-permute-start.3 = (f32[53,7,2,128]{3,2,1,0:T(2,128)S(1)}, f32[53,7,2,128]{3,2,1,0:T(2,128)S(1)}, u32[]{:S(2)}, u32[]{:S(2)}) collective-permute-start(f32[53,7,2,128]{3,2,1,0:T(2,128)S(1)} %slice.19), channel_id=1, source_target_pairs={{16,0},{32,16},{48,32},{64,48},{80,64},{96,80},{112,96},{128,112},... | collective-permute-start | bytes 1139720 | tf_op jit(solution)/shard_map/ppermute | solution.py:324
  21.8 0.0 copy-start.7
  21.8 0.0 copy-start.8
  21.8 0.0 copy-start.1
  21.8 0.0 copy-start.2
  21.8 1.9 %collective-permute-start.2 = (f32[53,2,4,128]{3,2,1,0:T(4,128)S(1)}, f32[53,2,4,128]{3,2,1,0:T(4,128)S(1)}, u32[]{:S(2)}, u32[]{:S(2)}) collective-permute-start(f32[53,2,4,128]{3,2,1,0:T(4,128)S(1)} %get-tuple-element.19), channel_id=1, source_target_pairs={{1,0},{2,1},{3,2},{4,3},{5,4},{6,5},{7,6},{8,7},{9,8},{10,9},{11,1... | collective-permute-start | bytes 651272 | tf_op jit(solution)/shard_map/ppermute | solution.py:326
  23.8 2.4 %collective-permute-start.1 = (f32[53,2,4,128]{3,2,1,0:T(4,128)S(1)}, f32[53,2,4,128]{3,2,1,0:T(4,128)S(1)}, u32[]{:S(2)}, u32[]{:S(2)}) collective-permute-start(f32[53,2,4,128]{3,2,1,0:T(4,128)S(1)} %get-tuple-element.20), channel_id=1, source_target_pairs={{0,1},{1,2},{2,3},{3,4},{4,5},{5,6},{6,7},{7,8},{8,9},{9,10},{10,1... | collective-permute-start | bytes 651272 | tf_op jit(solution)/shard_map/ppermute | solution.py:325
  26.2 0.0 copy-done.7
  26.2 0.0 copy-done.8
  26.2 0.0 copy-start.5
  26.2 0.0 copy-start.4
  26.3 0.0 copy-start.6
  26.3 0.0 copy-done.1
  26.3 0.0 copy-done.2
  26.3 0.6 %copy-done.5 = s32[325,2]{0,1:T(2,128)S(1)} copy-done((s32[325,2]{0,1:T(2,128)S(1)}, s32[325,2]{0,1:T(2,128)}, u32[]{:S(2)}) %copy-start.5) | copy-done | bytes 2624
  26.9 0.0 copy-done.4
  26.9 0.0 copy-done.6
  26.9 2.2 %prepare.1 = (bf16[336,128]{1,0:T(8,128)(2,1)S(1)}, bf16[3,64,256]{2,1,0:T(8,128)(2,1)S(1)}, f32[14,8,256]{2,1,0:T(8,128)S(1)}, f32[56,128]{1,0:T(8,128)S(1)}, f...) custom-call(f32[53,7,4,128]{3,2,1,0:T(4,128)S(1)} %bitcast.11, ...), custom_call_target="tpu_custom_call" | custom-call | tf_op jit(solution)/shard_map/prepare/pallas_call | solution.py:165
  29.2 6.1 %collective-permute-done.3.refs_3_.refs_4_.refs_5_ = f32[53,7,2,128]{3,2,1,0:T(2,128)S(1)} collective-permute-done((f32[53,7,2,128]{3,2,1,0:T(2,128)S(1)}, f32[53,7,2,128]{3,2,1,0:T(2,128)S(1)}, u32[]{:S(2)}, u32[]{:S(2)}) %collective-permute-start.3) | collective-permute-done | bytes 379936 | tf_op jit(solution)/shard_map/ppermute | solution.py:324
  35.3 0.0 copy-start.3
  35.3 0.7 %copy-done.3 = s32[1,224]{1,0:T(1,128)S(1)} copy-done((s32[1,224]{1,0:T(1,128)S(1)}, s32[1,224]{1,0:T(1,128)}, u32[]{:S(2)}) %copy-start.3) | copy-done | bytes 920
  36.0 2.6 %shard_map.91.refs_10_ = f32[3,64,256]{2,1,0:T(8,128)S(1)} custom-call(s32[1]{0:T(128)} %bitcast.refs_0_, s32[1,224]{1,0:T(1,128)S(1)} %copy-done.3, f32[3,64,256]{2,1,0:T(8,128)S(1)} %get-tuple-element.17.refs_2_, f32[53,7,2,128]{3,2,1,0:T(2,128)S(1)} %collective-permute-done.3.refs_3_.refs_4_.refs_5_, ...), custom_call_target="tpu_custom_call" | custom-call | tf_op jit(solution)/shard_map/pallas_call | solution.py:297
  38.5 0.0 collective-permute-done.2.refs_5_
  38.6 0.0 collective-permute-done.1.refs_4_
  38.6 2.8 %shard_map.92.refs_11_ = f32[4,64,256]{2,1,0:T(8,128)S(1)} custom-call(s32[1]{0:T(128)} %bitcast.refs_0_, s32[1,224]{1,0:T(1,128)S(1)} %copy-done.3, f32[4,64,256]{2,1,0:T(8,128)S(1)} %get-tuple-element.18.refs_2_, f32[53,7,2,128]{3,2,1,0:T(2,128)S(1)} %collective-permute-done.3.refs_3_.refs_4_.refs_5_, ...), custom_call_target="tpu_custom_call" | custom-call | tf_op jit(solution)/shard_map/pallas_call | solution.py:297
  41.4 0.0 collective-permute-done.refs_3_
  41.4 4.8 %shard_map.93 = f32[53,7,4,128]{3,2,1,0:T(4,128)} custom-call(s32[1]{0:T(128)} %bitcast.refs_0_, s32[1,224]{1,0:T(1,128)S(1)} %copy-done.3, f32[7,64,256]{2,1,0:T(8,128)S(1)} %get-tuple-element.12.refs_2_, f32[53,7,2,128]{3,2,1,0:T(2,128)S(1)} %collective-permute-done.refs_3_, f32[53,2,4,128]{3,2,1,0:T(4,128)S(1)} %collective-permute-done.1.refs_4_, ...), custom_call_target="tpu_custom_call" | custom-call | tf_op jit(solution)/shard_map/pallas_call | solution.py:297
  (3 shorter events, 0.0 us)
Async XLA Ops:
  0.0 5.9 %copy-start = (f32[53,4,7,128]{3,1,2,0:T(4,128)S(1)}, f32[53,4,7,128]{3,1,2,0:T(4,128)}, u32[]{:S(2)}) copy-start(f32[53,4,7,128]{3,1,2,0:T(4,128)} %param.9) | copy-start | bytes 2279428
  1.4 40.0 %collective-permute-start = (f32[53,7,2,128]{3,2,1,0:T(2,128)S(1)}, f32[53,7,2,128]{3,2,1,0:T(2,128)S(1)}, u32[]{:S(2)}, u32[]{:S(2)}) collective-permute-start(f32[53,7,2,128]{3,2,1,0:T(2,128)S(1)} %slice.16), channel_id=1, source_target_pairs={{0,16},{16,32},{32,48},{48,64},{64,80},{80,96},{96,112},{112,128},... | collective-permute-start | bytes 1139720 | tf_op jit(solution)/shard_map/ppermute | solution.py:322
  6.1 29.2 %collective-permute-start.3 = (f32[53,7,2,128]{3,2,1,0:T(2,128)S(1)}, f32[53,7,2,128]{3,2,1,0:T(2,128)S(1)}, u32[]{:S(2)}, u32[]{:S(2)}) collective-permute-start(f32[53,7,2,128]{3,2,1,0:T(2,128)S(1)} %slice.19), channel_id=1, source_target_pairs={{16,0},{32,16},{48,32},{64,48},{80,64},{96,80},{112,96},{128,112},... | collective-permute-start | bytes 1139720 | tf_op jit(solution)/shard_map/ppermute | solution.py:324
  21.8 4.4 %copy-start.7 = (f32[325]{0:T(512)S(1)}, f32[325]{0:T(512)}, u32[]{:S(2)}) copy-start(f32[325]{0:T(512)} %param.13) | copy-start | bytes 3904
  21.8 4.4 %copy-start.8 = (f32[325]{0:T(512)S(1)}, f32[325]{0:T(512)}, u32[]{:S(2)}) copy-start(f32[325]{0:T(512)} %param.14) | copy-start | bytes 3904
  21.8 4.5 %copy-start.1 = (f32[3,4,7,128]{3,1,2,0:T(4,128)S(1)}, f32[3,4,7,128]{3,1,2,0:T(4,128)}, u32[]{:S(2)}) copy-start(f32[3,4,7,128]{3,1,2,0:T(4,128)} %param.10) | copy-start | bytes 129028
  21.8 4.4 %copy-start.2 = (f32[4,7,128]{2,0,1:T(4,128)S(1)}, f32[4,7,128]{2,0,1:T(4,128)}, u32[]{:S(2)}) copy-start(f32[4,7,128]{2,0,1:T(4,128)} %param.11) | copy-start | bytes 43012
  21.8 16.7 %collective-permute-start.2 = (f32[53,2,4,128]{3,2,1,0:T(4,128)S(1)}, f32[53,2,4,128]{3,2,1,0:T(4,128)S(1)}, u32[]{:S(2)}, u32[]{:S(2)}) collective-permute-start(f32[53,2,4,128]{3,2,1,0:T(4,128)S(1)} %get-tuple-element.19), channel_id=1, source_target_pairs={{1,0},{2,1},{3,2},{4,3},{5,4},{6,5},{7,6},{8,7},{9,8},{10,9},{11,1... | collective-permute-start | bytes 651272 | tf_op jit(solution)/shard_map/ppermute | solution.py:326
  23.8 14.8 %collective-permute-start.1 = (f32[53,2,4,128]{3,2,1,0:T(4,128)S(1)}, f32[53,2,4,128]{3,2,1,0:T(4,128)S(1)}, u32[]{:S(2)}, u32[]{:S(2)}) collective-permute-start(f32[53,2,4,128]{3,2,1,0:T(4,128)S(1)} %get-tuple-element.20), channel_id=1, source_target_pairs={{0,1},{1,2},{2,3},{3,4},{4,5},{5,6},{6,7},{7,8},{8,9},{9,10},{10,1... | collective-permute-start | bytes 651272 | tf_op jit(solution)/shard_map/ppermute | solution.py:325
  26.2 0.7 %copy-start.5 = (s32[325,2]{0,1:T(2,128)S(1)}, s32[325,2]{0,1:T(2,128)}, u32[]{:S(2)}) copy-start(s32[325,2]{0,1:T(2,128)} %param.16) | copy-start | bytes 7804
  26.2 0.7 %copy-start.4 = (s32[325,2]{0,1:T(2,128)S(1)}, s32[325,2]{0,1:T(2,128)}, u32[]{:S(2)}) copy-start(s32[325,2]{0,1:T(2,128)} %param.15) | copy-start | bytes 7804
  26.3 0.7 %copy-start.6 = (f32[53]{0:T(128)S(1)}, f32[53]{0:T(128)}, u32[]{:S(2)}) copy-start(f32[53]{0:T(128)} %param.12) | copy-start | bytes 640
  35.3 0.7 %copy-start.3 = (s32[1,224]{1,0:T(1,128)S(1)}, s32[1,224]{1,0:T(1,128)}, u32[]{:S(2)}) copy-start(s32[1,224]{1,0:T(1,128)} %refs_1_.5) | copy-start | bytes 2692

commit v6 on v5

--- a/solution.py
+++ b/solution.py
@@ -51,7 +51,7 @@
 
 
 def prepare_kernel(
-    u_ref, speed_ref, heat_ref, spread_ref, amplitude_ref, energy_ref, consumed_ref, resulting_ref,
+    workers, place_ref, owner_ref, u_ref, speed_ref, heat_ref, spread_ref, amplitude_ref, energy_ref, consumed_ref, resulting_ref,
     gather_ref, change_ref, field_ref, slow_ref, lower_ref, middle_ref, edge_ref, wide_ref, index_ref, rate_ref
 ):
     species, depth, width, lanes = u_ref.shape
@@ -94,6 +94,9 @@
             for c in range(3):
                 field_ref[t, c : c + 1, part] = speed_ref[c, y, x : x + 1, :] * (1.0 / 12.0)
             field_ref[t, 3:4, part] = 1.0 / heat_ref[y, x : x + 1, :]
+            block = place_ref[0] * PATCHES_ON_UNIT + (x * depth + y) // 2
+            reacts = jnp.where(owner_ref[0, block] < workers, 1.0, 0.0)
+            field_ref[t, 4:5, part] = jnp.full((1, lanes), reacts, jnp.float32)
     spread = jnp.concatenate([spread_ref[...], jnp.zeros((1, lanes - species), jnp.float32)], axis=1)
     spread = jnp.transpose(jnp.broadcast_to(spread * (1.0 / 12.0), (lanes, lanes)))[0:slab]
     slow_ref[...] = spread
@@ -146,7 +149,8 @@
         lax.fori_loop(0, target.shape[0], tile, 0)
 
 
-def prepare(cells, speed, heat, spread, amplitude, energy, consumed, resulting):
+def prepare(workers, place, owners, cells, *args):
+    consumed = args[-1]
     species, depth, width, lanes = cells.shape
     count = consumed.shape[1]
     parts = chunks(count)
@@ -163,8 +167,9 @@
         ((4, ROWS, 2 * lanes), jnp.float32),
     ]
     return pl.pallas_call(
-        prepare_kernel,
+        functools.partial(prepare_kernel, workers),
         out_shape=[pltpu.VMEM(*shape) for shape in shapes],
+        in_specs=[pl.BlockSpec(memory_space=pltpu.SMEM)] * 2 + [pl.BlockSpec()] * (1 + len(args)),
         scratch_shapes=[
             pltpu.VMEM(((width + 4) * (depth + 4), slab, lanes), jnp.float32),
             pltpu.VMEM((8, reach), jnp.int32),
@@ -172,16 +177,15 @@
         ],
         compiler_params=pltpu.CompilerParams(vmem_limit_bytes=VMEM_LIMIT),
         name="prepare",
-    )(cells, speed, heat, spread, amplitude, energy, consumed, resulting)
-
-
-def part_kernel(first_x, rows, workers, *refs):
-    place_ref, owner_ref, base_ref, side_ref, ylo_ref, yhi_ref, field_ref, spread_ref = refs[:8]
-    gather_ref, change_ref = refs[8:10]
+    )(place, owners, cells, *args)
+
+
+def part_kernel(first_x, rows, *refs):
+    base_ref, side_ref, ylo_ref, yhi_ref, field_ref, spread_ref, gather_ref, change_ref = refs[:8]
     if first_x == 0:
-        middle_ref, edge_ref, out_ref, advected_ref, current_ref, whole_ref, sems = refs[10:]
+        middle_ref, edge_ref, out_ref, advected_ref, current_ref, whole_ref, sems = refs[8:]
     else:
-        out_ref, advected_ref, current_ref = refs[10:]
+        out_ref, advected_ref, current_ref = refs[8:]
     species, depth, _, lanes = side_ref.shape
     tiles = len(rows)
     first_tile = first_x // 2 * depth
@@ -247,8 +251,7 @@
         picked = []
         for x in range(2):
             part = slice(x * lanes, (x + 1) * lanes)
-            block = ((first_x + x) * depth + y) // 2
-            reacts = owner_ref[0, place_ref[0] * PATCHES_ON_UNIT + block] < workers
+            reacts = field_ref[first_tile + y, 4:5, part] > 0.5
             picked.append(jnp.where(reacts, current_ref[t, 0:species, part], advected_ref[t, :, part]))
         return picked
 
@@ -283,11 +286,10 @@
         copy.wait()
 
 
-def part(first_x, rows, shape, workers, *args):
+def part(first_x, rows, shape, *args):
     species, _, _, lanes = shape
     tiles = len(rows)
     block = (tiles, ROWS, 2 * lanes)
-    smem = pl.BlockSpec(memory_space=pltpu.SMEM)
     scratch = [
         pltpu.VMEM((tiles, species, 2 * lanes), jnp.float32),
         pltpu.VMEM(block, jnp.float32),
@@ -295,9 +297,8 @@
     if first_x == 0:
         scratch += [pltpu.VMEM(shape, jnp.float32), pltpu.SemaphoreType.DMA((tiles,))]
     return pl.pallas_call(
-        functools.partial(part_kernel, first_x, rows, workers),
+        functools.partial(part_kernel, first_x, rows),
         out_shape=pltpu.VMEM(block, jnp.float32) if first_x else jax.ShapeDtypeStruct(shape, jnp.float32),
-        in_specs=[smem, smem] + [pl.BlockSpec() for _ in args[2:]],
         out_specs=pl.BlockSpec() if first_x else pl.BlockSpec(memory_space=pl.ANY),
         scratch_shapes=scratch,
         compiler_params=pltpu.CompilerParams(vmem_limit_bytes=VMEM_LIMIT),
@@ -328,6 +329,9 @@
     workers = lax.axis_size("chem")
     place = lax.axis_index("chem").astype(jnp.int32).reshape(1)
     gather, change, field, spread, lower, middle, edge = prepare(
+        workers,
+        place,
+        patch_assignee,
         cells,
         fluid_speed_vector.transpose(0, 2, 1, 3),
         thermal_state.transpose(1, 0, 2),
@@ -338,14 +342,13 @@
         resulting_molecules.T,
     )
     shared = tuple(map(on_chip, (field, spread, gather, change)))
-    owners = (place, patch_assignee)
     xlo, xhi, ylo, yhi, lower, middle, edge = map(on_chip, (xlo, xhi, ylo, yhi, lower, middle, edge))
     inner = tuple(range(2, depth - 2))
     outer = (0, 1, depth - 2, depth - 1)
-    middle = part(2, inner, cells.shape, workers, *owners, middle, xhi, xhi, xhi, *shared)
-    edge = part(2, outer, cells.shape, workers, *owners, edge, xhi, ylo, yhi, *shared)
+    middle = part(2, inner, cells.shape, middle, xhi, xhi, xhi, *shared)
+    edge = part(2, outer, cells.shape, edge, xhi, ylo, yhi, *shared)
     out = part(
-        0, tuple(range(depth)), cells.shape, workers, *owners, lower, xlo, ylo, yhi, *shared,
+        0, tuple(range(depth)), cells.shape, lower, xlo, ylo, yhi, *shared,
         on_chip(middle), on_chip(edge)
     )
     return out.transpose(0, 2, 1, 3)

time: 46.6 us -> 45.3 us (0.972)
  the two profiles are of different devices: /device:TPU:2 before, /device:TPU:192 now
where the time goes in v6:
time: 45.3 us; the launch traced here: 45 us
  waiting for transfers between devices  15.9 us (35%)
  starting transfers between devices  15.3 us (34%)
  Pallas kernels  11.3 us (25%)
  local copies, waits for them, and re-layouts  2.25 us (5%)
    ppermute x1, waiting for transfers between devices, per_device(): xhi = lax.ppermute(again[:, :, :2], 'flow', flow_back)  12.8 us
    pallas_call x3, Pallas kernels, part(): pl.pallas_call(functools.partial(part_kernel, first_x, rows), out_shape=p...  8.56 us
    ppermute x1, starting transfers between devices, per_device(): yhi = lax.ppermute(cells[:, :2], 'chem', chem_back)  4.56 us
    ppermute x1, starting transfers between devices, per_device(): xlo = lax.ppermute(cells[:, :, width - 2:], 'flow', flow_next)  4.5 us
    ppermute x1, starting transfers between devices, per_device(): xhi = lax.ppermute(again[:, :, :2], 'flow', flow_back)  4.35 us
    ppermute x1, waiting for transfers between devices, per_device(): ylo = lax.ppermute(cells[:, depth - 2:], 'chem', chem_next)  3.08 us
    pallas_call x1, Pallas kernels, prepare(): pl.pallas_call(functools.partial(prepare_kernel, workers), out_shape=[plt...  2.79 us
    ppermute x1, starting transfers between devices, per_device(): ylo = lax.ppermute(cells[:, depth - 2:], 'chem', chem_next)  1.92 us
  transfers between devices with their start and end apart: 4, of which 2 were waited for; matrix products, arithmetic and copies ran while one was open for 0% of the time, Pallas kernels for 16%

profile of v6, /device:TPU:192, one launch (start us, length us, event | category | flops | bytes accessed | tf_op | source)
XLA Modules:
  0.0 45.0 jit_solution(4576890398633394205)
XLA Ops:
  0.0 0.0 copy-start
  0.0 1.4 %slice.16 = f32[53,7,2,128]{3,2,1,0:T(2,128)S(1)} slice(f32[53,7,4,128]{3,2,1,0:T(4,128)} %bitcast.8), slice={[0:53], [0:7], [2:4], [0:128]} | slice | bytes 759808 | tf_op jit(solution)/shard_map/slice | solution.py:323
  1.4 4.5 %collective-permute-start = (f32[53,7,2,128]{3,2,1,0:T(2,128)S(1)}, f32[53,7,2,128]{3,2,1,0:T(2,128)S(1)}, u32[]{:S(2)}, u32[]{:S(2)}) collective-permute-start(f32[53,7,2,128]{3,2,1,0:T(2,128)S(1)} %slice.16), channel_id=1, source_target_pairs={{0,16},{16,32},{32,48},{48,64},{64,80},{80,96},{96,112},{112,128},... | collective-permute-start | bytes 1139720 | tf_op jit(solution)/shard_map/ppermute | solution.py:323
  5.9 0.0 copy-done
  5.9 0.1 slice.19
  6.1 4.4 %collective-permute-start.3 = (f32[53,7,2,128]{3,2,1,0:T(2,128)S(1)}, f32[53,7,2,128]{3,2,1,0:T(2,128)S(1)}, u32[]{:S(2)}, u32[]{:S(2)}) collective-permute-start(f32[53,7,2,128]{3,2,1,0:T(2,128)S(1)} %slice.19), channel_id=1, source_target_pairs={{16,0},{32,16},{48,32},{64,48},{80,64},{96,80},{112,96},{128,112},... | collective-permute-start | bytes 1139720 | tf_op jit(solution)/shard_map/ppermute | solution.py:325
  10.4 0.0 copy-start.7
  10.4 0.0 copy-start.8
  10.4 0.0 copy-start.1
  10.5 0.0 copy-start.2
  10.5 4.6 %collective-permute-start.2 = (f32[53,2,4,128]{3,2,1,0:T(4,128)S(1)}, f32[53,2,4,128]{3,2,1,0:T(4,128)S(1)}, u32[]{:S(2)}, u32[]{:S(2)}) collective-permute-start(f32[53,2,4,128]{3,2,1,0:T(4,128)S(1)} %get-tuple-element.19), channel_id=1, source_target_pairs={{1,0},{2,1},{3,2},{4,3},{5,4},{6,5},{7,6},{8,7},{9,8},{10,9},{11,1... | collective-permute-start | bytes 651272 | tf_op jit(solution)/shard_map/ppermute | solution.py:327
  15.1 1.9 %collective-permute-start.1 = (f32[53,2,4,128]{3,2,1,0:T(4,128)S(1)}, f32[53,2,4,128]{3,2,1,0:T(4,128)S(1)}, u32[]{:S(2)}, u32[]{:S(2)}) collective-permute-start(f32[53,2,4,128]{3,2,1,0:T(4,128)S(1)} %get-tuple-element.20), channel_id=1, source_target_pairs={{0,1},{1,2},{2,3},{3,4},{4,5},{5,6},{6,7},{7,8},{8,9},{9,10},{10,1... | collective-permute-start | bytes 651272 | tf_op jit(solution)/shard_map/ppermute | solution.py:326
  17.0 0.0 copy-done.7
  17.0 0.0 copy-done.8
  17.0 0.0 copy-start.4
  17.1 0.0 copy-start.3
  17.1 0.0 copy-start.5
  17.1 0.0 copy-start.6
  17.1 0.0 copy-done.1
  17.1 0.0 copy-done.2
  17.1 0.6 %copy-done.4 = s32[325,2]{0,1:T(2,128)S(1)} copy-done((s32[325,2]{0,1:T(2,128)S(1)}, s32[325,2]{0,1:T(2,128)}, u32[]{:S(2)}) %copy-start.4) | copy-done | bytes 2624
  17.7 0.0 copy-done.3
  17.7 0.0 copy-done.5
  17.8 0.0 copy-done.6
  17.8 2.8 %prepare.1 = (bf16[336,128]{1,0:T(8,128)(2,1)S(1)}, bf16[3,64,256]{2,1,0:T(8,128)(2,1)S(1)}, f32[14,8,256]{2,1,0:T(8,128)S(1)}, f32[56,128]{1,0:T(8,128)S(1)}, f...) custom-call(s32[1]{0:T(128)} %bitcast.place_ref, s32[1,224]{1,0:T(1,128)S(1)} %copy-done.5, ...), custom_call_target="tpu_custom_call" | custom-call | tf_op jit(solution)/shard_map/prepare/pallas_call | solution.py:169
  20.6 12.8 %collective-permute-done.3.refs_1_.refs_2_.refs_3_ = f32[53,7,2,128]{3,2,1,0:T(2,128)S(1)} collective-permute-done((f32[53,7,2,128]{3,2,1,0:T(2,128)S(1)}, f32[53,7,2,128]{3,2,1,0:T(2,128)S(1)}, u32[]{:S(2)}, u32[]{:S(2)}) %collective-permute-start.3) | collective-permute-done | bytes 379936 | tf_op jit(solution)/shard_map/ppermute | solution.py:325
  33.3 2.0 %shard_map.91.refs_8_ = f32[3,64,256]{2,1,0:T(8,128)S(1)} custom-call(f32[3,64,256]{2,1,0:T(8,128)S(1)} %get-tuple-element.17.refs_0_, f32[53,7,2,128]{3,2,1,0:T(2,128)S(1)} %collective-permute-done.3.refs_1_.refs_2_.refs_3_, f32[53,7,2,128]{3,2,1,0:T(2,128)S(1)} %collective-permute-done.3.refs_1_.refs_2_.refs_3_, ...), custom_call_target="tpu_custom_call" | custom-call | tf_op jit(solution)/shard_map/pallas_call | solution.py:299
  35.3 0.0 collective-permute-done.2.refs_3_
  35.4 3.1 %collective-permute-done.1.refs_2_ = f32[53,2,4,128]{3,2,1,0:T(4,128)S(1)} collective-permute-done((f32[53,2,4,128]{3,2,1,0:T(4,128)S(1)}, f32[53,2,4,128]{3,2,1,0:T(4,128)S(1)}, u32[]{:S(2)}, u32[]{:S(2)}) %collective-permute-start.1) | collective-permute-done | bytes 217120 | tf_op jit(solution)/shard_map/ppermute | solution.py:326
  38.4 2.3 %shard_map.92.refs_9_ = f32[4,64,256]{2,1,0:T(8,128)S(1)} custom-call(f32[4,64,256]{2,1,0:T(8,128)S(1)} %get-tuple-element.18.refs_0_, f32[53,7,2,128]{3,2,1,0:T(2,128)S(1)} %collective-permute-done.3.refs_1_.refs_2_.refs_3_, f32[53,2,4,128]{3,2,1,0:T(4,128)S(1)} %collective-permute-done.1.refs_2_, f32[53,2,4,128]{3,2,1,0:T(4,128)S(1)} %collective-permute-done.2.refs_3_, ...), custom_call_target="tpu_custom_call" | custom-call | tf_op jit(solution)/shard_map/pallas_call | solution.py:299
  40.7 0.0 collective-permute-done.refs_1_
  40.7 4.3 %shard_map.93 = f32[53,7,4,128]{3,2,1,0:T(4,128)} custom-call(f32[7,64,256]{2,1,0:T(8,128)S(1)} %get-tuple-element.12.refs_0_, f32[53,7,2,128]{3,2,1,0:T(2,128)S(1)} %collective-permute-done.refs_1_, f32[53,2,4,128]{3,2,1,0:T(4,128)S(1)} %collective-permute-done.1.refs_2_, f32[53,2,4,128]{3,2,1,0:T(4,128)S(1)} %collective-permute-done.2.refs_3_, ...), custom_call_target="tpu_custom_call" | custom-call | tf_op jit(solution)/shard_map/pallas_call | solution.py:299
  (3 shorter events, 0.0 us)
Async XLA Ops:
  0.0 5.9 %copy-start = (f32[53,4,7,128]{3,1,2,0:T(4,128)S(1)}, f32[53,4,7,128]{3,1,2,0:T(4,128)}, u32[]{:S(2)}) copy-start(f32[53,4,7,128]{3,1,2,0:T(4,128)} %param.9) | copy-start | bytes 2279428
  1.4 39.3 %collective-permute-start = (f32[53,7,2,128]{3,2,1,0:T(2,128)S(1)}, f32[53,7,2,128]{3,2,1,0:T(2,128)S(1)}, u32[]{:S(2)}, u32[]{:S(2)}) collective-permute-start(f32[53,7,2,128]{3,2,1,0:T(2,128)S(1)} %slice.16), channel_id=1, source_target_pairs={{0,16},{16,32},{32,48},{48,64},{64,80},{80,96},{96,112},{112,128},... | collective-permute-start | bytes 1139720 | tf_op jit(solution)/shard_map/ppermute | solution.py:323
  6.1 27.3 %collective-permute-start.3 = (f32[53,7,2,128]{3,2,1,0:T(2,128)S(1)}, f32[53,7,2,128]{3,2,1,0:T(2,128)S(1)}, u32[]{:S(2)}, u32[]{:S(2)}) collective-permute-start(f32[53,7,2,128]{3,2,1,0:T(2,128)S(1)} %slice.19), channel_id=1, source_target_pairs={{16,0},{32,16},{48,32},{64,48},{80,64},{96,80},{112,96},{128,112},... | collective-permute-start | bytes 1139720 | tf_op jit(solution)/shard_map/ppermute | solution.py:325
  10.4 6.6 %copy-start.7 = (f32[325]{0:T(512)S(1)}, f32[325]{0:T(512)}, u32[]{:S(2)}) copy-start(f32[325]{0:T(512)} %param.13) | copy-start | bytes 3904
  10.4 6.6 %copy-start.8 = (f32[325]{0:T(512)S(1)}, f32[325]{0:T(512)}, u32[]{:S(2)}) copy-start(f32[325]{0:T(512)} %param.14) | copy-start | bytes 3904
  10.4 6.7 %copy-start.1 = (f32[3,4,7,128]{3,1,2,0:T(4,128)S(1)}, f32[3,4,7,128]{3,1,2,0:T(4,128)}, u32[]{:S(2)}) copy-start(f32[3,4,7,128]{3,1,2,0:T(4,128)} %param.10) | copy-start | bytes 129028
  10.5 6.6 %copy-start.2 = (f32[4,7,128]{2,0,1:T(4,128)S(1)}, f32[4,7,128]{2,0,1:T(4,128)}, u32[]{:S(2)}) copy-start(f32[4,7,128]{2,0,1:T(4,128)} %param.11) | copy-start | bytes 43012
  10.5 24.8 %collective-permute-start.2 = (f32[53,2,4,128]{3,2,1,0:T(4,128)S(1)}, f32[53,2,4,128]{3,2,1,0:T(4,128)S(1)}, u32[]{:S(2)}, u32[]{:S(2)}) collective-permute-start(f32[53,2,4,128]{3,2,1,0:T(4,128)S(1)} %get-tuple-element.19), channel_id=1, source_target_pairs={{1,0},{2,1},{3,2},{4,3},{5,4},{6,5},{7,6},{8,7},{9,8},{10,9},{11,1... | collective-permute-start | bytes 651272 | tf_op jit(solution)/shard_map/ppermute | solution.py:327
  15.1 23.4 %collective-permute-start.1 = (f32[53,2,4,128]{3,2,1,0:T(4,128)S(1)}, f32[53,2,4,128]{3,2,1,0:T(4,128)S(1)}, u32[]{:S(2)}, u32[]{:S(2)}) collective-permute-start(f32[53,2,4,128]{3,2,1,0:T(4,128)S(1)} %get-tuple-element.20), channel_id=1, source_target_pairs={{0,1},{1,2},{2,3},{3,4},{4,5},{5,6},{6,7},{7,8},{8,9},{9,10},{10,1... | collective-permute-start | bytes 651272 | tf_op jit(solution)/shard_map/ppermute | solution.py:326
  17.0 0.7 %copy-start.4 = (s32[325,2]{0,1:T(2,128)S(1)}, s32[325,2]{0,1:T(2,128)}, u32[]{:S(2)}) copy-start(s32[325,2]{0,1:T(2,128)} %param.16) | copy-start | bytes 7804
  17.1 0.7 %copy-start.3 = (s32[325,2]{0,1:T(2,128)S(1)}, s32[325,2]{0,1:T(2,128)}, u32[]{:S(2)}) copy-start(s32[325,2]{0,1:T(2,128)} %param.15) | copy-start | bytes 7804
  17.1 0.7 %copy-start.5 = (s32[1,224]{1,0:T(1,128)S(1)}, s32[1,224]{1,0:T(1,128)}, u32[]{:S(2)}) copy-start(s32[1,224]{1,0:T(1,128)} %owner_ref.1) | copy-start | bytes 2692
  17.1 0.7 %copy-start.6 = (f32[53]{0:T(128)S(1)}, f32[53]{0:T(128)}, u32[]{:S(2)}) copy-start(f32[53]{0:T(128)} %param.12) | copy-start | bytes 640

commit v7 on v6

--- a/solution.py
+++ b/solution.py
@@ -48,6 +48,24 @@
     species, ys, xs, lanes = ref.shape
     flat = ref.reshape(species * ys * xs, lanes)
     return lambda y, x: flat.at[pl.ds(y * xs + x, species, stride=ys * xs), :]
+
+
+def cut_kernel(cells_ref, out_ref, sem):
+    copy = pltpu.make_async_copy(cells_ref.at[:, :, cells_ref.shape[2] - 2 :], out_ref, sem)
+    copy.start()
+    copy.wait()
+
+
+def last_planes(cells):
+    species, depth, _, lanes = cells.shape
+    return pl.pallas_call(
+        cut_kernel,
+        out_shape=pltpu.VMEM((species, depth, 2, lanes), jnp.float32),
+        in_specs=[pl.BlockSpec(memory_space=pl.ANY)],
+        scratch_shapes=[pltpu.SemaphoreType.DMA],
+        compiler_params=pltpu.CompilerParams(vmem_limit_bytes=VMEM_LIMIT),
+        name="cut",
+    )(cells)
 
 
 def prepare_kernel(
@@ -316,11 +334,11 @@
     resulting_molecules,
     patch_assignee,
 ):
-    species, width, depth, _ = molar_fractions.shape
+    species, _, depth, _ = molar_fractions.shape
     cells = molar_fractions.transpose(0, 2, 1, 3)
     flow_next, flow_back = ring("flow")
     chem_next, chem_back = ring("chem")
-    xlo = lax.ppermute(cells[:, :, width - 2 :], "flow", flow_next)
+    xlo = lax.ppermute(jax.lax.optimization_barrier(last_planes(cells)), "flow", flow_next)
     again = lax.optimization_barrier(cells)
     xhi = lax.ppermute(again[:, :, :2], "flow", flow_back)
     ylo = lax.ppermute(cells[:, depth - 2 :], "chem", chem_next)

time: 45.3 us -> 45.3 us (level)
    slice x1 -> x0, local copies, waits for them, and re-layouts: 1.39 us -> none  [per_device(): xlo = lax.ppermute(cells[:, :, width - 2:], 'flow', flow_next)]
    unnamed x18 -> x20, local copies, waits for them, and re-layouts: 0.69 us -> 1.82 us
where the time goes in v7:
time: 45.3 us; the launch traced here: 45 us
  waiting for transfers between devices  15.9 us (35%)
  starting transfers between devices  15.5 us (34%)
  Pallas kernels  11.5 us (25%)
  local copies, waits for them, and re-layouts  1.98 us (4%)
    ppermute x1, waiting for transfers between devices, per_device(): xhi = lax.ppermute(again[:, :, :2], 'flow', flow_back)  12.8 us
    pallas_call x3, Pallas kernels, part(): pl.pallas_call(functools.partial(part_kernel, first_x, rows), out_shape=p...  8.55 us
    ppermute x1, starting transfers between devices, per_device(): lax.ppermute(jax.lax.optimization_barrier(last_planes(cells)), 'flow', fl...  4.63 us
    ppermute x1, starting transfers between devices, per_device(): yhi = lax.ppermute(cells[:, :2], 'chem', chem_back)  4.56 us
    ppermute x1, starting transfers between devices, per_device(): xhi = lax.ppermute(again[:, :, :2], 'flow', flow_back)  4.35 us
    ppermute x1, waiting for transfers between devices, per_device(): ylo = lax.ppermute(cells[:, depth - 2:], 'chem', chem_next)  3.08 us
    pallas_call x1, Pallas kernels, prepare(): pl.pallas_call(functools.partial(prepare_kernel, workers), out_shape=[plt...  2.79 us
    ppermute x1, starting transfers between devices, per_device(): ylo = lax.ppermute(cells[:, depth - 2:], 'chem', chem_next)  1.92 us
  transfers between devices with their start and end apart: 4, of which 2 were waited for; matrix products, arithmetic and copies ran while one was open for 0% of the time, Pallas kernels for 16%

profile of v7, /device:TPU:192, one launch (start us, length us, event | category | flops | bytes accessed | tf_op | source)
XLA Modules:
  0.0 45.0 jit_solution(10588667187070179121)
XLA Ops:
  0.0 1.1 %copy-done = f32[53,4,7,128]{3,1,2,0:T(4,128)S(1)} copy-done((f32[53,4,7,128]{3,1,2,0:T(4,128)S(1)}, f32[53,4,7,128]{3,1,2,0:T(4,128)}, u32[]{:S(2)}) %copy-start) | copy-done | bytes 759832
  1.1 0.1 cut.1
  1.3 4.6 %collective-permute-start = (f32[53,7,2,128]{3,2,1,0:T(2,128)S(1)}, f32[53,7,2,128]{3,2,1,0:T(2,128)S(1)}, u32[]{:S(2)}, u32[]{:S(2)}) collective-permute-start(f32[53,7,2,128]{3,2,1,0:T(2,128)S(1)} %cut.1), channel_id=1, source_target_pairs={{0,16},{16,32},{32,48},{48,64},{64,80},{80,96},{96,112},{112,128},... | collective-permute-start | bytes 1139720 | tf_op jit(solution)/shard_map/ppermute | solution.py:341
  5.9 0.0 copy-done.1
  5.9 0.1 slice.14
  6.1 4.4 %collective-permute-start.3 = (f32[53,7,2,128]{3,2,1,0:T(2,128)S(1)}, f32[53,7,2,128]{3,2,1,0:T(2,128)S(1)}, u32[]{:S(2)}, u32[]{:S(2)}) collective-permute-start(f32[53,7,2,128]{3,2,1,0:T(2,128)S(1)} %slice.14), channel_id=1, source_target_pairs={{16,0},{32,16},{48,32},{64,48},{80,64},{96,80},{112,96},{128,112},... | collective-permute-start | bytes 1139720 | tf_op jit(solution)/shard_map/ppermute | solution.py:343
  10.4 0.0 copy-start.8
  10.4 0.0 copy-start.9
  10.4 0.0 copy-start.2
  10.5 0.0 copy-start.3
  10.5 4.6 %collective-permute-start.2 = (f32[53,2,4,128]{3,2,1,0:T(4,128)S(1)}, f32[53,2,4,128]{3,2,1,0:T(4,128)S(1)}, u32[]{:S(2)}, u32[]{:S(2)}) collective-permute-start(f32[53,2,4,128]{3,2,1,0:T(4,128)S(1)} %get-tuple-element.19), channel_id=1, source_target_pairs={{1,0},{2,1},{3,2},{4,3},{5,4},{6,5},{7,6},{8,7},{9,8},{10,9},{11,1... | collective-permute-start | bytes 651272 | tf_op jit(solution)/shard_map/ppermute | solution.py:345
  15.1 1.9 %collective-permute-start.1 = (f32[53,2,4,128]{3,2,1,0:T(4,128)S(1)}, f32[53,2,4,128]{3,2,1,0:T(4,128)S(1)}, u32[]{:S(2)}, u32[]{:S(2)}) collective-permute-start(f32[53,2,4,128]{3,2,1,0:T(4,128)S(1)} %get-tuple-element.20), channel_id=1, source_target_pairs={{0,1},{1,2},{2,3},{3,4},{4,5},{5,6},{6,7},{7,8},{8,9},{9,10},{10,1... | collective-permute-start | bytes 651272 | tf_op jit(solution)/shard_map/ppermute | solution.py:344
  17.0 0.0 copy-done.8
  17.0 0.0 copy-done.9
  17.1 0.0 copy-start.5
  17.1 0.0 copy-start.4
  17.1 0.0 copy-start.6
  17.1 0.0 copy-start.7
  17.1 0.0 copy-done.2
  17.1 0.0 copy-done.3
  17.1 0.6 %copy-done.5 = s32[325,2]{0,1:T(2,128)S(1)} copy-done((s32[325,2]{0,1:T(2,128)S(1)}, s32[325,2]{0,1:T(2,128)}, u32[]{:S(2)}) %copy-start.5) | copy-done | bytes 2624
  17.7 0.0 copy-done.4
  17.8 0.0 copy-done.6
  17.8 0.0 copy-done.7
  17.8 2.8 %prepare.1 = (bf16[336,128]{1,0:T(8,128)(2,1)S(1)}, bf16[3,64,256]{2,1,0:T(8,128)(2,1)S(1)}, f32[14,8,256]{2,1,0:T(8,128)S(1)}, f32[56,128]{1,0:T(8,128)S(1)}, f...) custom-call(s32[1]{0:T(128)} %bitcast.place_ref, s32[1,224]{1,0:T(1,128)S(1)} %copy-done.6, ...), custom_call_target="tpu_custom_call" | custom-call | tf_op jit(solution)/shard_map/prepare/pallas_call | solution.py:187
  20.6 12.8 %collective-permute-done.3.refs_1_.refs_2_.refs_3_ = f32[53,7,2,128]{3,2,1,0:T(2,128)S(1)} collective-permute-done((f32[53,7,2,128]{3,2,1,0:T(2,128)S(1)}, f32[53,7,2,128]{3,2,1,0:T(2,128)S(1)}, u32[]{:S(2)}, u32[]{:S(2)}) %collective-permute-start.3) | collective-permute-done | bytes 379936 | tf_op jit(solution)/shard_map/ppermute | solution.py:343
  33.3 2.0 %shard_map.91.refs_8_ = f32[3,64,256]{2,1,0:T(8,128)S(1)} custom-call(f32[3,64,256]{2,1,0:T(8,128)S(1)} %get-tuple-element.17.refs_0_, f32[53,7,2,128]{3,2,1,0:T(2,128)S(1)} %collective-permute-done.3.refs_1_.refs_2_.refs_3_, f32[53,7,2,128]{3,2,1,0:T(2,128)S(1)} %collective-permute-done.3.refs_1_.refs_2_.refs_3_, ...), custom_call_target="tpu_custom_call" | custom-call | tf_op jit(solution)/shard_map/pallas_call | solution.py:317
  35.4 0.0 collective-permute-done.2.refs_3_
  35.4 3.1 %collective-permute-done.1.refs_2_ = f32[53,2,4,128]{3,2,1,0:T(4,128)S(1)} collective-permute-done((f32[53,2,4,128]{3,2,1,0:T(4,128)S(1)}, f32[53,2,4,128]{3,2,1,0:T(4,128)S(1)}, u32[]{:S(2)}, u32[]{:S(2)}) %collective-permute-start.1) | collective-permute-done | bytes 217120 | tf_op jit(solution)/shard_map/ppermute | solution.py:344
  38.4 2.3 %shard_map.92.refs_9_ = f32[4,64,256]{2,1,0:T(8,128)S(1)} custom-call(f32[4,64,256]{2,1,0:T(8,128)S(1)} %get-tuple-element.18.refs_0_, f32[53,7,2,128]{3,2,1,0:T(2,128)S(1)} %collective-permute-done.3.refs_1_.refs_2_.refs_3_, f32[53,2,4,128]{3,2,1,0:T(4,128)S(1)} %collective-permute-done.1.refs_2_, f32[53,2,4,128]{3,2,1,0:T(4,128)S(1)} %collective-permute-done.2.refs_3_, ...), custom_call_target="tpu_custom_call" | custom-call | tf_op jit(solution)/shard_map/pallas_call | solution.py:317
  40.7 0.0 collective-permute-done.refs_1_
  40.7 4.3 %shard_map.93 = f32[53,7,4,128]{3,2,1,0:T(4,128)} custom-call(f32[7,64,256]{2,1,0:T(8,128)S(1)} %get-tuple-element.12.refs_0_, f32[53,7,2,128]{3,2,1,0:T(2,128)S(1)} %collective-permute-done.refs_1_, f32[53,2,4,128]{3,2,1,0:T(4,128)S(1)} %collective-permute-done.1.refs_2_, f32[53,2,4,128]{3,2,1,0:T(4,128)S(1)} %collective-permute-done.2.refs_3_, ...), custom_call_target="tpu_custom_call" | custom-call | tf_op jit(solution)/shard_map/pallas_call | solution.py:317
  (5 shorter events, 0.0 us)
Async XLA Ops:
  0.0 1.1 %copy-start = (f32[53,4,7,128]{3,1,2,0:T(4,128)S(1)}, f32[53,4,7,128]{3,1,2,0:T(4,128)}, u32[]{:S(2)}) copy-start(f32[53,4,7,128]{3,1,2,0:T(4,128)} %param.9) | copy-start | bytes 2279428
  1.1 4.8 %copy-start.1 = (f32[53,4,7,128]{3,1,2,0:T(4,128)S(1)}, f32[53,4,7,128]{3,1,2,0:T(4,128)}, u32[]{:S(2)}) copy-start(f32[53,4,7,128]{3,1,2,0:T(4,128)} %param.9) | copy-start | bytes 2279428
  1.3 39.5 %collective-permute-start = (f32[53,7,2,128]{3,2,1,0:T(2,128)S(1)}, f32[53,7,2,128]{3,2,1,0:T(2,128)S(1)}, u32[]{:S(2)}, u32[]{:S(2)}) collective-permute-start(f32[53,7,2,128]{3,2,1,0:T(2,128)S(1)} %cut.1), channel_id=1, source_target_pairs={{0,16},{16,32},{32,48},{48,64},{64,80},{80,96},{96,112},{112,128},... | collective-permute-start | bytes 1139720 | tf_op jit(solution)/shard_map/ppermute | solution.py:341
  6.1 27.3 %collective-permute-start.3 = (f32[53,7,2,128]{3,2,1,0:T(2,128)S(1)}, f32[53,7,2,128]{3,2,1,0:T(2,128)S(1)}, u32[]{:S(2)}, u32[]{:S(2)}) collective-permute-start(f32[53,7,2,128]{3,2,1,0:T(2,128)S(1)} %slice.14), channel_id=1, source_target_pairs={{16,0},{32,16},{48,32},{64,48},{80,64},{96,80},{112,96},{128,112},... | collective-permute-start | bytes 1139720 | tf_op jit(solution)/shard_map/ppermute | solution.py:343
  10.4 6.6 %copy-start.8 = (f32[325]{0:T(512)S(1)}, f32[325]{0:T(512)}, u32[]{:S(2)}) copy-start(f32[325]{0:T(512)} %param.13) | copy-start | bytes 3904
  10.4 6.6 %copy-start.9 = (f32[325]{0:T(512)S(1)}, f32[325]{0:T(512)}, u32[]{:S(2)}) copy-start(f32[325]{0:T(512)} %param.14) | copy-start | bytes 3904
  10.4 6.7 %copy-start.2 = (f32[3,4,7,128]{3,1,2,0:T(4,128)S(1)}, f32[3,4,7,128]{3,1,2,0:T(4,128)}, u32[]{:S(2)}) copy-start(f32[3,4,7,128]{3,1,2,0:T(4,128)} %param.10) | copy-start | bytes 129028
  10.5 6.6 %copy-start.3 = (f32[4,7,128]{2,0,1:T(4,128)S(1)}, f32[4,7,128]{2,0,1:T(4,128)}, u32[]{:S(2)}) copy-start(f32[4,7,128]{2,0,1:T(4,128)} %param.11) | copy-start | bytes 43012
  10.5 24.8 %collective-permute-start.2 = (f32[53,2,4,128]{3,2,1,0:T(4,128)S(1)}, f32[53,2,4,128]{3,2,1,0:T(4,128)S(1)}, u32[]{:S(2)}, u32[]{:S(2)}) collective-permute-start(f32[53,2,4,128]{3,2,1,0:T(4,128)S(1)} %get-tuple-element.19), channel_id=1, source_target_pairs={{1,0},{2,1},{3,2},{4,3},{5,4},{6,5},{7,6},{8,7},{9,8},{10,9},{11,1... | collective-permute-start | bytes 651272 | tf_op jit(solution)/shard_map/ppermute | solution.py:345
  15.1 23.4 %collective-permute-start.1 = (f32[53,2,4,128]{3,2,1,0:T(4,128)S(1)}, f32[53,2,4,128]{3,2,1,0:T(4,128)S(1)}, u32[]{:S(2)}, u32[]{:S(2)}) collective-permute-start(f32[53,2,4,128]{3,2,1,0:T(4,128)S(1)} %get-tuple-element.20), channel_id=1, source_target_pairs={{0,1},{1,2},{2,3},{3,4},{4,5},{5,6},{6,7},{7,8},{8,9},{9,10},{10,1... | collective-permute-start | bytes 651272 | tf_op jit(solution)/shard_map/ppermute | solution.py:344
  17.1 0.7 %copy-start.5 = (s32[325,2]{0,1:T(2,128)S(1)}, s32[325,2]{0,1:T(2,128)}, u32[]{:S(2)}) copy-start(s32[325,2]{0,1:T(2,128)} %param.16) | copy-start | bytes 7804
  17.1 0.7 %copy-start.4 = (s32[325,2]{0,1:T(2,128)S(1)}, s32[325,2]{0,1:T(2,128)}, u32[]{:S(2)}) copy-start(s32[325,2]{0,1:T(2,128)} %param.15) | copy-start | bytes 7804
  17.1 0.7 %copy-start.6 = (s32[1,224]{1,0:T(1,128)S(1)}, s32[1,224]{1,0:T(1,128)}, u32[]{:S(2)}) copy-start(s32[1,224]{1,0:T(1,128)} %owner_ref.1) | copy-start | bytes 2692
  17.1 0.7 %copy-start.7 = (f32[53]{0:T(128)S(1)}, f32[53]{0:T(128)}, u32[]{:S(2)}) copy-start(f32[53]{0:T(128)} %param.12) | copy-start | bytes 640

commit v8 on v7

--- a/solution.py
+++ b/solution.py
@@ -61,11 +61,11 @@
     return pl.pallas_call(
         cut_kernel,
         out_shape=pltpu.VMEM((species, depth, 2, lanes), jnp.float32),
-        in_specs=[pl.BlockSpec(memory_space=pl.ANY)],
+        in_specs=[pl.BlockSpec(memory_space=pltpu.HBM)],
         scratch_shapes=[pltpu.SemaphoreType.DMA],
         compiler_params=pltpu.CompilerParams(vmem_limit_bytes=VMEM_LIMIT),
         name="cut",
-    )(cells)
+    )(pltpu.with_memory_space_constraint(cells, pltpu.HBM))
 
 
 def prepare_kernel(
@@ -282,11 +282,8 @@
                 write(y, x + 2)[...] = others[y][0:species, x * lanes : (x + 1) * lanes]
 
     order = [(i, t) for i in range(SUBSTEPS) for t in range(tiles)]
-    ready = exponent(0)
-    for n, (i, t) in enumerate(order):
-        powers = ready
-        if n + 1 < len(order):
-            ready = exponent(order[n + 1][1])
+    for i, t in order:
+        powers = exponent(t)
         current_ref[t] = current_ref[t] + gained(powers)
         if i + 1 < SUBSTEPS:
             continue

time: 45.3 us -> 44.8 us (0.989)
  local copies, waits for them, and re-layouts: 1.98 us -> 0.86 us
  Pallas kernels: 11.5 us -> 12.2 us
    unnamed x20 -> x18, local copies, waits for them, and re-layouts: 1.82 us -> 0.69 us
    pallas_call x1, Pallas kernels: 0.14 us -> 1.07 us  [last_planes(): pl.pallas_call(cut_kernel, out_shape=pltpu.VMEM((species, depth, 2, lanes...]
where the time goes in v8:
time: 44.8 us; the launch traced here: 44.5 us
  waiting for transfers between devices  15.9 us (35%)
  starting transfers between devices  15.3 us (34%)
  Pallas kernels  12.2 us (27%)
  local copies, waits for them, and re-layouts  0.86 us (2%)
    ppermute x1, waiting for transfers between devices, per_device(): xhi = lax.ppermute(again[:, :, :2], 'flow', flow_back)  12.8 us
    pallas_call x3, Pallas kernels, part(): pl.pallas_call(functools.partial(part_kernel, first_x, rows), out_shape=p...  8.35 us
    ppermute x1, starting transfers between devices, per_device(): yhi = lax.ppermute(cells[:, :2], 'chem', chem_back)  4.56 us
    ppermute x1, starting transfers between devices, per_device(): lax.ppermute(jax.lax.optimization_barrier(last_planes(cells)), 'flow', fl...  4.5 us
    ppermute x1, starting transfers between devices, per_device(): xhi = lax.ppermute(again[:, :, :2], 'flow', flow_back)  4.35 us
    ppermute x1, waiting for transfers between devices, per_device(): ylo = lax.ppermute(cells[:, depth - 2:], 'chem', chem_next)  3.07 us
    pallas_call x1, Pallas kernels, prepare(): pl.pallas_call(functools.partial(prepare_kernel, workers), out_shape=[plt...  2.79 us
    ppermute x1, starting transfers between devices, per_device(): ylo = lax.ppermute(cells[:, depth - 2:], 'chem', chem_next)  1.92 us
  transfers between devices with their start and end apart: 4, of which 2 were waited for; matrix products, arithmetic and copies ran while one was open for 0% of the time, Pallas kernels for 16%

profile of v8, /device:TPU:192, one launch (start us, length us, event | category | flops | bytes accessed | tf_op | source)
XLA Modules:
  0.0 44.5 jit_solution(8840920938868952638)
XLA Ops:
  0.0 0.0 copy-start
  0.0 1.1 %cut.1 = f32[53,7,2,128]{3,2,1,0:T(2,128)S(1)} custom-call(f32[53,7,4,128]{3,2,1,0:T(4,128)} %bitcast.8), custom_call_target="tpu_custom_call" | custom-call | tf_op jit(solution)/shard_map/cut/pallas_call | solution.py:61
  1.1 4.5 %collective-permute-start = (f32[53,7,2,128]{3,2,1,0:T(2,128)S(1)}, f32[53,7,2,128]{3,2,1,0:T(2,128)S(1)}, u32[]{:S(2)}, u32[]{:S(2)}) collective-permute-start(f32[53,7,2,128]{3,2,1,0:T(2,128)S(1)} %cut.1), channel_id=1, source_target_pairs={{0,16},{16,32},{32,48},{48,64},{64,80},{80,96},{96,112},{112,128},... | collective-permute-start | bytes 1139720 | tf_op jit(solution)/shard_map/ppermute | solution.py:338
  5.6 0.0 copy-done
  5.6 0.1 slice.14
  5.7 4.4 %collective-permute-start.3 = (f32[53,7,2,128]{3,2,1,0:T(2,128)S(1)}, f32[53,7,2,128]{3,2,1,0:T(2,128)S(1)}, u32[]{:S(2)}, u32[]{:S(2)}) collective-permute-start(f32[53,7,2,128]{3,2,1,0:T(2,128)S(1)} %slice.14), channel_id=1, source_target_pairs={{16,0},{32,16},{48,32},{64,48},{80,64},{96,80},{112,96},{128,112},... | collective-permute-start | bytes 1139720 | tf_op jit(solution)/shard_map/ppermute | solution.py:340
  10.1 0.0 copy-start.7
  10.1 0.0 copy-start.8
  10.1 0.0 copy-start.1
  10.2 0.0 copy-start.2
  10.2 4.6 %collective-permute-start.2 = (f32[53,2,4,128]{3,2,1,0:T(4,128)S(1)}, f32[53,2,4,128]{3,2,1,0:T(4,128)S(1)}, u32[]{:S(2)}, u32[]{:S(2)}) collective-permute-start(f32[53,2,4,128]{3,2,1,0:T(4,128)S(1)} %get-tuple-element.19), channel_id=1, source_target_pairs={{1,0},{2,1},{3,2},{4,3},{5,4},{6,5},{7,6},{8,7},{9,8},{10,9},{11,1... | collective-permute-start | bytes 651272 | tf_op jit(solution)/shard_map/ppermute | solution.py:342
  14.8 1.9 %collective-permute-start.1 = (f32[53,2,4,128]{3,2,1,0:T(4,128)S(1)}, f32[53,2,4,128]{3,2,1,0:T(4,128)S(1)}, u32[]{:S(2)}, u32[]{:S(2)}) collective-permute-start(f32[53,2,4,128]{3,2,1,0:T(4,128)S(1)} %get-tuple-element.20), channel_id=1, source_target_pairs={{0,1},{1,2},{2,3},{3,4},{4,5},{5,6},{6,7},{7,8},{8,9},{9,10},{10,1... | collective-permute-start | bytes 651272 | tf_op jit(solution)/shard_map/ppermute | solution.py:341
  16.7 0.0 copy-done.7
  16.7 0.0 copy-done.8
  16.7 0.0 copy-start.4
  16.7 0.0 copy-start.3
  16.8 0.0 copy-start.5
  16.8 0.0 copy-start.6
  16.8 0.0 copy-done.1
  16.8 0.0 copy-done.2
  16.8 0.6 %copy-done.4 = s32[325,2]{0,1:T(2,128)S(1)} copy-done((s32[325,2]{0,1:T(2,128)S(1)}, s32[325,2]{0,1:T(2,128)}, u32[]{:S(2)}) %copy-start.4) | copy-done | bytes 2624
  17.4 0.0 copy-done.3
  17.4 0.0 copy-done.5
  17.4 0.0 copy-done.6
  17.4 2.8 %prepare.1 = (bf16[336,128]{1,0:T(8,128)(2,1)S(1)}, bf16[3,64,256]{2,1,0:T(8,128)(2,1)S(1)}, f32[14,8,256]{2,1,0:T(8,128)S(1)}, f32[56,128]{1,0:T(8,128)S(1)}, f...) custom-call(s32[1]{0:T(128)} %bitcast.place_ref, s32[1,224]{1,0:T(1,128)S(1)} %copy-done.5, ...), custom_call_target="tpu_custom_call" | custom-call | tf_op jit(solution)/shard_map/prepare/pallas_call | solution.py:187
  20.2 12.8 %collective-permute-done.3.refs_1_.refs_2_.refs_3_ = f32[53,7,2,128]{3,2,1,0:T(2,128)S(1)} collective-permute-done((f32[53,7,2,128]{3,2,1,0:T(2,128)S(1)}, f32[53,7,2,128]{3,2,1,0:T(2,128)S(1)}, u32[]{:S(2)}, u32[]{:S(2)}) %collective-permute-start.3) | collective-permute-done | bytes 379936 | tf_op jit(solution)/shard_map/ppermute | solution.py:340
  33.0 2.0 %shard_map.91.refs_8_ = f32[3,64,256]{2,1,0:T(8,128)S(1)} custom-call(f32[3,64,256]{2,1,0:T(8,128)S(1)} %get-tuple-element.17.refs_0_, f32[53,7,2,128]{3,2,1,0:T(2,128)S(1)} %collective-permute-done.3.refs_1_.refs_2_.refs_3_, f32[53,7,2,128]{3,2,1,0:T(2,128)S(1)} %collective-permute-done.3.refs_1_.refs_2_.refs_3_, ...), custom_call_target="tpu_custom_call" | custom-call | tf_op jit(solution)/shard_map/pallas_call | solution.py:314
  35.0 0.0 collective-permute-done.2.refs_3_
  35.0 3.1 %collective-permute-done.1.refs_2_ = f32[53,2,4,128]{3,2,1,0:T(4,128)S(1)} collective-permute-done((f32[53,2,4,128]{3,2,1,0:T(4,128)S(1)}, f32[53,2,4,128]{3,2,1,0:T(4,128)S(1)}, u32[]{:S(2)}, u32[]{:S(2)}) %collective-permute-start.1) | collective-permute-done | bytes 217120 | tf_op jit(solution)/shard_map/ppermute | solution.py:341
  38.1 2.3 %shard_map.92.refs_9_ = f32[4,64,256]{2,1,0:T(8,128)S(1)} custom-call(f32[4,64,256]{2,1,0:T(8,128)S(1)} %get-tuple-element.18.refs_0_, f32[53,7,2,128]{3,2,1,0:T(2,128)S(1)} %collective-permute-done.3.refs_1_.refs_2_.refs_3_, f32[53,2,4,128]{3,2,1,0:T(4,128)S(1)} %collective-permute-done.1.refs_2_, f32[53,2,4,128]{3,2,1,0:T(4,128)S(1)} %collective-permute-done.2.refs_3_, ...), custom_call_target="tpu_custom_call" | custom-call | tf_op jit(solution)/shard_map/pallas_call | solution.py:314
  40.4 0.0 collective-permute-done.refs_1_
  40.4 4.1 %shard_map.93 = f32[53,7,4,128]{3,2,1,0:T(4,128)} custom-call(f32[7,64,256]{2,1,0:T(8,128)S(1)} %get-tuple-element.12.refs_0_, f32[53,7,2,128]{3,2,1,0:T(2,128)S(1)} %collective-permute-done.refs_1_, f32[53,2,4,128]{3,2,1,0:T(4,128)S(1)} %collective-permute-done.1.refs_2_, f32[53,2,4,128]{3,2,1,0:T(4,128)S(1)} %collective-permute-done.2.refs_3_, ...), custom_call_target="tpu_custom_call" | custom-call | tf_op jit(solution)/shard_map/pallas_call | solution.py:314
  (3 shorter events, 0.0 us)
Async XLA Ops:
  0.0 5.6 %copy-start = (f32[53,4,7,128]{3,1,2,0:T(4,128)S(1)}, f32[53,4,7,128]{3,1,2,0:T(4,128)}, u32[]{:S(2)}) copy-start(f32[53,4,7,128]{3,1,2,0:T(4,128)} %param.9) | copy-start | bytes 2279428
  1.1 39.3 %collective-permute-start = (f32[53,7,2,128]{3,2,1,0:T(2,128)S(1)}, f32[53,7,2,128]{3,2,1,0:T(2,128)S(1)}, u32[]{:S(2)}, u32[]{:S(2)}) collective-permute-start(f32[53,7,2,128]{3,2,1,0:T(2,128)S(1)} %cut.1), channel_id=1, source_target_pairs={{0,16},{16,32},{32,48},{48,64},{64,80},{80,96},{96,112},{112,128},... | collective-permute-start | bytes 1139720 | tf_op jit(solution)/shard_map/ppermute | solution.py:338
  5.7 27.3 %collective-permute-start.3 = (f32[53,7,2,128]{3,2,1,0:T(2,128)S(1)}, f32[53,7,2,128]{3,2,1,0:T(2,128)S(1)}, u32[]{:S(2)}, u32[]{:S(2)}) collective-permute-start(f32[53,7,2,128]{3,2,1,0:T(2,128)S(1)} %slice.14), channel_id=1, source_target_pairs={{16,0},{32,16},{48,32},{64,48},{80,64},{96,80},{112,96},{128,112},... | collective-permute-start | bytes 1139720 | tf_op jit(solution)/shard_map/ppermute | solution.py:340
  10.1 6.6 %copy-start.7 = (f32[325]{0:T(512)S(1)}, f32[325]{0:T(512)}, u32[]{:S(2)}) copy-start(f32[325]{0:T(512)} %param.13) | copy-start | bytes 3904
  10.1 6.6 %copy-start.8 = (f32[325]{0:T(512)S(1)}, f32[325]{0:T(512)}, u32[]{:S(2)}) copy-start(f32[325]{0:T(512)} %param.14) | copy-start | bytes 3904
  10.1 6.7 %copy-start.1 = (f32[3,4,7,128]{3,1,2,0:T(4,128)S(1)}, f32[3,4,7,128]{3,1,2,0:T(4,128)}, u32[]{:S(2)}) copy-start(f32[3,4,7,128]{3,1,2,0:T(4,128)} %param.10) | copy-start | bytes 129028
  10.2 6.6 %copy-start.2 = (f32[4,7,128]{2,0,1:T(4,128)S(1)}, f32[4,7,128]{2,0,1:T(4,128)}, u32[]{:S(2)}) copy-start(f32[4,7,128]{2,0,1:T(4,128)} %param.11) | copy-start | bytes 43012
  10.2 24.9 %collective-permute-start.2 = (f32[53,2,4,128]{3,2,1,0:T(4,128)S(1)}, f32[53,2,4,128]{3,2,1,0:T(4,128)S(1)}, u32[]{:S(2)}, u32[]{:S(2)}) collective-permute-start(f32[53,2,4,128]{3,2,1,0:T(4,128)S(1)} %get-tuple-element.19), channel_id=1, source_target_pairs={{1,0},{2,1},{3,2},{4,3},{5,4},{6,5},{7,6},{8,7},{9,8},{10,9},{11,1... | collective-permute-start | bytes 651272 | tf_op jit(solution)/shard_map/ppermute | solution.py:342
  14.8 23.4 %collective-permute-start.1 = (f32[53,2,4,128]{3,2,1,0:T(4,128)S(1)}, f32[53,2,4,128]{3,2,1,0:T(4,128)S(1)}, u32[]{:S(2)}, u32[]{:S(2)}) collective-permute-start(f32[53,2,4,128]{3,2,1,0:T(4,128)S(1)} %get-tuple-element.20), channel_id=1, source_target_pairs={{0,1},{1,2},{2,3},{3,4},{4,5},{5,6},{6,7},{7,8},{8,9},{9,10},{10,1... | collective-permute-start | bytes 651272 | tf_op jit(solution)/shard_map/ppermute | solution.py:341
  16.7 0.7 %copy-start.4 = (s32[325,2]{0,1:T(2,128)S(1)}, s32[325,2]{0,1:T(2,128)}, u32[]{:S(2)}) copy-start(s32[325,2]{0,1:T(2,128)} %param.16) | copy-start | bytes 7804
  16.7 0.7 %copy-start.3 = (s32[325,2]{0,1:T(2,128)S(1)}, s32[325,2]{0,1:T(2,128)}, u32[]{:S(2)}) copy-start(s32[325,2]{0,1:T(2,128)} %param.15) | copy-start | bytes 7804
  16.8 0.7 %copy-start.5 = (s32[1,224]{1,0:T(1,128)S(1)}, s32[1,224]{1,0:T(1,128)}, u32[]{:S(2)}) copy-start(s32[1,224]{1,0:T(1,128)} %owner_ref.1) | copy-start | bytes 2692
  16.8 0.7 %copy-start.6 = (f32[53]{0:T(128)S(1)}, f32[53]{0:T(128)}, u32[]{:S(2)}) copy-start(f32[53]{0:T(128)} %param.12) | copy-start | bytes 640
